TPU v7x, 32 devices: a whole 2x2x4 slice. The times are simulated.
32 devices in a mesh: sec: 4 (over y, x), col: 8 (over z, core).
Axes of the slice: x: 2, y: 2, z: 4, core: 2. Of those that a mesh axis runs over, the one named last changes fastest.
Arguments:
- state: float32 [16384, 7, 64], P(('sec', 'col')), may hold values from -6 to 6
- cosine: float32 [16384], P(('sec', 'col')), may hold values from 0.05 to 1
- grouping: int32 [32, 512], P(('sec', 'col')), may hold values from 0 to 511, each once within a row
- sunlit: int32 [32], P(('sec', 'col')), may hold values from 0 to 128
- absorb: float32 [256, 64, 448], P('sec'), may hold values from -0.25 to 0.25
- level_bias: float32 [256, 64], P('sec'), may hold values from -4 to 2
- planck: float32 [256], P('sec'), may hold values from 0.2 to 2
- solar_share: float32 [256], P('sec'), may hold values from 0.2 to 2
- stencil: int32 [3, 16384], P(None, ('sec', 'col')), may hold values from 0 to 143, as said below
- stencil_weight: float32 [3, 16384], P(None, ('sec', 'col')), may hold values from 0 to 1
Outputs:
- heating: float32 [64, 16384], P(None, ('sec', 'col'))
Inputs may be any that keep to these rules, and one draw needn't show every extreme that they name: Each row of grouping is a permutation of 0..511. stencil[k, p] lies within 8 of (p mod 512) // 4 + 8.
All inputs are finite; a program needn't handle non-finite values.
Results may differ from a plain program's by a relative error of at most 0.00007.
Values sent between devices are 32-bit elements; how exact they have to be, the bound alone decides.
No kernel may reach another device: no remote copies, remote signals or barrier semaphores. Data moves between devices by JAX's collectives and lax.ppermute only.
A program may use at most 128 MiB of HBM per device.

v0:
```python
import math

import jax
import jax.numpy as jnp
from jax import lax
from jax.sharding import PartitionSpec as P

G = 256
RIM = 8


def extended(block, sides, width):
    for axis, dim in sides:
        count = lax.axis_size(axis)
        forward = [(i, i + 1) for i in range(count - 1)]
        forward.append((count - 1, 0))
        backward = [(target, source) for source, target in forward]
        low = lax.ppermute(
            lax.slice_in_dim(block, block.shape[dim] - width, None, axis=dim), axis, forward
        )
        high = lax.ppermute(lax.slice_in_dim(block, 0, width, axis=dim), axis, backward)
        block = jnp.concatenate([low, block, high], axis=dim)
    return block


def sweep(trans, source, start, reverse):
    levels, g_local, width = trans.shape
    inner = math.gcd(levels, 8)
    outer = levels // inner
    t_blocks = trans.reshape(outer, inner, g_local, width)
    s_blocks = source.reshape(outer, inner, g_local, width)

    def step(carry, pair):
        t_here, s_here = pair
        sums = []
        order = range(inner - 1, -1, -1) if reverse else range(inner)
        for i in order:
            carry = t_here[i] * carry + s_here[i]
            sums.append(jnp.sum(carry, axis=0))
        if reverse:
            sums = sums[::-1]
        return (carry, jnp.stack(sums))

    last, sums = lax.scan(step, start, (t_blocks, s_blocks), reverse=reverse)
    return (last, sums.reshape(levels, width))


def radiate(rows, solar, absorb, level_bias, planck, solar_share):
    levels = level_bias.shape[1]
    warm = 2.0 + jnp.tanh(rows[:, :levels].T)
    z = jnp.einsum("glk,mk->lgm", absorb, rows, precision=lax.Precision.HIGHEST)
    z = z + level_bias.T[:, :, None]
    trans = jnp.exp(-0.1 * jax.nn.softplus(z))
    source = (1.0 - trans) * planck[None, :, None] * warm[:, None, :]
    top = solar_share[:, None] * solar[None, :]
    last, fall_below = sweep(trans, source, top, False)
    fall_sum = jnp.concatenate([jnp.sum(top, axis=0)[None], fall_below], axis=0)
    bottom = 0.3 * last + planck[:, None] * warm[-1][None]
    _, rise_above = sweep(trans, source, bottom, True)
    rise_sum = jnp.concatenate([rise_above, jnp.sum(bottom, axis=0)[None]], axis=0)
    net_sum = fall_sum - rise_sum
    return 4.0 / G * (net_sum[:-1] - net_sum[1:])


def shards(
    state,
    cosine,
    grouping,
    sunlit,
    absorb,
    level_bias,
    planck,
    solar_share,
    stencil,
    stencil_weight,
):
    f_dev, fields, levels = state.shape
    c_dev = f_dev // 4
    n_sec = lax.axis_size("sec")
    order = grouping[0]
    grouped = jnp.take(state, order, axis=0)
    rows = grouped.reshape(c_dev, 4, fields * levels).mean(axis=1)
    bright = jnp.take(cosine, order).reshape(c_dev, 4).mean(axis=1)
    lit = (jnp.arange(128, dtype=jnp.int32)[None, :] < sunlit[:, None]).reshape(c_dev)
    solar = jnp.where(lit, 4.0 * bright, 0.0)
    copied = jnp.broadcast_to(rows[None], (n_sec,) + rows.shape).reshape(
        n_sec * c_dev, fields * levels
    )
    lights = jnp.tile(solar, n_sec)
    got_rows, got_solar = (
        lax.all_to_all(copied, ("sec", "col"), split_axis=0, concat_axis=0, tiled=True),
        lax.all_to_all(lights, ("sec", "col"), split_axis=0, concat_axis=0, tiled=True),
    )
    heat = radiate(got_rows, got_solar, absorb, level_bias, planck, solar_share)
    returned = lax.all_to_all(heat, ("sec", "col"), split_axis=1, concat_axis=1, tiled=True)
    coarse_heat = returned.reshape(levels, n_sec, c_dev).sum(axis=1)
    padded = extended(coarse_heat, ((("sec", "col"), 1),), RIM)
    result = jnp.zeros((levels, f_dev), jnp.float32)
    for k in range(3):
        result = result + stencil_weight[k][None, :] * jnp.take(padded, stencil[k], axis=1)
    return result


def solution(mesh):
    placed = (
        P(("sec", "col"), None, None),
        P(("sec", "col")),
        P(("sec", "col"), None),
        P(("sec", "col")),
        P("sec", None, None),
        P("sec", None),
        P("sec"),
        P("sec"),
        P(None, ("sec", "col")),
        P(None, ("sec", "col")),
    )
    return jax.shard_map(
        shards, mesh=mesh, in_specs=placed, out_specs=P(None, ("sec", "col")), check_vma=False
    )
```

profile of v0, /device:TPU:0, one launch (start us, length us, event | category | flops | bytes accessed | tf_op | source)
XLA Modules:
  0.0 214.9 jit_solution(9431358948795877883)
XLA Ops:
  0.7 3.5 %gather_fusion = f32[512]{0:T(512)S(1)} fusion(f32[512]{0:T(512)S(1)} %copy-done, s32[1024]{0:T(1024)S(1)} %pad_clamp_fusion.3), kind=kCustom, calls=%fused_computation.3 | custom fusion | bytes 6144 | tf_op jit(solution)/shard_map/jit(_take)/gather | solution.py:83
  4.9 1.3 reduce.8
  7.8 7.3 %all-to-all-start = ((f32[32,16,1]{1,2,0:T(1,128)}), f32[32,16,1]{1,2,0:T(1,128)S(1)}, u32[]{:S(2)}, u32[]{:S(2)}) async-start(f32[32,16,1]{1,2,0:T(1,128)} %bitcast.55), calls=%async_computation | async-start | bytes 32768 | tf_op jit(solution)/shard_map/all_to_all | solution.py:92
  15.1 3.2 %copy.35 = f32[512,7,64]{2,1,0:T(8,128)} copy(f32[512,7,64]{0,2,1:T(8,128)} %param.16) | data formatting | bytes 1835008 | tf_op args[0]
  18.3 2.6 %gather_fusion.1 = f32[512,7,64]{2,1,0:T(8,128)S(1)} fusion(f32[512,7,64]{2,1,0:T(8,128)} %copy.35, s32[1024]{0:T(1024)S(1)} %pad_clamp_fusion.3), kind=kCustom, calls=%fused_computation.4 | custom fusion | bytes 1837056 | tf_op jit(solution)/shard_map/jit(_take)/gather | solution.py:81
  23.4 5.8 %all-to-all-start.1 = ((f32[32,16,448]{2,1,0:T(8,128)}), f32[32,16,448]{2,1,0:T(8,128)S(1)}, u32[]{:S(2)}, u32[]{:S(2)}) async-start(f32[32,16,448]{2,1,0:T(8,128)} %bitcast.57), calls=%async_computation.1 | async-start | bytes 2097152 | tf_op jit(solution)/shard_map/all_to_all | solution.py:91
  30.8 26.0 %all-to-all-done.1 = f32[32,16,448]{2,1,0:T(8,128)S(1)} async-done(((f32[32,16,448]{2,1,0:T(8,128)}), f32[32,16,448]{2,1,0:T(8,128)S(1)}, u32[]{:S(2)}, u32[]{:S(2)}) %all-to-all-start.1) | async-done | bytes 917536 | tf_op jit(solution)/shard_map/all_to_all | solution.py:91
  57.2 32.4 %fusion.34 = f32[64,64,512]{2,0,1:T(8,128)S(1)} fusion(f32[64,64]{0,1:T(8,128)S(1)} %bitcast.344, f32[512,448,1]{1,0,2:T(8,128)S(1)} %bitcast.311, f32[64,64,448]{2,1,0:T(8,128)} %param.20), kind=kOutput, calls=%fused_computation.74 | convolution fusion | flops 11291066368 | bytes 16662528 | tf_op jit(solution)/shard_map/glk,mk->lgm/dot_general | solution.py:51
  89.6 2.0 multiply_bitcast_fusion
  91.7 7.9 %copy.39 = f32[8,8,64,512]{3,2,1,0:T(8,128)} copy(f32[8,8,64,512]{3,1,0,2:T(8,128)S(1)} %multiply_bitcast_fusion) | data formatting | bytes 16777216 | tf_op jit(solution)/shard_map/while | solution.py:44
  99.6 8.0 %copy.38 = f32[8,8,64,512]{3,2,1,0:T(8,128)} copy(f32[8,8,64,512]{3,1,0,2:T(8,128)S(1)} %bitcast.309) | data formatting | bytes 16777216 | tf_op jit(solution)/shard_map/while | solution.py:44
  107.6 16.6 %while.28 = (s32[]{:T(128)}, f32[64,512]{1,0:T(8,128)S(1)}, f32[8,8,512]{2,1,0:T(8,128)S(1)}, f32[8,8,64,512]{3,2,1,0:T(8,128)}, f32[8,8,64,512]{3,2,1,0:T(8,128...) while((s32[]{:T(128)}, f32[64,512]{1,0:T(8,128)S(1)}, ...), condition=%wide.region_12.13_spmd, body=%wide.region_3.12_spmd.sunk | while | flops 782345 | bytes 4014365 | solution.py:44
  107.6 1.8 fusion.81
  109.6 1.8 fusion.81
  111.7 1.8 fusion.81
  113.8 1.8 fusion.81
  115.9 1.8 fusion.81
  117.9 1.8 fusion.81
  120.0 1.8 fusion.81
  122.1 1.8 fusion.81
  124.3 65.9 %while.29 = (s32[]{:T(128)}, f32[64,512]{1,0:T(8,128)S(1)}, f32[8,8,512]{2,1,0:T(8,128)S(1)}, f32[8,8,64,512]{3,2,1,0:T(8,128)}, f32[8,8,64,512]{3,2,1,0:T(8,128...) while((s32[]{:T(128)}, f32[64,512]{1,0:T(8,128)S(1)}, ...), condition=%wide.region_22.23_spmd, body=%wide.region_13.22_spmd.sunk | while | flops 782346 | bytes 4276525 | solution.py:44
  191.2 2.6 %all-to-all-start.2 = ((f32[32,1,1024]{2,1,0:T(1,128)}), f32[32,1,1024]{2,1,0:T(1,128)S(1)}, u32[]{:S(2)}, u32[]{:S(2)}) async-start(f32[32,1,1024]{2,1,0:T(1,128)} %reshape.243), calls=%async_computation.2 | async-start | bytes 262144 | tf_op jit(solution)/shard_map/all_to_all | solution.py:95
  193.8 8.1 %all-to-all-done.2 = f32[32,1,1024]{2,1,0:T(1,128)S(1)} async-done(((f32[32,1,1024]{2,1,0:T(1,128)}), f32[32,1,1024]{2,1,0:T(1,128)S(1)}, u32[]{:S(2)}, u32[]{:S(2)}) %all-to-all-start.2) | async-done | bytes 131104 | tf_op jit(solution)/shard_map/all_to_all | solution.py:95
  203.9 5.0 %collective-permute-start.1 = (f32[64,8]{0,1:T(8,128)S(1)}, f32[64,8]{0,1:T(8,128)S(1)}, u32[]{:S(2)}, u32[]{:S(2)}) collective-permute-start(f32[64,8]{0,1:T(8,128)S(1)} %get-tuple-element.230), channel_id=1, source_target_pairs={{1,0},{2,1},{3,2},{4,3},{5,4},{6,5},{7,6},{8,7},{9,8},{10,9},{11,1... | collective-permute-start | bytes 6152 | tf_op jit(solution)/shard_map/ppermute | solution.py:21
  (208 shorter events, 82.7 us)
Async XLA Ops:
  0.0 0.7 copy-start
  4.2 25.0 %copy-start.1 = (s32[3,512]{1,0:T(4,128)S(1)}, s32[3,512]{1,0:T(4,128)}, u32[]{:S(2)}) copy-start(s32[3,512]{1,0:T(4,128)} %param.24) | copy-start | bytes 18436
  4.2 26.5 %copy-start.4 = (f32[64]{0:T(128)S(1)}, f32[64]{0:T(128)}, u32[]{:S(2)}) copy-start(f32[64]{0:T(128)} %param.23) | copy-start | bytes 772
  7.8 14.4 %all-to-all-start = ((f32[32,16,1]{1,2,0:T(1,128)}), f32[32,16,1]{1,2,0:T(1,128)S(1)}, u32[]{:S(2)}, u32[]{:S(2)}) async-start(f32[32,16,1]{1,2,0:T(1,128)} %bitcast.55), calls=%async_computation | async-start | bytes 32768 | tf_op jit(solution)/shard_map/all_to_all | solution.py:92
  15.1 42.1 %copy-start.5 = (f32[64,64]{1,0:T(8,128)S(1)}, f32[64,64]{1,0:T(8,128)}, u32[]{:S(2)}) copy-start(f32[64,64]{1,0:T(8,128)} %param.21) | copy-start | bytes 49156
  23.4 33.4 %all-to-all-start.1 = ((f32[32,16,448]{2,1,0:T(8,128)}), f32[32,16,448]{2,1,0:T(8,128)S(1)}, u32[]{:S(2)}, u32[]{:S(2)}) async-start(f32[32,16,448]{2,1,0:T(8,128)} %bitcast.57), calls=%async_computation.1 | async-start | bytes 2097152 | tf_op jit(solution)/shard_map/all_to_all | solution.py:91
  57.2 32.4 %copy-start.3 = (f32[64]{0:T(128)S(1)}, f32[64]{0:T(128)}, u32[]{:S(2)}) copy-start(f32[64]{0:T(128)} %param.22) | copy-start | bytes 772
  124.2 69.6 %copy-start.2 = (f32[3,512]{1,0:T(4,128)S(1)}, f32[3,512]{1,0:T(4,128)}, u32[]{:S(2)}) copy-start(f32[3,512]{1,0:T(4,128)} %param.25) | copy-start | bytes 18436
  191.2 10.8 %all-to-all-start.2 = ((f32[32,1,1024]{2,1,0:T(1,128)}), f32[32,1,1024]{2,1,0:T(1,128)S(1)}, u32[]{:S(2)}, u32[]{:S(2)}) async-start(f32[32,1,1024]{2,1,0:T(1,128)} %reshape.243), calls=%async_computation.2 | async-start | bytes 262144 | tf_op jit(solution)/shard_map/all_to_all | solution.py:95
  203.6 6.7 %collective-permute-start = (f32[64,8]{0,1:T(8,128)S(1)}, f32[64,8]{0,1:T(8,128)S(1)}, u32[]{:S(2)}, u32[]{:S(2)}) collective-permute-start(f32[64,8]{0,1:T(8,128)S(1)} %get-tuple-element.229), channel_id=1, source_target_pairs={{0,1},{1,2},{2,3},{3,4},{4,5},{5,6},{6,7},{7,8},{8,9},{9,10},{10,1... | collective-permute-start | bytes 6152 | tf_op jit(solution)/shard_map/ppermute | solution.py:18
  203.9 6.4 %collective-permute-start.1 = (f32[64,8]{0,1:T(8,128)S(1)}, f32[64,8]{0,1:T(8,128)S(1)}, u32[]{:S(2)}, u32[]{:S(2)}) collective-permute-start(f32[64,8]{0,1:T(8,128)S(1)} %get-tuple-element.230), channel_id=1, source_target_pairs={{1,0},{2,1},{3,2},{4,3},{5,4},{6,5},{7,6},{8,7},{9,8},{10,9},{11,1... | collective-permute-start | bytes 6152 | tf_op jit(solution)/shard_map/ppermute | solution.py:21
where the time goes:
time: 217 us; the launch traced here: 215 us
  other arithmetic  88.7 us (41%)
  local copies, waits for them, and re-layouts  35.5 us (16%)
  waiting for transfers between devices  35.4 us (16%)
  matrix products  32.4 us (15%)
  starting transfers between devices  21.1 us (10%)
    reduce_sum x120, other arithmetic, step(): sums.append(jnp.sum(carry, axis=0))  81 us
    dot_general x1, matrix products, radiate(): z = jnp.einsum('glk,mk->lgm', absorb, rows, precision=lax.Precision.HIGHEST)  32.4 us
    all_to_all x1, waiting for transfers between devices, shards(): lax.all_to_all(copied, ('sec', 'col'), split_axis=0, concat_axis=0, tiled...  26 us
    while x2, local copies, waits for them, and re-layouts, sweep(): last, sums = lax.scan(step, start, (t_blocks, s_blocks), reverse=reverse)  15.9 us
    all_to_all x1, waiting for transfers between devices, shards(): lax.all_to_all(heat, ('sec', 'col'), split_axis=1, concat_axis=1, tiled=T...  8.13 us
    all_to_all x1, starting transfers between devices, shards(): lax.all_to_all(lights, ('sec', 'col'), split_axis=0, concat_axis=0, tiled...  7.3 us
    all_to_all x1, starting transfers between devices, shards(): lax.all_to_all(copied, ('sec', 'col'), split_axis=0, concat_axis=0, tiled...  5.83 us
    ppermute x1, starting transfers between devices, extended(): lax.ppermute(lax.slice_in_dim(block, 0, width, axis=dim), axis, backward)  5.03 us
  transfers between devices with their start and end apart: 5, of which 3 were waited for; matrix products, arithmetic and copies ran while one was open for 4% of the time, Pallas kernels for 0%

commit v1 on v0

v1 whole, which is shorter than its diff:
```python
import functools

import jax
import jax.numpy as jnp
from jax import lax
from jax.experimental import pallas as pl
from jax.experimental.pallas import tpu as pltpu
from jax.sharding import PartitionSpec as P

RIM = 8
MIB = 1 << 20
bf16 = jnp.bfloat16
f32 = jnp.float32
VMEM = pl.BlockSpec(memory_space=pltpu.VMEM)


def split(x, parts):
    terms = []
    for _ in range(parts):
        term = x.astype(bf16)
        terms.append(term)
        x = x - term.astype(f32)
    return terms


def dot(a, b):
    return jnp.dot(a, b, preferred_element_type=f32)


def group_body(state, cosine, grouping, sunlit, out):
    feat, fine = state.shape
    coarse = out.shape[1]
    place = lax.broadcasted_iota(jnp.int32, (fine, fine), 0)
    picks = jnp.where(place == grouping[...], 1.0, 0.0).astype(bf16)
    member = lax.broadcasted_iota(jnp.int32, (fine, coarse), 0) // 4
    home = lax.broadcasted_iota(jnp.int32, (fine, coarse), 1)
    mean = jnp.where(member == home, 0.25, 0.0).astype(bf16)
    weights = dot(picks, mean).astype(bf16)
    total = jnp.zeros((feat, coarse), f32)
    for term in split(state[...], 3)[::-1]:
        total = total + dot(term, weights)
    out[0:feat, :] = total
    light = jnp.zeros((8, coarse), f32)
    for term in split(jnp.broadcast_to(cosine[...], (8, fine)), 3)[::-1]:
        light = light + dot(term, weights)
    lane = lax.broadcasted_iota(jnp.int32, (8, coarse), 1)
    out[feat : feat + 8, :] = jnp.where(lane < sunlit[0], 4.0 * light, 0.0)


def group(state, cosine, grouping, sunlit):
    feat, fine = state.shape
    coarse = fine // 4
    return pl.pallas_call(
        group_body,
        out_shape=jax.ShapeDtypeStruct((feat + 8, coarse), f32),
        in_specs=[VMEM, VMEM, VMEM, pl.BlockSpec(memory_space=pltpu.SMEM)],
        out_specs=VMEM,
        compiler_params=pltpu.CompilerParams(vmem_limit_bytes=16 * MIB),
        cost_estimate=pl.CostEstimate(
            flops=8 * feat * fine * coarse, bytes_accessed=4 * feat * fine, transcendentals=0
        ),
        name="group",
    )(state, cosine, grouping, sunlit)


def tables_body(planck, share, stencil, weight, planck_out, share_out, high, low):
    def column(row):
        n = row.shape[1]
        eye = lax.broadcasted_iota(jnp.int32, (n, n), 0) == lax.broadcasted_iota(
            jnp.int32, (n, n), 1
        )
        return jnp.sum(jnp.where(eye, row, 0.0), axis=1, keepdims=True)

    planck_out[...] = jnp.broadcast_to(column(planck[...]), planck_out.shape)
    share_out[...] = jnp.broadcast_to(column(share[...]), share_out.shape)
    wide, fine = high.shape
    coarse = wide // 2
    place = lax.broadcasted_iota(jnp.int32, (wide, fine), 0)
    total = jnp.zeros((wide, fine), f32)
    for k in range(stencil.shape[0]):
        at = stencil[k : k + 1, :]
        spot = jnp.where(
            at < RIM,
            2 * coarse - RIM + at,
            jnp.where(at < coarse + RIM, at - RIM, at - RIM),
        )
        total = total + jnp.where(place == spot, weight[k : k + 1, :], 0.0)
    parts = split(total, 2)
    high[...] = parts[0]
    low[...] = parts[1]


def tables(planck, share, stencil, weight, coarse):
    g = planck.shape[1]
    fine = stencil.shape[1]
    column = jax.ShapeDtypeStruct((g, coarse), f32)
    table = jax.ShapeDtypeStruct((2 * coarse, fine), bf16)
    return pl.pallas_call(
        tables_body,
        out_shape=(column, column, table, table),
        in_specs=[VMEM] * 4,
        out_specs=[VMEM] * 4,
        compiler_params=pltpu.CompilerParams(vmem_limit_bytes=16 * MIB),
        cost_estimate=pl.CostEstimate(
            flops=20 * coarse * fine, bytes_accessed=8 * coarse * fine, transcendentals=0
        ),
        name="tables",
    )(planck, share, stencil, weight)


def prepare_body(absorb, bias, high, low):
    i = pl.program_id(0)
    count = absorb.shape[1]
    b = bias[...]
    lane = lax.broadcasted_iota(jnp.int32, b.shape, 1)
    for j in range(count):
        tail = jnp.where(lane == i * count + j, b, 0.0)
        parts = split(jnp.concatenate([absorb[:, j, :], tail], axis=1), 2)
        high[j] = parts[0]
        low[j] = parts[1]


def prepare(absorb, bias):
    g, levels, feat = absorb.shape
    block = 8
    depth = feat + levels
    table = jax.ShapeDtypeStruct((levels, g, depth), bf16)
    spec = pl.BlockSpec((block, g, depth), lambda i: (i, 0, 0))
    return pl.pallas_call(
        prepare_body,
        out_shape=(table, table),
        grid=(levels // block,),
        in_specs=[
            pl.BlockSpec((g, block, feat), lambda i: (0, i, 0)),
            pl.BlockSpec((g, levels), lambda i: (0, 0)),
        ],
        out_specs=[spec, spec],
        compiler_params=pltpu.CompilerParams(vmem_limit_bytes=16 * MIB),
        cost_estimate=pl.CostEstimate(
            flops=10 * g * levels * feat, bytes_accessed=8 * g * levels * depth, transcendentals=0
        ),
        name="prepare",
    )(absorb, bias)


def trans_of(z):
    low = jnp.log(1.0 + jnp.exp(jnp.minimum(z, 40.0)))
    return jnp.exp(-0.1 * jnp.maximum(low, z))


def flux_body(block, scale, high, low, rows, planck, share, out, right, zs, ts, downs, warms):
    levels, g, depth = high.shape
    feat = depth - levels
    n = rows.shape[1]
    blocks = levels // block
    parts = split(rows[0:feat, :], 2)
    right[0:feat, 0:n] = parts[0]
    right[0:feat, n : 2 * n] = parts[1]
    right[feat:depth, 0:n] = jnp.ones((levels, n), bf16)
    right[feat:depth, n : 2 * n] = jnp.zeros((levels, n), bf16)
    warms[0:levels, :] = 2.0 + jnp.tanh(rows[0:levels, :])
    warms[levels : levels + 8, :] = jnp.zeros((8, n), f32)
    weight = planck[...]

    def fold(x):
        return jnp.sum(x.reshape(g // 8, 8, n), axis=0)

    def absorb(b, slot):
        a = high[pl.ds(b * block, block)].reshape(block * g, depth)
        c = low[pl.ds(b * block, block)].reshape(block * g, depth)
        z = dot(a, right[...]) + dot(c, right[...])
        zs[slot] = z[:, 0:n] + z[:, n : 2 * n]

    def fall(b, slot, d):
        for j in range(block):
            l = b * block + j
            t = trans_of(zs[slot, j * g : (j + 1) * g, :])
            ts[l] = t
            d = t * d + weight * (warms[pl.ds(l, 1), :] - warms[pl.ds(l + 1, 1), :])
            downs[l + 1] = fold(d)
        return d

    d = share[...] * rows[feat : feat + 1, :] - weight * warms[0:1, :]
    downs[0] = fold(d)
    absorb(0, 0)

    def step(i, d):
        absorb(2 * i + 1, 1)
        d = fall(2 * i, 0, d)
        absorb(jnp.minimum(2 * i + 2, blocks - 1), 0)
        return fall(2 * i + 1, 1, d)

    d = lax.fori_loop(0, blocks // 2, step, d)
    total = jnp.sum(fold(weight), axis=0, keepdims=True)
    v = 0.3 * d

    def climb(i, carry):
        v, below = carry
        l = levels - 1 - i
        here = warms[pl.ds(l, 1), :]
        rise = here - warms[pl.ds(jnp.maximum(l - 1, 0), 1), :]
        v = ts[l] * v + weight * rise
        above = fold(v)
        part = (downs[l] - downs[l + 1]) + (below - above)
        row = jnp.sum(part, axis=0, keepdims=True)
        row = row + total * ((here - warms[pl.ds(l + 1, 1), :]) + rise)
        out[pl.ds(l, 1), :] = scale * row
        return v, above

    lax.fori_loop(0, levels, climb, (v, fold(v)), unroll=4)


def flux(high, low, rows, planck, share, scale):
    levels, g, depth = high.shape
    n = rows.shape[1]
    block = 4
    return pl.pallas_call(
        functools.partial(flux_body, block, scale),
        out_shape=jax.ShapeDtypeStruct((levels, n), f32),
        in_specs=[VMEM] * 5,
        out_specs=VMEM,
        scratch_shapes=[
            pltpu.VMEM((depth, 2 * n), bf16),
            pltpu.VMEM((2, block * g, n), f32),
            pltpu.VMEM((levels, g, n), f32),
            pltpu.VMEM((levels + 1, 8, n), f32),
            pltpu.VMEM((levels + 8, n), f32),
        ],
        compiler_params=pltpu.CompilerParams(vmem_limit_bytes=16 * MIB),
        cost_estimate=pl.CostEstimate(
            flops=8 * g * levels * depth * n,
            bytes_accessed=4 * g * levels * depth,
            transcendentals=3 * g * levels * n,
        ),
        name="flux",
    )(high, low, rows, planck, share)


def spread_body(own, first, second, parity, high, low, out):
    n = own.shape[1]
    lane = lax.broadcasted_iota(jnp.int32, own.shape, 1)
    late = jnp.where(lane >= n // 2, 1, 0)
    halo = jnp.where(late == parity[0], first[...], second[...])
    wide = jnp.concatenate([own[...], halo], axis=1)
    a, c = split(wide, 2)
    out[...] = dot(a, high[...]) + (dot(a, low[...]) + dot(c, high[...]))


def spread(own, first, second, parity, high, low):
    levels = own.shape[0]
    fine = high.shape[1]
    return pl.pallas_call(
        spread_body,
        out_shape=jax.ShapeDtypeStruct((levels, fine), f32),
        in_specs=[VMEM] * 3 + [pl.BlockSpec(memory_space=pltpu.SMEM)] + [VMEM] * 2,
        out_specs=VMEM,
        compiler_params=pltpu.CompilerParams(vmem_limit_bytes=16 * MIB),
        name="spread",
    )(own, first, second, parity, high, low)


def shards(
    state, cosine, grouping, sunlit, absorb, level_bias, planck, solar_share, stencil, stencil_weight
):
    fine, fields, levels = state.shape
    coarse = fine // 4
    n_sec = lax.axis_size("sec")
    devices = n_sec * lax.axis_size("col")
    columns = state.transpose(1, 2, 0).reshape(fields * levels, fine)
    rows = group(columns, cosine[None], grouping, sunlit)

    def swap(x, m):
        return lax.ppermute(x, "sec", [(i, i ^ m) for i in range(n_sec)])

    got = {m: swap(rows, m) for m in range(1, n_sec)}
    high, low = prepare(absorb, level_bias)
    weight, share, near, far = tables(planck[None], solar_share[None], stencil, stencil_weight, coarse)
    scale = 4.0 / (planck.shape[0] * n_sec)
    back = {}
    for m in range(1, n_sec):
        part = flux(high, low, got[m], weight, share, scale)
        back[m] = swap(part, m)
    total = flux(high, low, rows, weight, share, scale)
    for m in range(1, n_sec):
        total = total + back[m]
    pairs = [(i, i ^ 1) for i in range(devices)]
    across = [(i, (i + 1) % devices if i % 2 else (i - 1) % devices) for i in range(devices)]
    second = lax.ppermute(total, ("sec", "col"), across)
    first = lax.ppermute(total, ("sec", "col"), pairs)
    parity = (lax.axis_index(("sec", "col")) % 2).astype(jnp.int32).reshape(1)
    return spread(total, first, second, parity, near, far)


def solution(mesh):
    placed = (
        P(("sec", "col"), None, None),
        P(("sec", "col")),
        P(("sec", "col"), None),
        P(("sec", "col")),
        P("sec", None, None),
        P("sec", None),
        P("sec"),
        P("sec"),
        P(None, ("sec", "col")),
        P(None, ("sec", "col")),
    )
    return jax.shard_map(
        shards, mesh=mesh, in_specs=placed, out_specs=P(None, ("sec", "col")), check_vma=False
    )
```

time: 217 us -> 51.2 us (0.24)
  other arithmetic: 88.7 us -> 0.01 us
  waiting for transfers between devices: 35.4 us -> 1.73 us
  matrix products: 32.4 us -> 0 us
  local copies, waits for them, and re-layouts: 35.5 us -> 9.37 us
  Pallas kernels: 0 us -> 24.6 us
  starting transfers between devices: 21.1 us -> 14.3 us
    reduce_sum x125 -> x0, other arithmetic: 82.1 us -> none  [the longest x120 81 us: step(): sums.append(jnp.sum(carry, axis=0))]
    all_to_all x3 -> x0, waiting for transfers between devices: 34.1 us -> none  [the longest x1 26 us: shards(): lax.all_to_all(copied, ('sec', 'col'), split_axis=0, concat_axis=0, tiled...]
    dot_general x1 -> x0, matrix products: 32.4 us -> none  [radiate(): z = jnp.einsum('glk,mk->lgm', absorb, rows, precision=lax.Precision.HIGHEST)]
    pallas_call x0 -> x8, Pallas kernels: none -> 24.6 us  [the longest x4 18.9 us: flux(): pl.pallas_call(functools.partial(flux_body, block, scale), out_shape=jax....]
    while x2 -> x0, local copies, waits for them, and re-layouts: 15.9 us -> none  [sweep(): last, sums = lax.scan(step, start, (t_blocks, s_blocks), reverse=reverse)]
    all_to_all x3 -> x0, starting transfers between devices: 15.7 us -> none  [the longest x1 7.3 us: shards(): lax.all_to_all(lights, ('sec', 'col'), split_axis=0, concat_axis=0, tiled...]
    gather x7 -> x0, local copies, waits for them, and re-layouts: 9.87 us -> none  [the longest x2 3.6 us: shards(): bright = jnp.take(cosine, order).reshape(c_dev, 4).mean(axis=1)]
    ppermute x2 -> x8, starting transfers between devices: 5.39 us -> 14.3 us  [the longest x6 8.23 us: swap(): return lax.ppermute(x, 'sec', [(i, i ^ m) for i in range(n_sec)])]
  transfers between devices with their start and end apart: 5 -> 8, of which waited for: 3 -> 1; matrix products, arithmetic and copies ran while one was open for 4% -> 0% of each run, Pallas kernels for 0% -> 45%
where the time goes in v1:
time: 51.2 us; the launch traced here: 50.8 us
  Pallas kernels  24.6 us (48%)
  starting transfers between devices  14.3 us (28%)
  local copies, waits for them, and re-layouts  9.37 us (18%)
  waiting for transfers between devices  1.73 us (3%)
  between operations  0.74 us (1%)
    pallas_call x4, Pallas kernels, flux(): pl.pallas_call(functools.partial(flux_body, block, scale), out_shape=jax....  18.9 us
    unnamed x18, local copies, waits for them, and re-layouts  9.37 us
    ppermute x6, starting transfers between devices, swap(): return lax.ppermute(x, 'sec', [(i, i ^ m) for i in range(n_sec)])  8.23 us
    ppermute x1, starting transfers between devices, shards(): second = lax.ppermute(total, ('sec', 'col'), across)  6.02 us
    pallas_call x1, Pallas kernels, prepare(): pl.pallas_call(prepare_body, out_shape=(table, table), grid=(levels // bl...  3.27 us
    ppermute x1, waiting for transfers between devices, shards(): second = lax.ppermute(total, ('sec', 'col'), across)  1.67 us
    pallas_call x1, Pallas kernels, group(): pl.pallas_call(group_body, out_shape=jax.ShapeDtypeStruct((feat + 8, coar...  1.07 us
  transfers between devices with their start and end apart: 8, of which 1 were waited for; matrix products, arithmetic and copies ran while one was open for 0% of the time, Pallas kernels for 45%

profile of v1, /device:TPU:0, one launch (start us, length us, event | category | flops | bytes accessed | tf_op | source)
XLA Modules:
  0.0 50.8 jit_solution(14894425033279816465)
XLA Ops:
  0.7 1.2 %copy-done.1 = f32[512,7,64]{0,2,1:T(8,128)S(1)} copy-done((f32[512,7,64]{0,2,1:T(8,128)S(1)}, f32[512,7,64]{0,2,1:T(8,128)}, u32[]{:S(2)}) %copy-start.1) | copy-done | bytes 917528
  1.8 0.7 %copy-done.5 = f32[512]{0:T(512)S(1)} copy-done((f32[512]{0:T(512)S(1)}, f32[512]{0:T(512)}, u32[]{:S(2)}) %copy-start.5) | copy-done | bytes 2072
  2.5 0.7 %copy-done.6 = s32[1,512]{1,0:T(1,128)S(1)} copy-done((s32[1,512]{1,0:T(1,128)S(1)}, s32[1,512]{1,0:T(1,128)}, u32[]{:S(2)}) %copy-start.6) | copy-done | bytes 2072
  3.2 1.1 %group.1.rows = f32[456,128]{1,0:T(8,128)S(1)} custom-call(f32[448,512]{1,0:T(8,128)S(1)} %bitcast.7, f32[1,512]{1,0:T(1,128)S(1)} %bitcast.8, s32[1,512]{1,0:T(1,128)S(1)} %copy-done.6, s32[1]{0:T(128)S(6)} %copy.11.sunlit), custom_call_target="tpu_custom_call" | custom-call | flops 234881024 | bytes 917504 | tf_op jit(solution)/shard_map/group/pallas_call | solution.py:53
  4.3 3.0 %collective-permute-start = (f32[456,128]{1,0:T(8,128)S(1)}, f32[456,128]{1,0:T(8,128)S(1)}, u32[]{:S(2)}, u32[]{:S(2)}) collective-permute-start(f32[456,128]{1,0:T(8,128)S(1)} %group.1.rows), channel_id=1, source_target_pairs={{0,8},{8,0},{16,24},{24,16},{1,9},{9,1},{17,25},{25,17},{2,10},{10... | collective-permute-start | bytes 700424 | tf_op jit(solution)/shard_map/ppermute | solution.py:273
  7.3 1.5 %collective-permute-start.2 = (f32[456,128]{1,0:T(8,128)S(1)}, f32[456,128]{1,0:T(8,128)S(1)}, u32[]{:S(2)}, u32[]{:S(2)}) collective-permute-start(f32[456,128]{1,0:T(8,128)S(1)} %group.1.rows), channel_id=1, source_target_pairs={{0,16},{8,24},{16,0},{24,8},{1,17},{9,25},{17,1},{25,9},{2,18},{10... | collective-permute-start | bytes 700424 | tf_op jit(solution)/shard_map/ppermute | solution.py:273
  8.8 0.7 %copy-done.3 = s32[3,512]{1,0:T(4,128)S(1)} copy-done((s32[3,512]{1,0:T(4,128)S(1)}, s32[3,512]{1,0:T(4,128)}, u32[]{:S(2)}) %copy-start.3) | copy-done | bytes 6168
  9.5 0.7 %copy-done.4 = f32[3,512]{1,0:T(4,128)S(1)} copy-done((f32[3,512]{1,0:T(4,128)S(1)}, f32[3,512]{1,0:T(4,128)}, u32[]{:S(2)}) %copy-start.4) | copy-done | bytes 6168
  10.2 0.7 %copy-done.7 = f32[64]{0:T(128)S(1)} copy-done((f32[64]{0:T(128)S(1)}, f32[64]{0:T(128)}, u32[]{:S(2)}) %copy-start.7) | copy-done | bytes 280
  10.9 0.7 %copy-done.8 = f32[64]{0:T(128)S(1)} copy-done((f32[64]{0:T(128)S(1)}, f32[64]{0:T(128)}, u32[]{:S(2)}) %copy-start.8) | copy-done | bytes 280
  11.5 0.5 tables.1
  12.0 3.4 %copy-done = f32[64,64,448]{2,1,0:T(8,128)S(1)} copy-done((f32[64,64,448]{2,1,0:T(8,128)S(1)}, f32[64,64,448]{2,1,0:T(8,128)}, u32[]{:S(2)}) %copy-start) | copy-done | bytes 7340056
  15.4 0.8 %copy-done.2 = f32[64,64]{1,0:T(8,128)S(1)} copy-done((f32[64,64]{1,0:T(8,128)S(1)}, f32[64,64]{1,0:T(8,128)}, u32[]{:S(2)}) %copy-start.2) | copy-done | bytes 16408
  16.1 3.3 %prepare.1 = (bf16[64,64,512]{2,1,0:T(8,128)(2,1)S(1)}, bf16[64,64,512]{2,1,0:T(8,128)(2,1)S(1)}) custom-call(f32[64,64,448]{2,1,0:T(8,128)S(1)} %copy-done, f32[64,64]{1,0:T(8,128)S(1)} %copy-done.2), custom_call_target="tpu_custom_call" | custom-call | flops 18350080 | bytes 16777216 | tf_op jit(solution)/shard_map/prepare/pallas_call | solution.py:129
  19.4 4.7 %flux.5 = f32[64,128]{1,0:T(8,128)S(1)} custom-call(bf16[64,64,512]{2,1,0:T(8,128)(2,1)S(1)} %get-tuple-element.11.high, bf16[64,64,512]{2,1,0:T(8,128)(2,1)S(1)} %get-tuple-element.12.low, f32[456,128]{1,0:T(8,128)S(1)} %collective-permute-done.rows, f32[64,128]{1,0:T(8,128)S(1)} %get-tuple-element.13.planck, f32[64,128]{1,0:T(8,128)S(1)} %get-tuple-element.14.share), custom_call_target="tpu_custom_call" | custom-call | flops 2147483648 | bytes 8388608 | tf_op jit(solution)/shard_map/flux/pallas_call | solution.py:217
  24.2 2.0 %collective-permute-start.1 = (f32[64,128]{1,0:T(8,128)S(1)}, f32[64,128]{1,0:T(8,128)S(1)}, u32[]{:S(2)}, u32[]{:S(2)}) collective-permute-start(f32[64,128]{1,0:T(8,128)S(1)} %flux.5), channel_id=1, source_target_pairs={{0,8},{8,0},{16,24},{24,16},{1,9},{9,1},{17,25},{25,17},{2,10},{10... | collective-permute-start | bytes 98312 | tf_op jit(solution)/shard_map/ppermute | solution.py:273
  26.2 4.7 %flux.6 = f32[64,128]{1,0:T(8,128)S(1)} custom-call(bf16[64,64,512]{2,1,0:T(8,128)(2,1)S(1)} %get-tuple-element.11.high, bf16[64,64,512]{2,1,0:T(8,128)(2,1)S(1)} %get-tuple-element.12.low, f32[456,128]{1,0:T(8,128)S(1)} %collective-permute-done.2.rows, f32[64,128]{1,0:T(8,128)S(1)} %get-tuple-element.13.planck, f32[64,128]{1,0:T(8,128)S(1)} %get-tuple-element.14.share), custom_call_target="tpu_custom_call" | custom-call | flops 2147483648 | bytes 8388608 | tf_op jit(solution)/shard_map/flux/pallas_call | solution.py:217
  30.9 1.6 %collective-permute-start.3 = (f32[64,128]{1,0:T(8,128)S(1)}, f32[64,128]{1,0:T(8,128)S(1)}, u32[]{:S(2)}, u32[]{:S(2)}) collective-permute-start(f32[64,128]{1,0:T(8,128)S(1)} %flux.6), channel_id=1, source_target_pairs={{0,16},{8,24},{16,0},{24,8},{1,17},{9,25},{17,1},{25,9},{2,18},{10... | collective-permute-start | bytes 98312 | tf_op jit(solution)/shard_map/ppermute | solution.py:273
  32.5 4.7 %flux.7 = f32[64,128]{1,0:T(8,128)S(1)} custom-call(bf16[64,64,512]{2,1,0:T(8,128)(2,1)S(1)} %get-tuple-element.11.high, bf16[64,64,512]{2,1,0:T(8,128)(2,1)S(1)} %get-tuple-element.12.low, f32[456,128]{1,0:T(8,128)S(1)} %collective-permute-done.4.rows, f32[64,128]{1,0:T(8,128)S(1)} %get-tuple-element.13.planck, f32[64,128]{1,0:T(8,128)S(1)} %get-tuple-element.14.share), custom_call_target="tpu_custom_call" | custom-call | flops 2147483648 | bytes 8388608 | tf_op jit(solution)/shard_map/flux/pallas_call | solution.py:217
  37.2 0.1 collective-permute-start.5
  37.3 4.7 %flux.4 = f32[64,128]{1,0:T(8,128)S(1)} custom-call(bf16[64,64,512]{2,1,0:T(8,128)(2,1)S(1)} %get-tuple-element.11.high, bf16[64,64,512]{2,1,0:T(8,128)(2,1)S(1)} %get-tuple-element.12.low, f32[456,128]{1,0:T(8,128)S(1)} %group.1.rows, f32[64,128]{1,0:T(8,128)S(1)} %get-tuple-element.13.planck, f32[64,128]{1,0:T(8,128)S(1)} %get-tuple-element.14.share), custom_call_target="tpu_custom_call" | custom-call | flops 2147483648 | bytes 8388608 | tf_op jit(solution)/shard_map/flux/pallas_call | solution.py:217
  42.2 6.0 %collective-permute-start.7 = (f32[64,128]{1,0:T(8,128)S(1)}, f32[64,128]{1,0:T(8,128)S(1)}, u32[]{:S(2)}, u32[]{:S(2)}) collective-permute-start(f32[64,128]{1,0:T(8,128)S(1)} %add_add_fusion.own), channel_id=1, source_target_pairs={{0,31},{1,2},{2,1},{3,4},{4,3},{5,6},{6,5},{7,8},{8,7},{9,10},{10,... | collective-permute-start | bytes 98312 | tf_op jit(solution)/shard_map/ppermute | solution.py:288
  48.2 1.7 %collective-permute-done.7.second = f32[64,128]{1,0:T(8,128)S(1)} collective-permute-done((f32[64,128]{1,0:T(8,128)S(1)}, f32[64,128]{1,0:T(8,128)S(1)}, u32[]{:S(2)}, u32[]{:S(2)}) %collective-permute-start.7) | collective-permute-done | bytes 32800 | tf_op jit(solution)/shard_map/ppermute | solution.py:288
  49.9 0.9 %spread.1 = f32[64,512]{1,0:T(8,128)} custom-call(f32[64,128]{1,0:T(8,128)S(1)} %add_add_fusion.own, f32[64,128]{1,0:T(8,128)S(1)} %collective-permute-done.6.first, f32[64,128]{1,0:T(8,128)S(1)} %collective-permute-done.7.second, s32[1]{0:T(128)} %bitcast.5.parity, bf16[256,512]{1,0:T(8,128)(2,1)S(1)} %get-tuple-element.15.high, ...), custom_call_target="tpu_custom_call" | custom-call | tf_op jit(solution)/shard_map/spread/pallas_call | solution.py:252
  (19 shorter events, 0.2 us)
Async XLA Ops:
  0.7 1.2 %copy-start.1 = (f32[512,7,64]{0,2,1:T(8,128)S(1)}, f32[512,7,64]{0,2,1:T(8,128)}, u32[]{:S(2)}) copy-start(f32[512,7,64]{0,2,1:T(8,128)} %param.10) | copy-start | bytes 2752516
  1.8 0.7 %copy-start.5 = (f32[512]{0:T(512)S(1)}, f32[512]{0:T(512)}, u32[]{:S(2)}) copy-start(f32[512]{0:T(512)} %param.11) | copy-start | bytes 6148
  2.5 0.7 %copy-start.6 = (s32[1,512]{1,0:T(1,128)S(1)}, s32[1,512]{1,0:T(1,128)}, u32[]{:S(2)}) copy-start(s32[1,512]{1,0:T(1,128)} %grouping.1) | copy-start | bytes 6148
  4.3 15.2 %collective-permute-start = (f32[456,128]{1,0:T(8,128)S(1)}, f32[456,128]{1,0:T(8,128)S(1)}, u32[]{:S(2)}, u32[]{:S(2)}) collective-permute-start(f32[456,128]{1,0:T(8,128)S(1)} %group.1.rows), channel_id=1, source_target_pairs={{0,8},{8,0},{16,24},{24,16},{1,9},{9,1},{17,25},{25,17},{2,10},{10... | collective-permute-start | bytes 700424 | tf_op jit(solution)/shard_map/ppermute | solution.py:273
  7.3 18.9 %collective-permute-start.2 = (f32[456,128]{1,0:T(8,128)S(1)}, f32[456,128]{1,0:T(8,128)S(1)}, u32[]{:S(2)}, u32[]{:S(2)}) collective-permute-start(f32[456,128]{1,0:T(8,128)S(1)} %group.1.rows), channel_id=1, source_target_pairs={{0,16},{8,24},{16,0},{24,8},{1,17},{9,25},{17,1},{25,9},{2,18},{10... | collective-permute-start | bytes 700424 | tf_op jit(solution)/shard_map/ppermute | solution.py:273
  8.8 23.7 %collective-permute-start.4 = (f32[456,128]{1,0:T(8,128)S(1)}, f32[456,128]{1,0:T(8,128)S(1)}, u32[]{:S(2)}, u32[]{:S(2)}) collective-permute-start(f32[456,128]{1,0:T(8,128)S(1)} %group.1.rows), channel_id=1, source_target_pairs={{0,24},{8,16},{16,8},{24,0},{1,25},{9,17},{17,9},{25,1},{2,26},{10... | collective-permute-start | bytes 700424 | tf_op jit(solution)/shard_map/ppermute | solution.py:273
  8.8 0.7 %copy-start.3 = (s32[3,512]{1,0:T(4,128)S(1)}, s32[3,512]{1,0:T(4,128)}, u32[]{:S(2)}) copy-start(s32[3,512]{1,0:T(4,128)} %stencil.1) | copy-start | bytes 18436
  9.5 0.7 %copy-start.4 = (f32[3,512]{1,0:T(4,128)S(1)}, f32[3,512]{1,0:T(4,128)}, u32[]{:S(2)}) copy-start(f32[3,512]{1,0:T(4,128)} %weight.1) | copy-start | bytes 18436
  10.2 0.7 %copy-start.7 = (f32[64]{0:T(128)S(1)}, f32[64]{0:T(128)}, u32[]{:S(2)}) copy-start(f32[64]{0:T(128)} %param.16) | copy-start | bytes 772
  10.9 0.7 %copy-start.8 = (f32[64]{0:T(128)S(1)}, f32[64]{0:T(128)}, u32[]{:S(2)}) copy-start(f32[64]{0:T(128)} %param.17) | copy-start | bytes 772
  12.0 3.4 %copy-start = (f32[64,64,448]{2,1,0:T(8,128)S(1)}, f32[64,64,448]{2,1,0:T(8,128)}, u32[]{:S(2)}) copy-start(f32[64,64,448]{2,1,0:T(8,128)} %absorb.1) | copy-start | bytes 22020100
  15.4 0.8 %copy-start.2 = (f32[64,64]{1,0:T(8,128)S(1)}, f32[64,64]{1,0:T(8,128)}, u32[]{:S(2)}) copy-start(f32[64,64]{1,0:T(8,128)} %bias.1) | copy-start | bytes 49156
  24.2 17.9 %collective-permute-start.1 = (f32[64,128]{1,0:T(8,128)S(1)}, f32[64,128]{1,0:T(8,128)S(1)}, u32[]{:S(2)}, u32[]{:S(2)}) collective-permute-start(f32[64,128]{1,0:T(8,128)S(1)} %flux.5), channel_id=1, source_target_pairs={{0,8},{8,0},{16,24},{24,16},{1,9},{9,1},{17,25},{25,17},{2,10},{10... | collective-permute-start | bytes 98312 | tf_op jit(solution)/shard_map/ppermute | solution.py:273
  30.9 11.1 %collective-permute-start.3 = (f32[64,128]{1,0:T(8,128)S(1)}, f32[64,128]{1,0:T(8,128)S(1)}, u32[]{:S(2)}, u32[]{:S(2)}) collective-permute-start(f32[64,128]{1,0:T(8,128)S(1)} %flux.6), channel_id=1, source_target_pairs={{0,16},{8,24},{16,0},{24,8},{1,17},{9,25},{17,1},{25,9},{2,18},{10... | collective-permute-start | bytes 98312 | tf_op jit(solution)/shard_map/ppermute | solution.py:273
  37.2 4.9 %collective-permute-start.5 = (f32[64,128]{1,0:T(8,128)S(1)}, f32[64,128]{1,0:T(8,128)S(1)}, u32[]{:S(2)}, u32[]{:S(2)}) collective-permute-start(f32[64,128]{1,0:T(8,128)S(1)} %flux.7), channel_id=1, source_target_pairs={{0,24},{8,16},{16,8},{24,0},{1,25},{9,17},{17,9},{25,1},{2,26},{10... | collective-permute-start | bytes 98312 | tf_op jit(solution)/shard_map/ppermute | solution.py:273
  42.1 6.1 %collective-permute-start.6 = (f32[64,128]{1,0:T(8,128)S(1)}, f32[64,128]{1,0:T(8,128)S(1)}, u32[]{:S(2)}, u32[]{:S(2)}) collective-permute-start(f32[64,128]{1,0:T(8,128)S(1)} %add_add_fusion.own), channel_id=1, source_target_pairs={{0,1},{1,0},{2,3},{3,2},{4,5},{5,4},{6,7},{7,6},{8,9},{9,8},{10,11... | collective-permute-start | bytes 98312 | tf_op jit(solution)/shard_map/ppermute | solution.py:289
  42.2 7.7 %collective-permute-start.7 = (f32[64,128]{1,0:T(8,128)S(1)}, f32[64,128]{1,0:T(8,128)S(1)}, u32[]{:S(2)}, u32[]{:S(2)}) collective-permute-start(f32[64,128]{1,0:T(8,128)S(1)} %add_add_fusion.own), channel_id=1, source_target_pairs={{0,31},{1,2},{2,1},{3,4},{4,3},{5,6},{6,5},{7,8},{8,7},{9,10},{10,... | collective-permute-start | bytes 98312 | tf_op jit(solution)/shard_map/ppermute | solution.py:288

commit v2 on v1

v2 whole, which is shorter than its diff:
```python
import functools

import jax
import jax.numpy as jnp
from jax import lax
from jax.experimental import pallas as pl
from jax.experimental.pallas import tpu as pltpu
from jax.sharding import PartitionSpec as P

RIM = 8
MIB = 1 << 20
bf16 = jnp.bfloat16
f32 = jnp.float32
VMEM = pl.BlockSpec(memory_space=pltpu.VMEM)


def split(x, parts):
    terms = []
    for _ in range(parts):
        term = x.astype(bf16)
        terms.append(term)
        x = x - term.astype(f32)
    return terms


def dot(a, b):
    return jnp.dot(a, b, preferred_element_type=f32)


HBM = pl.BlockSpec(memory_space=pltpu.HBM)


def stay(x):
    return pltpu.with_memory_space_constraint(x, pltpu.HBM)


def group_body(state_in, cosine_in, grouping_in, sunlit, out, state, cosine, grouping, sems):
    copies = [
        pltpu.make_async_copy(source, target, sems.at[i])
        for i, (source, target) in enumerate(
            ((grouping_in, grouping), (cosine_in, cosine), (state_in, state))
        )
    ]
    for copy in copies:
        copy.start()
    feat, fine = state.shape
    coarse = out.shape[1]
    place = lax.broadcasted_iota(jnp.int32, (fine, fine), 0)
    member = lax.broadcasted_iota(jnp.int32, (fine, coarse), 0) // 4
    home = lax.broadcasted_iota(jnp.int32, (fine, coarse), 1)
    mean = jnp.where(member == home, 0.25, 0.0).astype(bf16)
    copies[0].wait()
    picks = jnp.where(place == grouping[...], 1.0, 0.0).astype(bf16)
    weights = dot(picks, mean).astype(bf16)
    copies[1].wait()
    copies[2].wait()
    total = jnp.zeros((feat, coarse), f32)
    for term in split(state[...], 3)[::-1]:
        total = total + dot(term, weights)
    out[0:feat, :] = total
    light = jnp.zeros((8, coarse), f32)
    for term in split(jnp.broadcast_to(cosine[...], (8, fine)), 3)[::-1]:
        light = light + dot(term, weights)
    lane = lax.broadcasted_iota(jnp.int32, (8, coarse), 1)
    out[feat : feat + 8, :] = jnp.where(lane < sunlit[0], 4.0 * light, 0.0)


def group(state, cosine, grouping, sunlit):
    feat, fine = state.shape
    coarse = fine // 4
    return pl.pallas_call(
        group_body,
        out_shape=jax.ShapeDtypeStruct((feat + 8, coarse), f32),
        in_specs=[HBM, HBM, HBM, pl.BlockSpec(memory_space=pltpu.SMEM)],
        out_specs=VMEM,
        scratch_shapes=[
            pltpu.VMEM((feat, fine), f32),
            pltpu.VMEM((1, fine), f32),
            pltpu.VMEM((1, fine), jnp.int32),
            pltpu.SemaphoreType.DMA((3,)),
        ],
        compiler_params=pltpu.CompilerParams(vmem_limit_bytes=16 * MIB),
        cost_estimate=pl.CostEstimate(
            flops=8 * feat * fine * coarse, bytes_accessed=4 * feat * fine, transcendentals=0
        ),
        name="group",
    )(stay(state), stay(cosine), stay(grouping), sunlit)


def prepare_body(
    block,
    absorb_in,
    bias_in,
    planck_in,
    share_in,
    stencil_in,
    weight_in,
    table,
    planck_out,
    share_out,
    high,
    low,
    absorb,
    bias,
    planck,
    share,
    stencil,
    weight,
    sems,
):
    levels, g, double = table.shape
    depth = double // 2
    blocks = levels // block
    small = [
        pltpu.make_async_copy(source, target, sems.at[i])
        for i, (source, target) in enumerate(
            (
                (bias_in, bias),
                (planck_in, planck),
                (share_in, share),
                (stencil_in, stencil),
                (weight_in, weight),
            )
        )
    ]
    large = [
        pltpu.make_async_copy(
            absorb_in.at[:, pl.ds(i * block, block), :], absorb.at[i], sems.at[len(small) + i]
        )
        for i in range(blocks)
    ]
    for copy in small + large:
        copy.start()
    for copy in small:
        copy.wait()

    def column(row):
        n = row.shape[1]
        eye = lax.broadcasted_iota(jnp.int32, (n, n), 0) == lax.broadcasted_iota(
            jnp.int32, (n, n), 1
        )
        return jnp.sum(jnp.where(eye, row, 0.0), axis=1, keepdims=True)

    planck_out[...] = jnp.broadcast_to(column(planck[...]), planck_out.shape)
    share_out[...] = jnp.broadcast_to(column(share[...]), share_out.shape)
    wide, fine = high.shape
    place = lax.broadcasted_iota(jnp.int32, (wide, fine), 0)
    total = jnp.zeros((wide, fine), f32)
    for k in range(stencil.shape[0]):
        at = stencil[k : k + 1, :]
        spot = jnp.where(at < RIM, wide - RIM + at, at - RIM)
        total = total + jnp.where(place == spot, weight[k : k + 1, :], 0.0)
    parts = split(total, 2)
    high[...] = parts[0]
    low[...] = parts[1]

    b = bias[...]
    lane = lax.broadcasted_iota(jnp.int32, b.shape, 1)
    for i in range(blocks):
        large[i].wait()
        for j in range(block):
            tail = jnp.where(lane == i * block + j, b, 0.0)
            parts = split(jnp.concatenate([absorb[i, :, j, :], tail], axis=1), 2)
            table[i * block + j, :, 0:depth] = parts[0]
            table[i * block + j, :, depth:double] = parts[1]


def prepare(absorb, bias, planck, share, stencil, weight, coarse):
    g, levels, feat = absorb.shape
    fine = stencil.shape[1]
    block = 8
    depth = feat + levels
    column = jax.ShapeDtypeStruct((g, coarse), f32)
    spread_table = jax.ShapeDtypeStruct((2 * coarse, fine), bf16)
    return pl.pallas_call(
        functools.partial(prepare_body, block),
        out_shape=(
            jax.ShapeDtypeStruct((levels, g, 2 * depth), bf16),
            column,
            column,
            spread_table,
            spread_table,
        ),
        in_specs=[HBM] * 6,
        out_specs=[VMEM] * 5,
        scratch_shapes=[
            pltpu.VMEM((levels // block, g, block, feat), f32),
            pltpu.VMEM(bias.shape, f32),
            pltpu.VMEM(planck.shape, f32),
            pltpu.VMEM(share.shape, f32),
            pltpu.VMEM(stencil.shape, jnp.int32),
            pltpu.VMEM(weight.shape, f32),
            pltpu.SemaphoreType.DMA((5 + levels // block,)),
        ],
        compiler_params=pltpu.CompilerParams(vmem_limit_bytes=28 * MIB),
        cost_estimate=pl.CostEstimate(
            flops=10 * g * levels * feat, bytes_accessed=8 * g * levels * depth, transcendentals=0
        ),
        name="prepare",
    )(*(stay(x) for x in (absorb, bias, planck, share, stencil, weight)))


def trans_of(z):
    low = jnp.log(1.0 + jnp.exp(jnp.minimum(z, 40.0)))
    return jnp.exp(-0.1 * jnp.maximum(low, z))


def flux_body(block, scale, table, first, second, planck, share, out, other, right, zs, ts, downs, warms):
    levels, g, double = table.shape
    depth = double // 2
    feat = depth - levels
    half = first.shape[1]
    n = 2 * half
    blocks = levels // block
    for i, rows in enumerate((first, second)):
        lanes = slice(half * i, half * (i + 1))
        parts = split(rows[0:feat, :], 2)
        right[0:feat, lanes] = parts[0]
        right[depth : depth + feat, lanes] = parts[1]
        warms[0:levels, lanes] = 2.0 + jnp.tanh(rows[0:levels, :])
    right[feat:depth, :] = jnp.ones((levels, n), bf16)
    right[depth + feat : double, :] = jnp.zeros((levels, n), bf16)
    warms[levels : levels + 8, :] = jnp.zeros((8, n), f32)
    weight = jnp.concatenate([planck[...]] * 2, axis=1)

    def fold(x):
        return jnp.sum(x.reshape(g // 8, 8, n), axis=0)

    def absorb(b, slot):
        a = table[pl.ds(b * block, block)].reshape(block * g, double)
        c = right[0:depth, :]
        z = dot(a[:, 0:depth], c) + dot(a[:, depth:double], c)
        zs[slot] = z + dot(a[:, 0:depth], right[depth:double, :])

    def fall(b, slot, d):
        for j in range(block):
            l = b * block + j
            t = trans_of(zs[slot, j * g : (j + 1) * g, :])
            ts[l] = t
            d = t * d + weight * (warms[pl.ds(l, 1), :] - warms[pl.ds(l + 1, 1), :])
            downs[l + 1] = fold(d)
        return d

    lights = [rows[feat : feat + 1, :] for rows in (first, second)]
    d = jnp.concatenate([share[...]] * 2, axis=1) * jnp.concatenate(lights, axis=1)
    d = d - weight * warms[0:1, :]
    downs[0] = fold(d)
    absorb(0, 0)

    def step(i, d):
        absorb(2 * i + 1, 1)
        d = fall(2 * i, 0, d)
        absorb(jnp.minimum(2 * i + 2, blocks - 1), 0)
        return fall(2 * i + 1, 1, d)

    d = lax.fori_loop(0, blocks // 2, step, d)
    v = 0.3 * d

    def climb(i, carry):
        v, below = carry
        l = levels - 1 - i
        rise = warms[pl.ds(l, 1), :] - warms[pl.ds(jnp.maximum(l - 1, 0), 1), :]
        v = ts[l] * v + weight * rise
        above = fold(v)
        downs[l + 1] = (downs[l] - downs[l + 1]) + (below - above)
        return v, above

    lax.fori_loop(0, levels, climb, (v, fold(v)), unroll=8)
    heat = downs[1 : levels + 1, 0, :]
    for s in range(1, 8):
        heat = heat + downs[1 : levels + 1, s, :]
    here = warms[0:levels, :]
    prior = jnp.concatenate([here[0:1], here[0 : levels - 1]], axis=0)
    total = jnp.sum(fold(weight), axis=0, keepdims=True)
    heat = scale * (heat + total * ((here - warms[1 : levels + 1, :]) + (here - prior)))
    out[...] = heat[:, 0:half]
    other[...] = heat[:, half:n]


def flux(table, first, second, planck, share, scale):
    levels, g, double = table.shape
    half = first.shape[1]
    n = 2 * half
    block = 8
    heat = jax.ShapeDtypeStruct((levels, half), f32)
    return pl.pallas_call(
        functools.partial(flux_body, block, scale),
        out_shape=(heat, heat),
        in_specs=[VMEM] * 5,
        out_specs=[VMEM] * 2,
        scratch_shapes=[
            pltpu.VMEM((double, n), bf16),
            pltpu.VMEM((2, block * g, n), f32),
            pltpu.VMEM((levels, g, n), f32),
            pltpu.VMEM((levels + 1, 8, n), f32),
            pltpu.VMEM((levels + 8, n), f32),
        ],
        compiler_params=pltpu.CompilerParams(vmem_limit_bytes=20 * MIB),
        cost_estimate=pl.CostEstimate(
            flops=3 * g * levels * double * n,
            bytes_accessed=2 * g * levels * double,
            transcendentals=3 * g * levels * n,
        ),
        name="flux",
    )(table, first, second, planck, share)


def spread_body(own, first, second, parity, high, low, out):
    n = own.shape[1]
    lane = lax.broadcasted_iota(jnp.int32, own.shape, 1)
    late = jnp.where(lane >= n // 2, 1, 0)
    halo = jnp.where(late == parity[0], first[...], second[...])
    wide = jnp.concatenate([own[...], halo], axis=1)
    a, c = split(wide, 2)
    out[...] = dot(a, high[...]) + (dot(a, low[...]) + dot(c, high[...]))


def spread(own, first, second, parity, high, low):
    levels = own.shape[0]
    fine = high.shape[1]
    return pl.pallas_call(
        spread_body,
        out_shape=jax.ShapeDtypeStruct((levels, fine), f32),
        in_specs=[VMEM] * 3 + [pl.BlockSpec(memory_space=pltpu.SMEM)] + [VMEM] * 2,
        out_specs=VMEM,
        compiler_params=pltpu.CompilerParams(vmem_limit_bytes=16 * MIB),
        name="spread",
    )(own, first, second, parity, high, low)


def shards(
    state, cosine, grouping, sunlit, absorb, level_bias, planck, solar_share, stencil, stencil_weight
):
    fine, fields, levels = state.shape
    coarse = fine // 4
    n_sec = lax.axis_size("sec")
    devices = n_sec * lax.axis_size("col")
    columns = state.transpose(1, 2, 0).reshape(fields * levels, fine)
    rows = group(columns, cosine[None], grouping, sunlit)

    def swap(x, m):
        return lax.ppermute(x, "sec", [(i, i ^ m) for i in range(n_sec)])

    got = [rows] + [swap(rows, m) for m in range(1, n_sec)]
    table, weight, share, near, far = prepare(
        absorb, level_bias, planck[None], solar_share[None], stencil, stencil_weight, coarse
    )
    scale = 4.0 / (planck.shape[0] * n_sec)
    total, last = flux(table, got[0], got[1], weight, share, scale)
    returned = [swap(last, 1)]
    for m in range(2, n_sec, 2):
        *pair, total = lax.optimization_barrier((got[m], got[m + 1], total))
        heats = flux(table, *pair, weight, share, scale)
        returned += [swap(heats[0], m), swap(heats[1], m + 1)]
    for part in returned:
        total = total + part
    pairs = [(i, i ^ 1) for i in range(devices)]
    across = [(i, (i + 1) % devices if i % 2 else (i - 1) % devices) for i in range(devices)]
    second = lax.ppermute(total, ("sec", "col"), across)
    first = lax.ppermute(total, ("sec", "col"), pairs)
    parity = jnp.bitwise_and(lax.axis_index(("sec", "col")), 1).astype(jnp.int32).reshape(1)
    return spread(total, first, second, parity, near, far)


def solution(mesh):
    placed = (
        P(("sec", "col"), None, None),
        P(("sec", "col")),
        P(("sec", "col"), None),
        P(("sec", "col")),
        P("sec", None, None),
        P("sec", None),
        P("sec"),
        P("sec"),
        P(None, ("sec", "col")),
        P(None, ("sec", "col")),
    )
    return jax.shard_map(
        shards, mesh=mesh, in_specs=placed, out_specs=P(None, ("sec", "col")), check_vma=False
    )
```

time: 51.2 us -> 41.5 us (0.81)
  local copies, waits for them, and re-layouts: 9.37 us -> 0 us
  waiting for transfers between devices: 1.73 us -> 7.44 us
  Pallas kernels: 24.6 us -> 20.3 us
  starting transfers between devices: 14.3 us -> 12.9 us
    unnamed x18 -> x0, local copies, waits for them, and re-layouts: 9.37 us -> none
    pallas_call x6 -> x3, Pallas kernels: 22.6 us -> 17.4 us  [the longest x2 13.3 us: flux(): pl.pallas_call(functools.partial(flux_body, block, scale), out_shape=(hea...]
    ppermute x6, waiting for transfers between devices: 0.05 us -> 4.71 us  [swap(): return lax.ppermute(x, 'sec', [(i, i ^ m) for i in range(n_sec)])]
    ppermute x1, starting transfers between devices: 6.02 us -> 4.59 us  [shards(): second = lax.ppermute(total, ('sec', 'col'), across)]
    ppermute x1, waiting for transfers between devices: 1.67 us -> 2.73 us  [shards(): second = lax.ppermute(total, ('sec', 'col'), across)]
    pallas_call x1, Pallas kernels: 1.07 us -> 1.95 us  [group(): pl.pallas_call(group_body, out_shape=jax.ShapeDtypeStruct((feat + 8, coar...]
  transfers between devices with their start and end apart: 8 -> 8, of which waited for: 1 -> 5; matrix products, arithmetic and copies ran while one was open for 0% -> 0% of each run, Pallas kernels for 45% -> 26%
where the time goes in v2:
time: 41.5 us; the launch traced here: 41.4 us
  Pallas kernels  20.3 us (49%)
  starting transfers between devices  12.9 us (31%)
  waiting for transfers between devices  7.44 us (18%)
  between operations  0.71 us (2%)
    pallas_call x2, Pallas kernels, flux(): pl.pallas_call(functools.partial(flux_body, block, scale), out_shape=(hea...  13.3 us
    ppermute x6, starting transfers between devices, swap(): return lax.ppermute(x, 'sec', [(i, i ^ m) for i in range(n_sec)])  8.24 us
    ppermute x6, waiting for transfers between devices, swap(): return lax.ppermute(x, 'sec', [(i, i ^ m) for i in range(n_sec)])  4.71 us
    ppermute x1, starting transfers between devices, shards(): second = lax.ppermute(total, ('sec', 'col'), across)  4.59 us
    pallas_call x1, Pallas kernels, prepare(): pl.pallas_call(functools.partial(prepare_body, block), out_shape=(jax.Sha...  4.09 us
    ppermute x1, waiting for transfers between devices, shards(): second = lax.ppermute(total, ('sec', 'col'), across)  2.73 us
    pallas_call x1, Pallas kernels, group(): pl.pallas_call(group_body, out_shape=jax.ShapeDtypeStruct((feat + 8, coar...  1.95 us
    pallas_call x1, Pallas kernels, spread(): pl.pallas_call(spread_body, out_shape=jax.ShapeDtypeStruct((levels, fine)...  0.9 us
  transfers between devices with their start and end apart: 8, of which 5 were waited for; matrix products, arithmetic and copies ran while one was open for 0% of the time, Pallas kernels for 26%

profile of v2, /device:TPU:0, one launch (start us, length us, event | category | flops | bytes accessed | tf_op | source)
XLA Modules:
  0.0 41.4 jit_solution(16869575803693180495)
XLA Ops:
  0.7 2.0 %group.1.first = f32[456,128]{1,0:T(8,128)S(1)} custom-call(f32[448,512]{1,0:T(8,128)} %bitcast.7, f32[1,512]{1,0:T(1,128)} %bitcast.8, s32[1,512]{1,0:T(1,128)} %grouping_in.1, s32[1]{0:T(128)S(6)} %copy.11.sunlit), custom_call_target="tpu_custom_call" | custom-call | flops 234881024 | bytes 917504 | tf_op jit(solution)/shard_map/group/pallas_call | solution.py:71
  2.6 3.0 %collective-permute-start.2 = (f32[456,128]{1,0:T(8,128)S(1)}, f32[456,128]{1,0:T(8,128)S(1)}, u32[]{:S(2)}, u32[]{:S(2)}) collective-permute-start(f32[456,128]{1,0:T(8,128)S(1)} %group.1.first), channel_id=1, source_target_pairs={{0,8},{8,0},{16,24},{24,16},{1,9},{9,1},{17,25},{25,17},{2,10},{10... | collective-permute-start | bytes 700424 | tf_op jit(solution)/shard_map/ppermute | solution.py:342
  5.6 1.5 %collective-permute-start = (f32[456,128]{1,0:T(8,128)S(1)}, f32[456,128]{1,0:T(8,128)S(1)}, u32[]{:S(2)}, u32[]{:S(2)}) collective-permute-start(f32[456,128]{1,0:T(8,128)S(1)} %group.1.first), channel_id=1, source_target_pairs={{0,16},{8,24},{16,0},{24,8},{1,17},{9,25},{17,1},{25,9},{2,18},{10... | collective-permute-start | bytes 700424 | tf_op jit(solution)/shard_map/ppermute | solution.py:342
  7.1 0.0 collective-permute-start.1
  7.2 4.1 %prepare.1 = (bf16[64,64,1024]{2,1,0:T(8,128)(2,1)S(1)}, f32[64,128]{1,0:T(8,128)S(1)}, f32[64,128]{1,0:T(8,128)S(1)}, bf16[256,512]{1,0:T(8,128)(2,1)S(1)}, bf16[256,512]{1,0:T(8,128)(2,1)S(1)}) custom-call(f32[64,64,448]{2,1,0:T(8,128)} %absorb_in.1, f32[64,64]{1,0:T(8,128)} %bias_in.1, f32[1,64]{1,0:T(1,128)} %bitcast.9, f32[1,64]{1,0:T(1,128)} %bitcast.10, ...), custom_call_target="tpu_custom_call" | custom-call | flops 18350080 | bytes 16777216 | tf_op jit(solution)/shard_map/prepare/pallas_call | solution.py:175
  11.3 0.9 %collective-permute-done.2.second = f32[456,128]{1,0:T(8,128)S(1)} collective-permute-done((f32[456,128]{1,0:T(8,128)S(1)}, f32[456,128]{1,0:T(8,128)S(1)}, u32[]{:S(2)}, u32[]{:S(2)}) %collective-permute-start.2) | collective-permute-done | bytes 233504 | tf_op jit(solution)/shard_map/ppermute | solution.py:342
  12.1 6.7 %flux.2 = (f32[64,128]{1,0:T(8,128)S(1)}, f32[64,128]{1,0:T(8,128)S(1)}) custom-call(bf16[64,64,1024]{2,1,0:T(8,128)(2,1)S(1)} %get-tuple-element.17.table, f32[456,128]{1,0:T(8,128)S(1)} %group.1.first, f32[456,128]{1,0:T(8,128)S(1)} %collective-permute-done.2.second, f32[64,128]{1,0:T(8,128)S(1)} %get-tuple-element.18.planck, ...), custom_call_target="tpu_custom_call" | custom-call | flops 3221225472 | bytes 8388608 | tf_op jit(solution)/shard_map/flux/pallas_call | solution.py:286
  18.8 0.0 collective-permute-done.first
  18.8 0.0 collective-permute-done.1.second
  18.8 6.7 %flux.3 = (f32[64,128]{1,0:T(8,128)S(1)}, f32[64,128]{1,0:T(8,128)S(1)}) custom-call(bf16[64,64,1024]{2,1,0:T(8,128)(2,1)S(1)} %get-tuple-element.17.table, f32[456,128]{1,0:T(8,128)S(1)} %collective-permute-done.first, f32[456,128]{1,0:T(8,128)S(1)} %collective-permute-done.1.second, f32[64,128]{1,0:T(8,128)S(1)} %get-tuple-element.18.planck, ...), custom_call_target="tpu_custom_call" | custom-call | flops 3221225472 | bytes 8388608 | tf_op jit(solution)/shard_map/flux/pallas_call | solution.py:286
  25.5 2.2 %collective-permute-start.4 = (f32[64,128]{1,0:T(8,128)S(1)}, f32[64,128]{1,0:T(8,128)S(1)}, u32[]{:S(2)}, u32[]{:S(2)}) collective-permute-start(f32[64,128]{1,0:T(8,128)S(1)} %get-tuple-element.25), channel_id=1, source_target_pairs={{0,16},{8,24},{16,0},{24,8},{1,17},{9,25},{17,1},{25,9},{2,18},{10... | collective-permute-start | bytes 98312 | tf_op jit(solution)/shard_map/ppermute | solution.py:342
  27.7 1.4 %collective-permute-start.5 = (f32[64,128]{1,0:T(8,128)S(1)}, f32[64,128]{1,0:T(8,128)S(1)}, u32[]{:S(2)}, u32[]{:S(2)}) collective-permute-start(f32[64,128]{1,0:T(8,128)S(1)} %get-tuple-element.26), channel_id=1, source_target_pairs={{0,24},{8,16},{16,8},{24,0},{1,25},{9,17},{17,9},{25,1},{2,26},{10... | collective-permute-start | bytes 98312 | tf_op jit(solution)/shard_map/ppermute | solution.py:342
  29.1 0.1 collective-permute-start.3
  29.2 0.4 collective-permute-done.4
  29.6 2.9 %collective-permute-done.5 = f32[64,128]{1,0:T(8,128)S(1)} collective-permute-done((f32[64,128]{1,0:T(8,128)S(1)}, f32[64,128]{1,0:T(8,128)S(1)}, u32[]{:S(2)}, u32[]{:S(2)}) %collective-permute-start.5) | collective-permute-done | bytes 32800 | tf_op jit(solution)/shard_map/ppermute | solution.py:342
  32.5 0.6 %collective-permute-done.3 = f32[64,128]{1,0:T(8,128)S(1)} collective-permute-done((f32[64,128]{1,0:T(8,128)S(1)}, f32[64,128]{1,0:T(8,128)S(1)}, u32[]{:S(2)}, u32[]{:S(2)}) %collective-permute-start.3) | collective-permute-done | bytes 32800 | tf_op jit(solution)/shard_map/ppermute | solution.py:342
  33.1 0.1 collective-permute-start.6
  33.1 4.6 %collective-permute-start.7 = (f32[64,128]{1,0:T(8,128)S(1)}, f32[64,128]{1,0:T(8,128)S(1)}, u32[]{:S(2)}, u32[]{:S(2)}) collective-permute-start(f32[64,128]{1,0:T(8,128)S(1)} %add_add_fusion.own), channel_id=1, source_target_pairs={{0,31},{1,2},{2,1},{3,4},{4,3},{5,6},{6,5},{7,8},{8,7},{9,10},{10,... | collective-permute-start | bytes 98312 | tf_op jit(solution)/shard_map/ppermute | solution.py:359
  37.7 0.0 collective-permute-done.6.first
  37.7 2.7 %collective-permute-done.7.second = f32[64,128]{1,0:T(8,128)S(1)} collective-permute-done((f32[64,128]{1,0:T(8,128)S(1)}, f32[64,128]{1,0:T(8,128)S(1)}, u32[]{:S(2)}, u32[]{:S(2)}) %collective-permute-start.7) | collective-permute-done | bytes 32800 | tf_op jit(solution)/shard_map/ppermute | solution.py:359
  40.5 0.9 %spread.1 = f32[64,512]{1,0:T(8,128)} custom-call(f32[64,128]{1,0:T(8,128)S(1)} %add_add_fusion.own, f32[64,128]{1,0:T(8,128)S(1)} %collective-permute-done.6.first, f32[64,128]{1,0:T(8,128)S(1)} %collective-permute-done.7.second, s32[1]{0:T(128)} %bitcast.5.parity, bf16[256,512]{1,0:T(8,128)(2,1)S(1)} %get-tuple-element.27.high, ...), custom_call_target="tpu_custom_call" | custom-call | tf_op jit(solution)/shard_map/spread/pallas_call | solution.py:321
  (1 shorter events, 0.0 us)
Async XLA Ops:
  2.6 9.5 %collective-permute-start.2 = (f32[456,128]{1,0:T(8,128)S(1)}, f32[456,128]{1,0:T(8,128)S(1)}, u32[]{:S(2)}, u32[]{:S(2)}) collective-permute-start(f32[456,128]{1,0:T(8,128)S(1)} %group.1.first), channel_id=1, source_target_pairs={{0,8},{8,0},{16,24},{24,16},{1,9},{9,1},{17,25},{25,17},{2,10},{10... | collective-permute-start | bytes 700424 | tf_op jit(solution)/shard_map/ppermute | solution.py:342
  5.6 13.2 %collective-permute-start = (f32[456,128]{1,0:T(8,128)S(1)}, f32[456,128]{1,0:T(8,128)S(1)}, u32[]{:S(2)}, u32[]{:S(2)}) collective-permute-start(f32[456,128]{1,0:T(8,128)S(1)} %group.1.first), channel_id=1, source_target_pairs={{0,16},{8,24},{16,0},{24,8},{1,17},{9,25},{17,1},{25,9},{2,18},{10... | collective-permute-start | bytes 700424 | tf_op jit(solution)/shard_map/ppermute | solution.py:342
  7.1 11.7 %collective-permute-start.1 = (f32[456,128]{1,0:T(8,128)S(1)}, f32[456,128]{1,0:T(8,128)S(1)}, u32[]{:S(2)}, u32[]{:S(2)}) collective-permute-start(f32[456,128]{1,0:T(8,128)S(1)} %group.1.first), channel_id=1, source_target_pairs={{0,24},{8,16},{16,8},{24,0},{1,25},{9,17},{17,9},{25,1},{2,26},{10... | collective-permute-start | bytes 700424 | tf_op jit(solution)/shard_map/ppermute | solution.py:342
  25.5 4.1 %collective-permute-start.4 = (f32[64,128]{1,0:T(8,128)S(1)}, f32[64,128]{1,0:T(8,128)S(1)}, u32[]{:S(2)}, u32[]{:S(2)}) collective-permute-start(f32[64,128]{1,0:T(8,128)S(1)} %get-tuple-element.25), channel_id=1, source_target_pairs={{0,16},{8,24},{16,0},{24,8},{1,17},{9,25},{17,1},{25,9},{2,18},{10... | collective-permute-start | bytes 98312 | tf_op jit(solution)/shard_map/ppermute | solution.py:342
  27.7 4.8 %collective-permute-start.5 = (f32[64,128]{1,0:T(8,128)S(1)}, f32[64,128]{1,0:T(8,128)S(1)}, u32[]{:S(2)}, u32[]{:S(2)}) collective-permute-start(f32[64,128]{1,0:T(8,128)S(1)} %get-tuple-element.26), channel_id=1, source_target_pairs={{0,24},{8,16},{16,8},{24,0},{1,25},{9,17},{17,9},{25,1},{2,26},{10... | collective-permute-start | bytes 98312 | tf_op jit(solution)/shard_map/ppermute | solution.py:342
  29.1 3.9 %collective-permute-start.3 = (f32[64,128]{1,0:T(8,128)S(1)}, f32[64,128]{1,0:T(8,128)S(1)}, u32[]{:S(2)}, u32[]{:S(2)}) collective-permute-start(f32[64,128]{1,0:T(8,128)S(1)} %get-tuple-element.22), channel_id=1, source_target_pairs={{0,8},{8,0},{16,24},{24,16},{1,9},{9,1},{17,25},{25,17},{2,10},{10... | collective-permute-start | bytes 98312 | tf_op jit(solution)/shard_map/ppermute | solution.py:342
  33.1 4.7 %collective-permute-start.6 = (f32[64,128]{1,0:T(8,128)S(1)}, f32[64,128]{1,0:T(8,128)S(1)}, u32[]{:S(2)}, u32[]{:S(2)}) collective-permute-start(f32[64,128]{1,0:T(8,128)S(1)} %add_add_fusion.own), channel_id=1, source_target_pairs={{0,1},{1,0},{2,3},{3,2},{4,5},{5,4},{6,7},{7,6},{8,9},{9,8},{10,11... | collective-permute-start | bytes 98312 | tf_op jit(solution)/shard_map/ppermute | solution.py:360
  33.1 7.3 %collective-permute-start.7 = (f32[64,128]{1,0:T(8,128)S(1)}, f32[64,128]{1,0:T(8,128)S(1)}, u32[]{:S(2)}, u32[]{:S(2)}) collective-permute-start(f32[64,128]{1,0:T(8,128)S(1)} %add_add_fusion.own), channel_id=1, source_target_pairs={{0,31},{1,2},{2,1},{3,4},{4,3},{5,6},{6,5},{7,8},{8,7},{9,10},{10,... | collective-permute-start | bytes 98312 | tf_op jit(solution)/shard_map/ppermute | solution.py:359

commit v3 on v2

--- a/solution.py
+++ b/solution.py
@@ -8,6 +8,7 @@
 from jax.sharding import PartitionSpec as P
 
 RIM = 8
+LOG2E = 1.4426950408889634
 MIB = 1 << 20
 bf16 = jnp.bfloat16
 f32 = jnp.float32
@@ -154,7 +155,7 @@
     high[...] = parts[0]
     low[...] = parts[1]
 
-    b = bias[...]
+    b = bias[...] * LOG2E
     lane = lax.broadcasted_iota(jnp.int32, b.shape, 1)
     for i in range(blocks):
         large[i].wait()
@@ -200,9 +201,9 @@
     )(*(stay(x) for x in (absorb, bias, planck, share, stencil, weight)))
 
 
-def trans_of(z):
-    low = jnp.log(1.0 + jnp.exp(jnp.minimum(z, 40.0)))
-    return jnp.exp(-0.1 * jnp.maximum(low, z))
+def trans_of(y):
+    low = lax.log2(1.0 + jnp.exp2(jnp.minimum(y, 64.0)))
+    return jnp.exp2(-0.1 * jnp.maximum(low, y))
 
 
 def flux_body(block, scale, table, first, second, planck, share, out, other, right, zs, ts, downs, warms):
@@ -214,7 +215,7 @@
     blocks = levels // block
     for i, rows in enumerate((first, second)):
         lanes = slice(half * i, half * (i + 1))
-        parts = split(rows[0:feat, :], 2)
+        parts = split(rows[0:feat, :] * LOG2E, 2)
         right[0:feat, lanes] = parts[0]
         right[depth : depth + feat, lanes] = parts[1]
         warms[0:levels, lanes] = 2.0 + jnp.tanh(rows[0:levels, :])
@@ -247,13 +248,10 @@
     downs[0] = fold(d)
     absorb(0, 0)
 
-    def step(i, d):
-        absorb(2 * i + 1, 1)
-        d = fall(2 * i, 0, d)
-        absorb(jnp.minimum(2 * i + 2, blocks - 1), 0)
-        return fall(2 * i + 1, 1, d)
-
-    d = lax.fori_loop(0, blocks // 2, step, d)
+    for b in range(blocks):
+        if b + 1 < blocks:
+            absorb(b + 1, (b + 1) % 2)
+        d = fall(b, b % 2, d)
     v = 0.3 * d
 
     def climb(i, carry):
@@ -281,7 +279,7 @@
     levels, g, double = table.shape
     half = first.shape[1]
     n = 2 * half
-    block = 8
+    block = 4
     heat = jax.ShapeDtypeStruct((levels, half), f32)
     return pl.pallas_call(
         functools.partial(flux_body, block, scale),
@@ -341,11 +339,13 @@
     def swap(x, m):
         return lax.ppermute(x, "sec", [(i, i ^ m) for i in range(n_sec)])
 
-    got = [rows] + [swap(rows, m) for m in range(1, n_sec)]
     table, weight, share, near, far = prepare(
         absorb, level_bias, planck[None], solar_share[None], stencil, stencil_weight, coarse
     )
     scale = 4.0 / (planck.shape[0] * n_sec)
+    got = [rows] + [swap(rows, m) for m in range(1, n_sec - 1)]
+    later, table = lax.optimization_barrier((rows, table))
+    got.append(swap(later, n_sec - 1))
     total, last = flux(table, got[0], got[1], weight, share, scale)
     returned = [swap(last, 1)]
     for m in range(2, n_sec, 2):
@@ -359,7 +359,7 @@
     second = lax.ppermute(total, ("sec", "col"), across)
     first = lax.ppermute(total, ("sec", "col"), pairs)
     parity = jnp.bitwise_and(lax.axis_index(("sec", "col")), 1).astype(jnp.int32).reshape(1)
-    return spread(total, first, second, parity, near, far)
+    return spread(total, second, first, 1 - parity, near, far)
 
 
 def solution(mesh):

time: 41.5 us -> 38.6 us (0.930)
  starting transfers between devices: 12.9 us -> 9.92 us
  waiting for transfers between devices: 7.44 us -> 9.79 us
  Pallas kernels: 20.3 us -> 18 us
    ppermute x1, starting transfers between devices: 4.59 us -> 0.9 us  [shards(): second = lax.ppermute(total, ('sec', 'col'), across)]
    ppermute x1, waiting for transfers between devices: 2.73 us -> 5.24 us  [shards(): second = lax.ppermute(total, ('sec', 'col'), across)]
    pallas_call x2, Pallas kernels: 13.3 us -> 11.1 us  [flux(): pl.pallas_call(functools.partial(flux_body, block, scale), out_shape=(hea...]
    ppermute x1, starting transfers between devices: 0.07 us -> 0.86 us  [shards(): first = lax.ppermute(total, ('sec', 'col'), pairs)]
  transfers between devices with their start and end apart: 8 -> 8, of which waited for: 5 -> 5; matrix products, arithmetic and copies ran while one was open for 0% -> 0% of each run, Pallas kernels for 26% -> 25%
where the time goes in v3:
time: 38.6 us; the launch traced here: 38.4 us
  Pallas kernels  18 us (47%)
  starting transfers between devices  9.92 us (26%)
  waiting for transfers between devices  9.79 us (25%)
  between operations  0.69 us (2%)
    pallas_call x2, Pallas kernels, flux(): pl.pallas_call(functools.partial(flux_body, block, scale), out_shape=(hea...  11.1 us
    ppermute x6, starting transfers between devices, swap(): return lax.ppermute(x, 'sec', [(i, i ^ m) for i in range(n_sec)])  8.16 us
    ppermute x1, waiting for transfers between devices, shards(): second = lax.ppermute(total, ('sec', 'col'), across)  5.24 us
    ppermute x6, waiting for transfers between devices, swap(): return lax.ppermute(x, 'sec', [(i, i ^ m) for i in range(n_sec)])  4.54 us
    pallas_call x1, Pallas kernels, prepare(): pl.pallas_call(functools.partial(prepare_body, block), out_shape=(jax.Sha...  4.09 us
    pallas_call x1, Pallas kernels, group(): pl.pallas_call(group_body, out_shape=jax.ShapeDtypeStruct((feat + 8, coar...  1.95 us
    pallas_call x1, Pallas kernels, spread(): pl.pallas_call(spread_body, out_shape=jax.ShapeDtypeStruct((levels, fine)...  0.91 us
    ppermute x1, starting transfers between devices, shards(): second = lax.ppermute(total, ('sec', 'col'), across)  0.9 us
  transfers between devices with their start and end apart: 8, of which 5 were waited for; matrix products, arithmetic and copies ran while one was open for 0% of the time, Pallas kernels for 25%

profile of v3, /device:TPU:0, one launch (start us, length us, event | category | flops | bytes accessed | tf_op | source)
XLA Modules:
  0.0 38.4 jit_solution(4237282614951074686)
XLA Ops:
  0.7 2.0 %group.1.first = f32[456,128]{1,0:T(8,128)S(1)} custom-call(f32[448,512]{1,0:T(8,128)} %bitcast.7, f32[1,512]{1,0:T(1,128)} %bitcast.8, s32[1,512]{1,0:T(1,128)} %grouping_in.1, s32[1]{0:T(128)S(6)} %copy.11.sunlit), custom_call_target="tpu_custom_call" | custom-call | flops 234881024 | bytes 917504 | tf_op jit(solution)/shard_map/group/pallas_call | solution.py:72
  2.6 3.0 %collective-permute-start.2 = (f32[456,128]{1,0:T(8,128)S(1)}, f32[456,128]{1,0:T(8,128)S(1)}, u32[]{:S(2)}, u32[]{:S(2)}) collective-permute-start(f32[456,128]{1,0:T(8,128)S(1)} %group.1.first), channel_id=1, source_target_pairs={{0,8},{8,0},{16,24},{24,16},{1,9},{9,1},{17,25},{25,17},{2,10},{10... | collective-permute-start | bytes 700424 | tf_op jit(solution)/shard_map/ppermute | solution.py:340
  5.6 1.5 %collective-permute-start = (f32[456,128]{1,0:T(8,128)S(1)}, f32[456,128]{1,0:T(8,128)S(1)}, u32[]{:S(2)}, u32[]{:S(2)}) collective-permute-start(f32[456,128]{1,0:T(8,128)S(1)} %group.1.first), channel_id=1, source_target_pairs={{0,16},{8,24},{16,0},{24,8},{1,17},{9,25},{17,1},{25,9},{2,18},{10... | collective-permute-start | bytes 700424 | tf_op jit(solution)/shard_map/ppermute | solution.py:340
  7.1 4.1 %prepare.1 = (bf16[64,64,1024]{2,1,0:T(8,128)(2,1)S(1)}, f32[64,128]{1,0:T(8,128)S(1)}, f32[64,128]{1,0:T(8,128)S(1)}, bf16[256,512]{1,0:T(8,128)(2,1)S(1)}, bf16[256,512]{1,0:T(8,128)(2,1)S(1)}) custom-call(f32[64,64,448]{2,1,0:T(8,128)} %absorb_in.1, f32[64,64]{1,0:T(8,128)} %bias_in.1, f32[1,64]{1,0:T(1,128)} %bitcast.9, f32[1,64]{1,0:T(1,128)} %bitcast.10, ...), custom_call_target="tpu_custom_call" | custom-call | flops 18350080 | bytes 16777216 | tf_op jit(solution)/shard_map/prepare/pallas_call | solution.py:176
  11.2 0.1 collective-permute-start.1
  11.3 0.0 collective-permute-done.2.second
  11.3 5.6 %flux.2 = (f32[64,128]{1,0:T(8,128)S(1)}, f32[64,128]{1,0:T(8,128)S(1)}) custom-call(bf16[64,64,1024]{2,1,0:T(8,128)(2,1)S(1)} %get-tuple-element.21.table, f32[456,128]{1,0:T(8,128)S(1)} %group.1.first, f32[456,128]{1,0:T(8,128)S(1)} %collective-permute-done.2.second, f32[64,128]{1,0:T(8,128)S(1)} %get-tuple-element.22.planck, ...), custom_call_target="tpu_custom_call" | custom-call | flops 3221225472 | bytes 8388608 | tf_op jit(solution)/shard_map/flux/pallas_call | solution.py:284
  17.0 2.1 %collective-permute-done.1.second = f32[456,128]{1,0:T(8,128)S(1)} collective-permute-done((f32[456,128]{1,0:T(8,128)S(1)}, f32[456,128]{1,0:T(8,128)S(1)}, u32[]{:S(2)}, u32[]{:S(2)}) %collective-permute-start.1) | collective-permute-done | bytes 233504 | tf_op jit(solution)/shard_map/ppermute | solution.py:340
  19.1 0.0 collective-permute-done.first
  19.1 5.4 %flux.3 = (f32[64,128]{1,0:T(8,128)S(1)}, f32[64,128]{1,0:T(8,128)S(1)}) custom-call(bf16[64,64,1024]{2,1,0:T(8,128)(2,1)S(1)} %get-tuple-element.21.table, f32[456,128]{1,0:T(8,128)S(1)} %collective-permute-done.first, f32[456,128]{1,0:T(8,128)S(1)} %collective-permute-done.1.second, f32[64,128]{1,0:T(8,128)S(1)} %get-tuple-element.22.planck, ...), custom_call_target="tpu_custom_call" | custom-call | flops 3221225472 | bytes 8388608 | tf_op jit(solution)/shard_map/flux/pallas_call | solution.py:284
  24.5 0.6 %collective-permute-start.4 = (f32[64,128]{1,0:T(8,128)S(1)}, f32[64,128]{1,0:T(8,128)S(1)}, u32[]{:S(2)}, u32[]{:S(2)}) collective-permute-start(f32[64,128]{1,0:T(8,128)S(1)} %get-tuple-element.29), channel_id=1, source_target_pairs={{0,16},{8,24},{16,0},{24,8},{1,17},{9,25},{17,1},{25,9},{2,18},{10... | collective-permute-start | bytes 98312 | tf_op jit(solution)/shard_map/ppermute | solution.py:340
  25.1 1.5 %collective-permute-start.5 = (f32[64,128]{1,0:T(8,128)S(1)}, f32[64,128]{1,0:T(8,128)S(1)}, u32[]{:S(2)}, u32[]{:S(2)}) collective-permute-start(f32[64,128]{1,0:T(8,128)S(1)} %get-tuple-element.30), channel_id=1, source_target_pairs={{0,24},{8,16},{16,8},{24,0},{1,25},{9,17},{17,9},{25,1},{2,26},{10... | collective-permute-start | bytes 98312 | tf_op jit(solution)/shard_map/ppermute | solution.py:340
  26.6 1.5 %collective-permute-start.3 = (f32[64,128]{1,0:T(8,128)S(1)}, f32[64,128]{1,0:T(8,128)S(1)}, u32[]{:S(2)}, u32[]{:S(2)}) collective-permute-start(f32[64,128]{1,0:T(8,128)S(1)} %get-tuple-element.26), channel_id=1, source_target_pairs={{0,8},{8,0},{16,24},{24,16},{1,9},{9,1},{17,25},{25,17},{2,10},{10... | collective-permute-start | bytes 98312 | tf_op jit(solution)/shard_map/ppermute | solution.py:340
  28.1 0.4 %collective-permute-done.4 = f32[64,128]{1,0:T(8,128)S(1)} collective-permute-done((f32[64,128]{1,0:T(8,128)S(1)}, f32[64,128]{1,0:T(8,128)S(1)}, u32[]{:S(2)}, u32[]{:S(2)}) %collective-permute-start.4) | collective-permute-done | bytes 32800 | tf_op jit(solution)/shard_map/ppermute | solution.py:340
  28.5 1.4 %collective-permute-done.5 = f32[64,128]{1,0:T(8,128)S(1)} collective-permute-done((f32[64,128]{1,0:T(8,128)S(1)}, f32[64,128]{1,0:T(8,128)S(1)}, u32[]{:S(2)}, u32[]{:S(2)}) %collective-permute-start.5) | collective-permute-done | bytes 32800 | tf_op jit(solution)/shard_map/ppermute | solution.py:340
  29.9 0.6 %collective-permute-done.3 = f32[64,128]{1,0:T(8,128)S(1)} collective-permute-done((f32[64,128]{1,0:T(8,128)S(1)}, f32[64,128]{1,0:T(8,128)S(1)}, u32[]{:S(2)}, u32[]{:S(2)}) %collective-permute-start.3) | collective-permute-done | bytes 32800 | tf_op jit(solution)/shard_map/ppermute | solution.py:340
  30.5 0.9 %collective-permute-start.6 = (f32[64,128]{1,0:T(8,128)S(1)}, f32[64,128]{1,0:T(8,128)S(1)}, u32[]{:S(2)}, u32[]{:S(2)}) collective-permute-start(f32[64,128]{1,0:T(8,128)S(1)} %add_add_fusion.own), channel_id=1, source_target_pairs={{0,31},{1,2},{2,1},{3,4},{4,3},{5,6},{6,5},{7,8},{8,7},{9,10},{10,... | collective-permute-start | bytes 98312 | tf_op jit(solution)/shard_map/ppermute | solution.py:359
  31.4 0.9 %collective-permute-start.7 = (f32[64,128]{1,0:T(8,128)S(1)}, f32[64,128]{1,0:T(8,128)S(1)}, u32[]{:S(2)}, u32[]{:S(2)}) collective-permute-start(f32[64,128]{1,0:T(8,128)S(1)} %add_add_fusion.own), channel_id=1, source_target_pairs={{0,1},{1,0},{2,3},{3,2},{4,5},{5,4},{6,7},{7,6},{8,9},{9,8},{10,11... | collective-permute-start | bytes 98312 | tf_op jit(solution)/shard_map/ppermute | solution.py:360
  32.3 5.2 %collective-permute-done.6.first = f32[64,128]{1,0:T(8,128)S(1)} collective-permute-done((f32[64,128]{1,0:T(8,128)S(1)}, f32[64,128]{1,0:T(8,128)S(1)}, u32[]{:S(2)}, u32[]{:S(2)}) %collective-permute-start.6) | collective-permute-done | bytes 32800 | tf_op jit(solution)/shard_map/ppermute | solution.py:359
  37.5 0.0 collective-permute-done.7.second
  37.5 0.9 %spread.1 = f32[64,512]{1,0:T(8,128)} custom-call(f32[64,128]{1,0:T(8,128)S(1)} %add_add_fusion.own, f32[64,128]{1,0:T(8,128)S(1)} %collective-permute-done.6.first, f32[64,128]{1,0:T(8,128)S(1)} %collective-permute-done.7.second, s32[1]{0:T(128)} %bitcast.5.parity, bf16[256,512]{1,0:T(8,128)(2,1)S(1)} %get-tuple-element.31.high, ...), custom_call_target="tpu_custom_call" | custom-call | tf_op jit(solution)/shard_map/spread/pallas_call | solution.py:319
  (1 shorter events, 0.0 us)
Async XLA Ops:
  2.6 8.7 %collective-permute-start.2 = (f32[456,128]{1,0:T(8,128)S(1)}, f32[456,128]{1,0:T(8,128)S(1)}, u32[]{:S(2)}, u32[]{:S(2)}) collective-permute-start(f32[456,128]{1,0:T(8,128)S(1)} %group.1.first), channel_id=1, source_target_pairs={{0,8},{8,0},{16,24},{24,16},{1,9},{9,1},{17,25},{25,17},{2,10},{10... | collective-permute-start | bytes 700424 | tf_op jit(solution)/shard_map/ppermute | solution.py:340
  5.6 13.5 %collective-permute-start = (f32[456,128]{1,0:T(8,128)S(1)}, f32[456,128]{1,0:T(8,128)S(1)}, u32[]{:S(2)}, u32[]{:S(2)}) collective-permute-start(f32[456,128]{1,0:T(8,128)S(1)} %group.1.first), channel_id=1, source_target_pairs={{0,16},{8,24},{16,0},{24,8},{1,17},{9,25},{17,1},{25,9},{2,18},{10... | collective-permute-start | bytes 700424 | tf_op jit(solution)/shard_map/ppermute | solution.py:340
  11.2 7.8 %collective-permute-start.1 = (f32[456,128]{1,0:T(8,128)S(1)}, f32[456,128]{1,0:T(8,128)S(1)}, u32[]{:S(2)}, u32[]{:S(2)}) collective-permute-start(f32[456,128]{1,0:T(8,128)S(1)} %group.1.first), channel_id=1, source_target_pairs={{0,24},{8,16},{16,8},{24,0},{1,25},{9,17},{17,9},{25,1},{2,26},{10... | collective-permute-start | bytes 700424 | tf_op jit(solution)/shard_map/ppermute | solution.py:340
  24.5 4.0 %collective-permute-start.4 = (f32[64,128]{1,0:T(8,128)S(1)}, f32[64,128]{1,0:T(8,128)S(1)}, u32[]{:S(2)}, u32[]{:S(2)}) collective-permute-start(f32[64,128]{1,0:T(8,128)S(1)} %get-tuple-element.29), channel_id=1, source_target_pairs={{0,16},{8,24},{16,0},{24,8},{1,17},{9,25},{17,1},{25,9},{2,18},{10... | collective-permute-start | bytes 98312 | tf_op jit(solution)/shard_map/ppermute | solution.py:340
  25.1 4.8 %collective-permute-start.5 = (f32[64,128]{1,0:T(8,128)S(1)}, f32[64,128]{1,0:T(8,128)S(1)}, u32[]{:S(2)}, u32[]{:S(2)}) collective-permute-start(f32[64,128]{1,0:T(8,128)S(1)} %get-tuple-element.30), channel_id=1, source_target_pairs={{0,24},{8,16},{16,8},{24,0},{1,25},{9,17},{17,9},{25,1},{2,26},{10... | collective-permute-start | bytes 98312 | tf_op jit(solution)/shard_map/ppermute | solution.py:340
  26.6 3.9 %collective-permute-start.3 = (f32[64,128]{1,0:T(8,128)S(1)}, f32[64,128]{1,0:T(8,128)S(1)}, u32[]{:S(2)}, u32[]{:S(2)}) collective-permute-start(f32[64,128]{1,0:T(8,128)S(1)} %get-tuple-element.26), channel_id=1, source_target_pairs={{0,8},{8,0},{16,24},{24,16},{1,9},{9,1},{17,25},{25,17},{2,10},{10... | collective-permute-start | bytes 98312 | tf_op jit(solution)/shard_map/ppermute | solution.py:340
  30.5 7.0 %collective-permute-start.6 = (f32[64,128]{1,0:T(8,128)S(1)}, f32[64,128]{1,0:T(8,128)S(1)}, u32[]{:S(2)}, u32[]{:S(2)}) collective-permute-start(f32[64,128]{1,0:T(8,128)S(1)} %add_add_fusion.own), channel_id=1, source_target_pairs={{0,31},{1,2},{2,1},{3,4},{4,3},{5,6},{6,5},{7,8},{8,7},{9,10},{10,... | collective-permute-start | bytes 98312 | tf_op jit(solution)/shard_map/ppermute | solution.py:359
  31.4 6.1 %collective-permute-start.7 = (f32[64,128]{1,0:T(8,128)S(1)}, f32[64,128]{1,0:T(8,128)S(1)}, u32[]{:S(2)}, u32[]{:S(2)}) collective-permute-start(f32[64,128]{1,0:T(8,128)S(1)} %add_add_fusion.own), channel_id=1, source_target_pairs={{0,1},{1,0},{2,3},{3,2},{4,5},{5,4},{6,7},{7,6},{8,9},{9,8},{10,11... | collective-permute-start | bytes 98312 | tf_op jit(solution)/shard_map/ppermute | solution.py:360

commit v4 on v3

--- a/solution.py
+++ b/solution.py
@@ -33,6 +33,12 @@
 
 def stay(x):
     return pltpu.with_memory_space_constraint(x, pltpu.HBM)
+
+
+def column_of(place, coarse):
+    quarter = coarse // 4
+    inner = jnp.where(place < 2 * quarter, place + 2 * quarter, place - quarter)
+    return jnp.where(place < quarter, place, inner)
 
 
 def group_body(state_in, cosine_in, grouping_in, sunlit, out, state, cosine, grouping, sems):
@@ -48,7 +54,7 @@
     coarse = out.shape[1]
     place = lax.broadcasted_iota(jnp.int32, (fine, fine), 0)
     member = lax.broadcasted_iota(jnp.int32, (fine, coarse), 0) // 4
-    home = lax.broadcasted_iota(jnp.int32, (fine, coarse), 1)
+    home = column_of(lax.broadcasted_iota(jnp.int32, (fine, coarse), 1), coarse)
     mean = jnp.where(member == home, 0.25, 0.0).astype(bf16)
     copies[0].wait()
     picks = jnp.where(place == grouping[...], 1.0, 0.0).astype(bf16)
@@ -62,7 +68,7 @@
     light = jnp.zeros((8, coarse), f32)
     for term in split(jnp.broadcast_to(cosine[...], (8, fine)), 3)[::-1]:
         light = light + dot(term, weights)
-    lane = lax.broadcasted_iota(jnp.int32, (8, coarse), 1)
+    lane = column_of(lax.broadcasted_iota(jnp.int32, (8, coarse), 1), coarse)
     out[feat : feat + 8, :] = jnp.where(lane < sunlit[0], 4.0 * light, 0.0)
 
 
@@ -86,6 +92,93 @@
         ),
         name="group",
     )(stay(state), stay(cosine), stay(grouping), sunlit)
+
+
+def trans_of(y):
+    low = lax.log2(1.0 + jnp.exp2(jnp.minimum(y, 64.0)))
+    return jnp.exp2(-0.1 * jnp.maximum(low, y))
+
+
+def sweeps(block, scale, table, chunks, planck, share, outs, scratch):
+    right, zs, ts, downs, warms = scratch
+    levels, g, double = table.shape
+    depth = double // 2
+    feat = depth - levels
+    half = chunks[0].shape[1]
+    count = len(chunks)
+    n = count * half
+    blocks = levels // block
+    top = 0 if count == 1 else depth
+    for i, rows in enumerate(chunks):
+        lanes = slice(half * i, half * (i + 1))
+        under = slice(half, 2 * half) if count == 1 else lanes
+        parts = split(rows[0:feat, :] * LOG2E, 2)
+        right[0:feat, lanes] = parts[0]
+        right[top : top + feat, under] = parts[1]
+        warms[0:levels, lanes] = 2.0 + jnp.tanh(rows[0:levels, :])
+        right[feat:depth, lanes] = jnp.ones((levels, half), bf16)
+        right[top + feat : top + depth, under] = jnp.zeros((levels, half), bf16)
+    warms[levels : levels + 8, :] = jnp.zeros((8, n), f32)
+
+    def fold(x):
+        return jnp.sum(x.reshape(g // 8, 8, n), axis=0)
+
+    def absorb(b):
+        a = table[b * block : (b + 1) * block].reshape(block * g, double)
+        c = right[0:depth, :]
+        z = dot(a[:, 0:depth], c) + dot(a[:, depth:double], c)
+        if count == 1:
+            zs[b % 2] = z[:, 0:n] + z[:, n : 2 * n]
+        else:
+            zs[b % 2] = z + dot(a[:, 0:depth], right[depth:double, :])
+
+    absorb(0)
+    weight = jnp.concatenate([planck[...]] * count, axis=1)
+    lights = jnp.concatenate([rows[feat : feat + 1, :] for rows in chunks], axis=1)
+    d = jnp.concatenate([share[...]] * count, axis=1) * lights - weight * warms[0:1, :]
+    downs[0] = fold(d)
+    for b in range(blocks):
+        if b + 1 < blocks:
+            absorb(b + 1)
+        for j in range(block):
+            l = b * block + j
+            t = trans_of(zs[b % 2, j * g : (j + 1) * g, :])
+            ts[l] = t
+            d = t * d + weight * (warms[l : l + 1, :] - warms[l + 1 : l + 2, :])
+            downs[l + 1] = fold(d)
+    v = 0.3 * d
+
+    def climb(i, carry):
+        v, below = carry
+        l = levels - 1 - i
+        rise = warms[pl.ds(l, 1), :] - warms[pl.ds(jnp.maximum(l - 1, 0), 1), :]
+        v = ts[l] * v + weight * rise
+        above = fold(v)
+        downs[l + 1] = (downs[l] - downs[l + 1]) + (below - above)
+        return v, above
+
+    lax.fori_loop(0, levels, climb, (v, fold(v)), unroll=8)
+    heat = downs[1 : levels + 1, 0, :]
+    for s in range(1, 8):
+        heat = heat + downs[1 : levels + 1, s, :]
+    here = warms[0:levels, :]
+    prior = jnp.concatenate([here[0:1], here[0 : levels - 1]], axis=0)
+    total = jnp.sum(fold(weight), axis=0, keepdims=True)
+    heat = scale * (heat + total * ((here - warms[1 : levels + 1, :]) + (here - prior)))
+    wide = n // len(outs)
+    for i, out in enumerate(outs):
+        out[...] = heat[:, wide * i : wide * (i + 1)]
+
+
+def sweep_scratch(block, g, levels, depth, count, half):
+    n = count * half
+    return [
+        pltpu.VMEM((depth, 2 * n) if count == 1 else (2 * depth, n), bf16),
+        pltpu.VMEM((2, block * g, n), f32),
+        pltpu.VMEM((levels, g, n), f32),
+        pltpu.VMEM((levels + 1, 8, n), f32),
+        pltpu.VMEM((levels + 8, n), f32),
+    ]
 
 
 def prepare_body(
@@ -145,11 +238,16 @@
     planck_out[...] = jnp.broadcast_to(column(planck[...]), planck_out.shape)
     share_out[...] = jnp.broadcast_to(column(share[...]), share_out.shape)
     wide, fine = high.shape
+    quarter = wide // 6
     place = lax.broadcasted_iota(jnp.int32, (wide, fine), 0)
     total = jnp.zeros((wide, fine), f32)
     for k in range(stencil.shape[0]):
         at = stencil[k : k + 1, :]
-        spot = jnp.where(at < RIM, wide - RIM + at, at - RIM)
+        own = at - RIM
+        spot = jnp.where(own < 3 * quarter, own + quarter, own - 2 * quarter)
+        spot = jnp.where(own < quarter, own, spot)
+        spot = jnp.where(own < 0, wide + own, spot)
+        spot = jnp.where(own < 4 * quarter, spot, own)
         total = total + jnp.where(place == spot, weight[k : k + 1, :], 0.0)
     parts = split(total, 2)
     high[...] = parts[0]
@@ -172,7 +270,7 @@
     block = 8
     depth = feat + levels
     column = jax.ShapeDtypeStruct((g, coarse), f32)
-    spread_table = jax.ShapeDtypeStruct((2 * coarse, fine), bf16)
+    spread_table = jax.ShapeDtypeStruct((3 * coarse // 2, fine), bf16)
     return pl.pallas_call(
         functools.partial(prepare_body, block),
         out_shape=(
@@ -201,129 +299,62 @@
     )(*(stay(x) for x in (absorb, bias, planck, share, stencil, weight)))
 
 
-def trans_of(y):
-    low = lax.log2(1.0 + jnp.exp2(jnp.minimum(y, 64.0)))
-    return jnp.exp2(-0.1 * jnp.maximum(low, y))
-
-
-def flux_body(block, scale, table, first, second, planck, share, out, other, right, zs, ts, downs, warms):
+def flux_body(block, scale, part, table, planck, share, first, second, out, other, *scratch):
+    chunks = [first, second]
+    if part is not None:
+        joined, *scratch = scratch
+        half = joined.shape[1] // 2
+        for i, rows in enumerate(chunks):
+            joined[:, half * i : half * (i + 1)] = rows[:, half * part : half * (part + 1)]
+        chunks = [joined]
+    sweeps(block, scale, table, chunks, planck, share, [out, other], scratch)
+
+
+def flux(table, planck, share, first, second, scale, part=None):
     levels, g, double = table.shape
-    depth = double // 2
-    feat = depth - levels
-    half = first.shape[1]
-    n = 2 * half
-    blocks = levels // block
-    for i, rows in enumerate((first, second)):
-        lanes = slice(half * i, half * (i + 1))
-        parts = split(rows[0:feat, :] * LOG2E, 2)
-        right[0:feat, lanes] = parts[0]
-        right[depth : depth + feat, lanes] = parts[1]
-        warms[0:levels, lanes] = 2.0 + jnp.tanh(rows[0:levels, :])
-    right[feat:depth, :] = jnp.ones((levels, n), bf16)
-    right[depth + feat : double, :] = jnp.zeros((levels, n), bf16)
-    warms[levels : levels + 8, :] = jnp.zeros((8, n), f32)
-    weight = jnp.concatenate([planck[...]] * 2, axis=1)
-
-    def fold(x):
-        return jnp.sum(x.reshape(g // 8, 8, n), axis=0)
-
-    def absorb(b, slot):
-        a = table[pl.ds(b * block, block)].reshape(block * g, double)
-        c = right[0:depth, :]
-        z = dot(a[:, 0:depth], c) + dot(a[:, depth:double], c)
-        zs[slot] = z + dot(a[:, 0:depth], right[depth:double, :])
-
-    def fall(b, slot, d):
-        for j in range(block):
-            l = b * block + j
-            t = trans_of(zs[slot, j * g : (j + 1) * g, :])
-            ts[l] = t
-            d = t * d + weight * (warms[pl.ds(l, 1), :] - warms[pl.ds(l + 1, 1), :])
-            downs[l + 1] = fold(d)
-        return d
-
-    lights = [rows[feat : feat + 1, :] for rows in (first, second)]
-    d = jnp.concatenate([share[...]] * 2, axis=1) * jnp.concatenate(lights, axis=1)
-    d = d - weight * warms[0:1, :]
-    downs[0] = fold(d)
-    absorb(0, 0)
-
-    for b in range(blocks):
-        if b + 1 < blocks:
-            absorb(b + 1, (b + 1) % 2)
-        d = fall(b, b % 2, d)
-    v = 0.3 * d
-
-    def climb(i, carry):
-        v, below = carry
-        l = levels - 1 - i
-        rise = warms[pl.ds(l, 1), :] - warms[pl.ds(jnp.maximum(l - 1, 0), 1), :]
-        v = ts[l] * v + weight * rise
-        above = fold(v)
-        downs[l + 1] = (downs[l] - downs[l + 1]) + (below - above)
-        return v, above
-
-    lax.fori_loop(0, levels, climb, (v, fold(v)), unroll=8)
-    heat = downs[1 : levels + 1, 0, :]
-    for s in range(1, 8):
-        heat = heat + downs[1 : levels + 1, s, :]
-    here = warms[0:levels, :]
-    prior = jnp.concatenate([here[0:1], here[0 : levels - 1]], axis=0)
-    total = jnp.sum(fold(weight), axis=0, keepdims=True)
-    heat = scale * (heat + total * ((here - warms[1 : levels + 1, :]) + (here - prior)))
-    out[...] = heat[:, 0:half]
-    other[...] = heat[:, half:n]
-
-
-def flux(table, first, second, planck, share, scale):
-    levels, g, double = table.shape
-    half = first.shape[1]
-    n = 2 * half
+    width = first.shape[1]
+    count = 2 if part is None else 1
     block = 4
-    heat = jax.ShapeDtypeStruct((levels, half), f32)
+    heat = jax.ShapeDtypeStruct((levels, width * count // 2), f32)
+    joined = [] if part is None else [pltpu.VMEM(first.shape, f32)]
     return pl.pallas_call(
-        functools.partial(flux_body, block, scale),
+        functools.partial(flux_body, block, scale, part),
         out_shape=(heat, heat),
         in_specs=[VMEM] * 5,
-        out_specs=[VMEM] * 2,
-        scratch_shapes=[
-            pltpu.VMEM((double, n), bf16),
-            pltpu.VMEM((2, block * g, n), f32),
-            pltpu.VMEM((levels, g, n), f32),
-            pltpu.VMEM((levels + 1, 8, n), f32),
-            pltpu.VMEM((levels + 8, n), f32),
-        ],
+        out_specs=(VMEM, VMEM),
+        scratch_shapes=joined + sweep_scratch(block, g, levels, double // 2, count, width),
         compiler_params=pltpu.CompilerParams(vmem_limit_bytes=20 * MIB),
         cost_estimate=pl.CostEstimate(
-            flops=3 * g * levels * double * n,
+            flops=3 * g * levels * double * count * width,
             bytes_accessed=2 * g * levels * double,
-            transcendentals=3 * g * levels * n,
+            transcendentals=3 * g * levels * count * width,
         ),
         name="flux",
-    )(table, first, second, planck, share)
-
-
-def spread_body(own, first, second, parity, high, low, out):
-    n = own.shape[1]
-    lane = lax.broadcasted_iota(jnp.int32, own.shape, 1)
+    )(table, planck, share, first, second)
+
+
+def spread_body(first, second, side, far, own, back, ends, parity, high, low, out):
+    n = ends.shape[1]
+    lane = lax.broadcasted_iota(jnp.int32, ends.shape, 1)
     late = jnp.where(lane >= n // 2, 1, 0)
     halo = jnp.where(late == parity[0], first[...], second[...])
-    wide = jnp.concatenate([own[...], halo], axis=1)
+    middle = own[:, n : 2 * n] + back[:, n : 2 * n] + side[...] + far[...]
+    wide = jnp.concatenate([ends[...], middle, halo], axis=1)
     a, c = split(wide, 2)
     out[...] = dot(a, high[...]) + (dot(a, low[...]) + dot(c, high[...]))
 
 
-def spread(own, first, second, parity, high, low):
-    levels = own.shape[0]
+def spread(first, second, side, far, own, back, ends, parity, high, low):
+    levels = ends.shape[0]
     fine = high.shape[1]
     return pl.pallas_call(
         spread_body,
         out_shape=jax.ShapeDtypeStruct((levels, fine), f32),
-        in_specs=[VMEM] * 3 + [pl.BlockSpec(memory_space=pltpu.SMEM)] + [VMEM] * 2,
+        in_specs=[VMEM] * 7 + [pl.BlockSpec(memory_space=pltpu.SMEM)] + [VMEM] * 2,
         out_specs=VMEM,
         compiler_params=pltpu.CompilerParams(vmem_limit_bytes=16 * MIB),
         name="spread",
-    )(own, first, second, parity, high, low)
+    )(first, second, side, far, own, back, ends, parity, high, low)
 
 
 def shards(
@@ -339,27 +370,29 @@
     def swap(x, m):
         return lax.ppermute(x, "sec", [(i, i ^ m) for i in range(n_sec)])
 
+    scale = 4.0 / (planck.shape[0] * n_sec)
+    got = [rows, swap(rows, 1), swap(rows, 2)]
     table, weight, share, near, far = prepare(
         absorb, level_bias, planck[None], solar_share[None], stencil, stencil_weight, coarse
     )
-    scale = 4.0 / (planck.shape[0] * n_sec)
-    got = [rows] + [swap(rows, m) for m in range(1, n_sec - 1)]
     later, table = lax.optimization_barrier((rows, table))
-    got.append(swap(later, n_sec - 1))
-    total, last = flux(table, got[0], got[1], weight, share, scale)
-    returned = [swap(last, 1)]
-    for m in range(2, n_sec, 2):
-        *pair, total = lax.optimization_barrier((got[m], got[m + 1], total))
-        heats = flux(table, *pair, weight, share, scale)
-        returned += [swap(heats[0], m), swap(heats[1], m + 1)]
-    for part in returned:
-        total = total + part
+    got.append(swap(later, 3))
+    own, heat = flux(table, weight, share, got[0], got[1], scale)
+    *late, own, table = lax.optimization_barrier((*got[2:], own, table))
+    back = swap(heat, 1)
+    half = coarse // 2
+    heats = flux(table, weight, share, *late, scale, 0)
+    *late, table, h0, h1 = lax.optimization_barrier((*late, table, *heats))
+    rest = flux(table, weight, share, *late, scale, 1)
+    ends = own[:, :half] + back[:, :half] + swap(h0, 2) + swap(h1, 3)
+    ends, *rest = lax.optimization_barrier((ends, *rest))
+    side, diagonal = swap(rest[0], 2), swap(rest[1], 3)
     pairs = [(i, i ^ 1) for i in range(devices)]
     across = [(i, (i + 1) % devices if i % 2 else (i - 1) % devices) for i in range(devices)]
-    second = lax.ppermute(total, ("sec", "col"), across)
-    first = lax.ppermute(total, ("sec", "col"), pairs)
+    second = lax.ppermute(ends, ("sec", "col"), across)
+    first = lax.ppermute(ends, ("sec", "col"), pairs)
     parity = jnp.bitwise_and(lax.axis_index(("sec", "col")), 1).astype(jnp.int32).reshape(1)
-    return spread(total, second, first, 1 - parity, near, far)
+    return spread(second, first, side, diagonal, own, back, ends, 1 - parity, near, far)
 
 
 def solution(mesh):

time: 38.6 us -> 37.6 us (0.974)
  waiting for transfers between devices: 9.79 us -> 5.75 us
  starting transfers between devices: 9.92 us -> 12 us
  Pallas kernels: 18 us -> 19 us
    ppermute x2, waiting for transfers between devices: 5.24 us -> 3.17 us  [the longest x1 3.17 us: shards(): second = lax.ppermute(ends, ('sec', 'col'), across)]
    ppermute x6 -> x8, starting transfers between devices: 8.16 us -> 10.2 us  [swap(): return lax.ppermute(x, 'sec', [(i, i ^ m) for i in range(n_sec)])]
    ppermute x6 -> x8, waiting for transfers between devices: 4.54 us -> 2.58 us  [swap(): return lax.ppermute(x, 'sec', [(i, i ^ m) for i in range(n_sec)])]
    pallas_call x2 -> x3, Pallas kernels: 11.1 us -> 12 us  [flux(): pl.pallas_call(functools.partial(flux_body, block, scale, part), out_shap...]
  transfers between devices with their start and end apart: 8 -> 10, of which waited for: 5 -> 3; matrix products, arithmetic and copies ran while one was open for 0% -> 0% of each run, Pallas kernels for 25% -> 34%
where the time goes in v4:
time: 37.6 us; the launch traced here: 37.4 us
  Pallas kernels  19 us (51%)
  starting transfers between devices  12 us (32%)
  waiting for transfers between devices  5.75 us (15%)
  between operations  0.7 us (2%)
    pallas_call x3, Pallas kernels, flux(): pl.pallas_call(functools.partial(flux_body, block, scale, part), out_shap...  12 us
    ppermute x8, starting transfers between devices, swap(): return lax.ppermute(x, 'sec', [(i, i ^ m) for i in range(n_sec)])  10.2 us
    pallas_call x1, Pallas kernels, prepare(): pl.pallas_call(functools.partial(prepare_body, block), out_shape=(jax.Sha...  4.09 us
    ppermute x1, waiting for transfers between devices, shards(): second = lax.ppermute(ends, ('sec', 'col'), across)  3.17 us
    ppermute x8, waiting for transfers between devices, swap(): return lax.ppermute(x, 'sec', [(i, i ^ m) for i in range(n_sec)])  2.58 us
    pallas_call x1, Pallas kernels, group(): pl.pallas_call(group_body, out_shape=jax.ShapeDtypeStruct((feat + 8, coar...  1.95 us
    ppermute x1, starting transfers between devices, shards(): second = lax.ppermute(ends, ('sec', 'col'), across)  1.54 us
    pallas_call x1, Pallas kernels, spread(): pl.pallas_call(spread_body, out_shape=jax.ShapeDtypeStruct((levels, fine)...  0.93 us
  transfers between devices with their start and end apart: 10, of which 3 were waited for; matrix products, arithmetic and copies ran while one was open for 0% of the time, Pallas kernels for 34%

profile of v4, /device:TPU:0, one launch (start us, length us, event | category | flops | bytes accessed | tf_op | source)
XLA Modules:
  0.0 37.4 jit_solution(101493233727941683)
XLA Ops:
  0.7 2.0 %group.1.first = f32[456,128]{1,0:T(8,128)S(1)} custom-call(f32[448,512]{1,0:T(8,128)} %bitcast.7, f32[1,512]{1,0:T(1,128)} %bitcast.8, s32[1,512]{1,0:T(1,128)} %grouping_in.1, s32[1]{0:T(128)S(6)} %copy.11.sunlit), custom_call_target="tpu_custom_call" | custom-call | flops 234881024 | bytes 917504 | tf_op jit(solution)/shard_map/group/pallas_call | solution.py:78
  2.6 3.0 %collective-permute-start.2 = (f32[456,128]{1,0:T(8,128)S(1)}, f32[456,128]{1,0:T(8,128)S(1)}, u32[]{:S(2)}, u32[]{:S(2)}) collective-permute-start(f32[456,128]{1,0:T(8,128)S(1)} %group.1.first), channel_id=1, source_target_pairs={{0,8},{8,0},{16,24},{24,16},{1,9},{9,1},{17,25},{25,17},{2,10},{10... | collective-permute-start | bytes 700424 | tf_op jit(solution)/shard_map/ppermute | solution.py:371
  5.6 1.5 %collective-permute-start = (f32[456,128]{1,0:T(8,128)S(1)}, f32[456,128]{1,0:T(8,128)S(1)}, u32[]{:S(2)}, u32[]{:S(2)}) collective-permute-start(f32[456,128]{1,0:T(8,128)S(1)} %group.1.first), channel_id=1, source_target_pairs={{0,16},{8,24},{16,0},{24,8},{1,17},{9,25},{17,1},{25,9},{2,18},{10... | collective-permute-start | bytes 700424 | tf_op jit(solution)/shard_map/ppermute | solution.py:371
  7.1 4.1 %prepare.1 = (bf16[64,64,1024]{2,1,0:T(8,128)(2,1)S(1)}, f32[64,128]{1,0:T(8,128)S(1)}, f32[64,128]{1,0:T(8,128)S(1)}, bf16[192,512]{1,0:T(8,128)(2,1)S(1)}, bf16[192,512]{1,0:T(8,128)(2,1)S(1)}) custom-call(f32[64,64,448]{2,1,0:T(8,128)} %absorb_in.1, f32[64,64]{1,0:T(8,128)} %bias_in.1, f32[1,64]{1,0:T(1,128)} %bitcast.9, f32[1,64]{1,0:T(1,128)} %bitcast.10, ...), custom_call_target="tpu_custom_call" | custom-call | flops 18350080 | bytes 16777216 | tf_op jit(solution)/shard_map/prepare/pallas_call | solution.py:274
  11.2 0.1 collective-permute-start.1
  11.3 0.0 collective-permute-done.2.second
  11.3 5.5 %flux.3 = (f32[64,128]{1,0:T(8,128)S(1)}, f32[64,128]{1,0:T(8,128)S(1)}) custom-call(bf16[64,64,1024]{2,1,0:T(8,128)(2,1)S(1)} %get-tuple-element.45.table, f32[64,128]{1,0:T(8,128)S(1)} %get-tuple-element.33.planck, f32[64,128]{1,0:T(8,128)S(1)} %get-tuple-element.34.share, f32[456,128]{1,0:T(8,128)S(1)} %group.1.first, ...), custom_call_target="tpu_custom_call" | custom-call | flops 3221225472 | bytes 8388608 | tf_op jit(solution)/shard_map/flux/pallas_call | solution.py:320
  16.8 2.2 %collective-permute-done.1.second = f32[456,128]{1,0:T(8,128)S(1)} collective-permute-done((f32[456,128]{1,0:T(8,128)S(1)}, f32[456,128]{1,0:T(8,128)S(1)}, u32[]{:S(2)}, u32[]{:S(2)}) %collective-permute-start.1) | collective-permute-done | bytes 233504 | tf_op jit(solution)/shard_map/ppermute | solution.py:371
  19.1 0.0 collective-permute-done.first
  19.1 3.2 %flux.4 = (f32[64,64]{1,0:T(8,128)S(1)}, f32[64,64]{1,0:T(8,128)S(1)}) custom-call(bf16[64,64,1024]{2,1,0:T(8,128)(2,1)S(1)} %get-tuple-element.45.table, f32[64,128]{1,0:T(8,128)S(1)} %get-tuple-element.33.planck, f32[64,128]{1,0:T(8,128)S(1)} %get-tuple-element.34.share, f32[456,128]{1,0:T(8,128)S(1)} %collective-permute-done.first, ...), custom_call_target="tpu_custom_call" | custom-call | flops 1610612736 | bytes 8388608 | tf_op jit(solution)/shard_map/flux/pallas_call | solution.py:320
  22.3 0.5 %collective-permute-start.4 = (f32[64,64]{1,0:T(8,128)S(1)}, f32[64,64]{1,0:T(8,128)S(1)}, u32[]{:S(2)}, u32[]{:S(2)}) collective-permute-start(f32[64,64]{1,0:T(8,128)S(1)} %get-tuple-element.43), channel_id=1, source_target_pairs={{0,16},{8,24},{16,0},{24,8},{1,17},{9,25},{17,1},{25,9},{2,18},{10... | collective-permute-start | bytes 49160 | tf_op jit(solution)/shard_map/ppermute | solution.py:371
  22.8 1.5 %collective-permute-start.5 = (f32[64,64]{1,0:T(8,128)S(1)}, f32[64,64]{1,0:T(8,128)S(1)}, u32[]{:S(2)}, u32[]{:S(2)}) collective-permute-start(f32[64,64]{1,0:T(8,128)S(1)} %get-tuple-element.44), channel_id=1, source_target_pairs={{0,24},{8,16},{16,8},{24,0},{1,25},{9,17},{17,9},{25,1},{2,26},{10... | collective-permute-start | bytes 49160 | tf_op jit(solution)/shard_map/ppermute | solution.py:371
  24.3 1.5 %collective-permute-start.3 = (f32[64,128]{1,0:T(8,128)S(1)}, f32[64,128]{1,0:T(8,128)S(1)}, u32[]{:S(2)}, u32[]{:S(2)}) collective-permute-start(f32[64,128]{1,0:T(8,128)S(1)} %get-tuple-element.37), channel_id=1, source_target_pairs={{0,8},{8,0},{16,24},{24,16},{1,9},{9,1},{17,25},{25,17},{2,10},{10... | collective-permute-start | bytes 98312 | tf_op jit(solution)/shard_map/ppermute | solution.py:371
  25.8 3.3 %flux.5 = (f32[64,64]{1,0:T(8,128)S(1)}, f32[64,64]{1,0:T(8,128)S(1)}) custom-call(bf16[64,64,1024]{2,1,0:T(8,128)(2,1)S(1)} %get-tuple-element.45.table, f32[64,128]{1,0:T(8,128)S(1)} %get-tuple-element.33.planck, f32[64,128]{1,0:T(8,128)S(1)} %get-tuple-element.34.share, f32[456,128]{1,0:T(8,128)S(1)} %collective-permute-done.first, ...), custom_call_target="tpu_custom_call" | custom-call | flops 1610612736 | bytes 8388608 | tf_op jit(solution)/shard_map/flux/pallas_call | solution.py:320
  29.1 0.0 collective-permute-done.3.back
  29.1 1.5 %collective-permute-start.6 = (f32[64,64]{1,0:T(8,128)S(1)}, f32[64,64]{1,0:T(8,128)S(1)}, u32[]{:S(2)}, u32[]{:S(2)}) collective-permute-start(f32[64,64]{1,0:T(8,128)S(1)} %fusion.1.ends), channel_id=1, source_target_pairs={{0,31},{1,2},{2,1},{3,4},{4,3},{5,6},{6,5},{7,8},{8,7},{9,10},{10,... | collective-permute-start | bytes 49160 | tf_op jit(solution)/shard_map/ppermute | solution.py:392
  30.6 0.2 collective-permute-start.7
  30.9 0.5 %collective-permute-start.8 = (f32[64,64]{1,0:T(8,128)S(1)}, f32[64,64]{1,0:T(8,128)S(1)}, u32[]{:S(2)}, u32[]{:S(2)}) collective-permute-start(f32[64,64]{1,0:T(8,128)S(1)} %get-tuple-element.51), channel_id=1, source_target_pairs={{0,16},{8,24},{16,0},{24,8},{1,17},{9,25},{17,1},{25,9},{2,18},{10... | collective-permute-start | bytes 49160 | tf_op jit(solution)/shard_map/ppermute | solution.py:371
  31.4 1.6 %collective-permute-start.9 = (f32[64,64]{1,0:T(8,128)S(1)}, f32[64,64]{1,0:T(8,128)S(1)}, u32[]{:S(2)}, u32[]{:S(2)}) collective-permute-start(f32[64,64]{1,0:T(8,128)S(1)} %get-tuple-element.52), channel_id=1, source_target_pairs={{0,24},{8,16},{16,8},{24,0},{1,25},{9,17},{17,9},{25,1},{2,26},{10... | collective-permute-start | bytes 49160 | tf_op jit(solution)/shard_map/ppermute | solution.py:371
  33.0 3.2 %collective-permute-done.6.first = f32[64,64]{1,0:T(8,128)S(1)} collective-permute-done((f32[64,64]{1,0:T(8,128)S(1)}, f32[64,64]{1,0:T(8,128)S(1)}, u32[]{:S(2)}, u32[]{:S(2)}) %collective-permute-start.6) | collective-permute-done | bytes 16416 | tf_op jit(solution)/shard_map/ppermute | solution.py:392
  36.1 0.0 collective-permute-done.7.second
  36.1 0.0 collective-permute-done.8.side
  36.1 0.3 collective-permute-done.9.far
  36.5 0.9 %spread.1 = f32[64,512]{1,0:T(8,128)} custom-call(f32[64,64]{1,0:T(8,128)S(1)} %collective-permute-done.6.first, f32[64,64]{1,0:T(8,128)S(1)} %collective-permute-done.7.second, f32[64,64]{1,0:T(8,128)S(1)} %collective-permute-done.8.side, f32[64,64]{1,0:T(8,128)S(1)} %collective-permute-done.9.far, f32[64,128]{1,0:T(8,128)S(1)} %get-tuple-element.36.own, ...), custom_call_target="tpu_custom_call" | custom-call | tf_op jit(solution)/shard_map/spread/pallas_call | solution.py:350
  (3 shorter events, 0.0 us)
Async XLA Ops:
  2.6 8.7 %collective-permute-start.2 = (f32[456,128]{1,0:T(8,128)S(1)}, f32[456,128]{1,0:T(8,128)S(1)}, u32[]{:S(2)}, u32[]{:S(2)}) collective-permute-start(f32[456,128]{1,0:T(8,128)S(1)} %group.1.first), channel_id=1, source_target_pairs={{0,8},{8,0},{16,24},{24,16},{1,9},{9,1},{17,25},{25,17},{2,10},{10... | collective-permute-start | bytes 700424 | tf_op jit(solution)/shard_map/ppermute | solution.py:371
  5.6 13.5 %collective-permute-start = (f32[456,128]{1,0:T(8,128)S(1)}, f32[456,128]{1,0:T(8,128)S(1)}, u32[]{:S(2)}, u32[]{:S(2)}) collective-permute-start(f32[456,128]{1,0:T(8,128)S(1)} %group.1.first), channel_id=1, source_target_pairs={{0,16},{8,24},{16,0},{24,8},{1,17},{9,25},{17,1},{25,9},{2,18},{10... | collective-permute-start | bytes 700424 | tf_op jit(solution)/shard_map/ppermute | solution.py:371
  11.2 7.8 %collective-permute-start.1 = (f32[456,128]{1,0:T(8,128)S(1)}, f32[456,128]{1,0:T(8,128)S(1)}, u32[]{:S(2)}, u32[]{:S(2)}) collective-permute-start(f32[456,128]{1,0:T(8,128)S(1)} %group.1.first), channel_id=1, source_target_pairs={{0,24},{8,16},{16,8},{24,0},{1,25},{9,17},{17,9},{25,1},{2,26},{10... | collective-permute-start | bytes 700424 | tf_op jit(solution)/shard_map/ppermute | solution.py:371
  22.3 6.8 %collective-permute-start.4 = (f32[64,64]{1,0:T(8,128)S(1)}, f32[64,64]{1,0:T(8,128)S(1)}, u32[]{:S(2)}, u32[]{:S(2)}) collective-permute-start(f32[64,64]{1,0:T(8,128)S(1)} %get-tuple-element.43), channel_id=1, source_target_pairs={{0,16},{8,24},{16,0},{24,8},{1,17},{9,25},{17,1},{25,9},{2,18},{10... | collective-permute-start | bytes 49160 | tf_op jit(solution)/shard_map/ppermute | solution.py:371
  22.8 6.2 %collective-permute-start.5 = (f32[64,64]{1,0:T(8,128)S(1)}, f32[64,64]{1,0:T(8,128)S(1)}, u32[]{:S(2)}, u32[]{:S(2)}) collective-permute-start(f32[64,64]{1,0:T(8,128)S(1)} %get-tuple-element.44), channel_id=1, source_target_pairs={{0,24},{8,16},{16,8},{24,0},{1,25},{9,17},{17,9},{25,1},{2,26},{10... | collective-permute-start | bytes 49160 | tf_op jit(solution)/shard_map/ppermute | solution.py:371
  24.3 4.8 %collective-permute-start.3 = (f32[64,128]{1,0:T(8,128)S(1)}, f32[64,128]{1,0:T(8,128)S(1)}, u32[]{:S(2)}, u32[]{:S(2)}) collective-permute-start(f32[64,128]{1,0:T(8,128)S(1)} %get-tuple-element.37), channel_id=1, source_target_pairs={{0,8},{8,0},{16,24},{24,16},{1,9},{9,1},{17,25},{25,17},{2,10},{10... | collective-permute-start | bytes 98312 | tf_op jit(solution)/shard_map/ppermute | solution.py:371
  29.1 7.0 %collective-permute-start.6 = (f32[64,64]{1,0:T(8,128)S(1)}, f32[64,64]{1,0:T(8,128)S(1)}, u32[]{:S(2)}, u32[]{:S(2)}) collective-permute-start(f32[64,64]{1,0:T(8,128)S(1)} %fusion.1.ends), channel_id=1, source_target_pairs={{0,31},{1,2},{2,1},{3,4},{4,3},{5,6},{6,5},{7,8},{8,7},{9,10},{10,... | collective-permute-start | bytes 49160 | tf_op jit(solution)/shard_map/ppermute | solution.py:392
  30.6 5.5 %collective-permute-start.7 = (f32[64,64]{1,0:T(8,128)S(1)}, f32[64,64]{1,0:T(8,128)S(1)}, u32[]{:S(2)}, u32[]{:S(2)}) collective-permute-start(f32[64,64]{1,0:T(8,128)S(1)} %fusion.1.ends), channel_id=1, source_target_pairs={{0,1},{1,0},{2,3},{3,2},{4,5},{5,4},{6,7},{7,6},{8,9},{9,8},{10,11... | collective-permute-start | bytes 49160 | tf_op jit(solution)/shard_map/ppermute | solution.py:393
  30.9 5.3 %collective-permute-start.8 = (f32[64,64]{1,0:T(8,128)S(1)}, f32[64,64]{1,0:T(8,128)S(1)}, u32[]{:S(2)}, u32[]{:S(2)}) collective-permute-start(f32[64,64]{1,0:T(8,128)S(1)} %get-tuple-element.51), channel_id=1, source_target_pairs={{0,16},{8,24},{16,0},{24,8},{1,17},{9,25},{17,1},{25,9},{2,18},{10... | collective-permute-start | bytes 49160 | tf_op jit(solution)/shard_map/ppermute | solution.py:371
  31.4 5.1 %collective-permute-start.9 = (f32[64,64]{1,0:T(8,128)S(1)}, f32[64,64]{1,0:T(8,128)S(1)}, u32[]{:S(2)}, u32[]{:S(2)}) collective-permute-start(f32[64,64]{1,0:T(8,128)S(1)} %get-tuple-element.52), channel_id=1, source_target_pairs={{0,24},{8,16},{16,8},{24,0},{1,25},{9,17},{17,9},{25,1},{2,26},{10... | collective-permute-start | bytes 49160 | tf_op jit(solution)/shard_map/ppermute | solution.py:371

commit v5 on v4

--- a/solution.py
+++ b/solution.py
@@ -33,12 +33,6 @@
 
 def stay(x):
     return pltpu.with_memory_space_constraint(x, pltpu.HBM)
-
-
-def column_of(place, coarse):
-    quarter = coarse // 4
-    inner = jnp.where(place < 2 * quarter, place + 2 * quarter, place - quarter)
-    return jnp.where(place < quarter, place, inner)
 
 
 def group_body(state_in, cosine_in, grouping_in, sunlit, out, state, cosine, grouping, sems):
@@ -54,7 +48,7 @@
     coarse = out.shape[1]
     place = lax.broadcasted_iota(jnp.int32, (fine, fine), 0)
     member = lax.broadcasted_iota(jnp.int32, (fine, coarse), 0) // 4
-    home = column_of(lax.broadcasted_iota(jnp.int32, (fine, coarse), 1), coarse)
+    home = lax.broadcasted_iota(jnp.int32, (fine, coarse), 1)
     mean = jnp.where(member == home, 0.25, 0.0).astype(bf16)
     copies[0].wait()
     picks = jnp.where(place == grouping[...], 1.0, 0.0).astype(bf16)
@@ -68,7 +62,7 @@
     light = jnp.zeros((8, coarse), f32)
     for term in split(jnp.broadcast_to(cosine[...], (8, fine)), 3)[::-1]:
         light = light + dot(term, weights)
-    lane = column_of(lax.broadcasted_iota(jnp.int32, (8, coarse), 1), coarse)
+    lane = lax.broadcasted_iota(jnp.int32, (8, coarse), 1)
     out[feat : feat + 8, :] = jnp.where(lane < sunlit[0], 4.0 * light, 0.0)
 
 
@@ -165,9 +159,8 @@
     prior = jnp.concatenate([here[0:1], here[0 : levels - 1]], axis=0)
     total = jnp.sum(fold(weight), axis=0, keepdims=True)
     heat = scale * (heat + total * ((here - warms[1 : levels + 1, :]) + (here - prior)))
-    wide = n // len(outs)
     for i, out in enumerate(outs):
-        out[...] = heat[:, wide * i : wide * (i + 1)]
+        out[...] = heat[:, half * i : half * (i + 1)]
 
 
 def sweep_scratch(block, g, levels, depth, count, half):
@@ -238,16 +231,11 @@
     planck_out[...] = jnp.broadcast_to(column(planck[...]), planck_out.shape)
     share_out[...] = jnp.broadcast_to(column(share[...]), share_out.shape)
     wide, fine = high.shape
-    quarter = wide // 6
     place = lax.broadcasted_iota(jnp.int32, (wide, fine), 0)
     total = jnp.zeros((wide, fine), f32)
     for k in range(stencil.shape[0]):
         at = stencil[k : k + 1, :]
-        own = at - RIM
-        spot = jnp.where(own < 3 * quarter, own + quarter, own - 2 * quarter)
-        spot = jnp.where(own < quarter, own, spot)
-        spot = jnp.where(own < 0, wide + own, spot)
-        spot = jnp.where(own < 4 * quarter, spot, own)
+        spot = jnp.where(at < RIM, wide - RIM + at, at - RIM)
         total = total + jnp.where(place == spot, weight[k : k + 1, :], 0.0)
     parts = split(total, 2)
     high[...] = parts[0]
@@ -270,7 +258,7 @@
     block = 8
     depth = feat + levels
     column = jax.ShapeDtypeStruct((g, coarse), f32)
-    spread_table = jax.ShapeDtypeStruct((3 * coarse // 2, fine), bf16)
+    spread_table = jax.ShapeDtypeStruct((2 * coarse, fine), bf16)
     return pl.pallas_call(
         functools.partial(prepare_body, block),
         out_shape=(
@@ -299,62 +287,52 @@
     )(*(stay(x) for x in (absorb, bias, planck, share, stencil, weight)))
 
 
-def flux_body(block, scale, part, table, planck, share, first, second, out, other, *scratch):
-    chunks = [first, second]
-    if part is not None:
-        joined, *scratch = scratch
-        half = joined.shape[1] // 2
-        for i, rows in enumerate(chunks):
-            joined[:, half * i : half * (i + 1)] = rows[:, half * part : half * (part + 1)]
-        chunks = [joined]
-    sweeps(block, scale, table, chunks, planck, share, [out, other], scratch)
-
-
-def flux(table, planck, share, first, second, scale, part=None):
+def flux_body(block, scale, count, table, planck, share, *refs):
+    chunks, outs, scratch = refs[:count], refs[count : 2 * count], refs[2 * count :]
+    sweeps(block, scale, table, chunks, planck, share, outs, scratch)
+
+
+def flux(table, planck, share, chunks, scale):
     levels, g, double = table.shape
-    width = first.shape[1]
-    count = 2 if part is None else 1
+    count, half = len(chunks), chunks[0].shape[1]
     block = 4
-    heat = jax.ShapeDtypeStruct((levels, width * count // 2), f32)
-    joined = [] if part is None else [pltpu.VMEM(first.shape, f32)]
     return pl.pallas_call(
-        functools.partial(flux_body, block, scale, part),
-        out_shape=(heat, heat),
-        in_specs=[VMEM] * 5,
-        out_specs=(VMEM, VMEM),
-        scratch_shapes=joined + sweep_scratch(block, g, levels, double // 2, count, width),
+        functools.partial(flux_body, block, scale, count),
+        out_shape=(jax.ShapeDtypeStruct((levels, half), f32),) * count,
+        in_specs=[VMEM] * (3 + count),
+        out_specs=(VMEM,) * count,
+        scratch_shapes=sweep_scratch(block, g, levels, double // 2, count, half),
         compiler_params=pltpu.CompilerParams(vmem_limit_bytes=20 * MIB),
         cost_estimate=pl.CostEstimate(
-            flops=3 * g * levels * double * count * width,
+            flops=3 * g * levels * double * count * half,
             bytes_accessed=2 * g * levels * double,
-            transcendentals=3 * g * levels * count * width,
+            transcendentals=3 * g * levels * count * half,
         ),
         name="flux",
-    )(table, planck, share, first, second)
-
-
-def spread_body(first, second, side, far, own, back, ends, parity, high, low, out):
-    n = ends.shape[1]
-    lane = lax.broadcasted_iota(jnp.int32, ends.shape, 1)
+    )(table, planck, share, *chunks)
+
+
+def spread_body(own, first, second, parity, high, low, out):
+    n = own.shape[1]
+    lane = lax.broadcasted_iota(jnp.int32, own.shape, 1)
     late = jnp.where(lane >= n // 2, 1, 0)
     halo = jnp.where(late == parity[0], first[...], second[...])
-    middle = own[:, n : 2 * n] + back[:, n : 2 * n] + side[...] + far[...]
-    wide = jnp.concatenate([ends[...], middle, halo], axis=1)
+    wide = jnp.concatenate([own[...], halo], axis=1)
     a, c = split(wide, 2)
     out[...] = dot(a, high[...]) + (dot(a, low[...]) + dot(c, high[...]))
 
 
-def spread(first, second, side, far, own, back, ends, parity, high, low):
-    levels = ends.shape[0]
+def spread(own, first, second, parity, high, low):
+    levels = own.shape[0]
     fine = high.shape[1]
     return pl.pallas_call(
         spread_body,
         out_shape=jax.ShapeDtypeStruct((levels, fine), f32),
-        in_specs=[VMEM] * 7 + [pl.BlockSpec(memory_space=pltpu.SMEM)] + [VMEM] * 2,
+        in_specs=[VMEM] * 3 + [pl.BlockSpec(memory_space=pltpu.SMEM)] + [VMEM] * 2,
         out_specs=VMEM,
         compiler_params=pltpu.CompilerParams(vmem_limit_bytes=16 * MIB),
         name="spread",
-    )(first, second, side, far, own, back, ends, parity, high, low)
+    )(own, first, second, parity, high, low)
 
 
 def shards(
@@ -371,28 +349,26 @@
         return lax.ppermute(x, "sec", [(i, i ^ m) for i in range(n_sec)])
 
     scale = 4.0 / (planck.shape[0] * n_sec)
-    got = [rows, swap(rows, 1), swap(rows, 2)]
+    first, second = swap(rows, 1), swap(rows, 2)
     table, weight, share, near, far = prepare(
         absorb, level_bias, planck[None], solar_share[None], stencil, stencil_weight, coarse
     )
-    later, table = lax.optimization_barrier((rows, table))
-    got.append(swap(later, 3))
-    own, heat = flux(table, weight, share, got[0], got[1], scale)
-    *late, own, table = lax.optimization_barrier((*got[2:], own, table))
-    back = swap(heat, 1)
-    half = coarse // 2
-    heats = flux(table, weight, share, *late, scale, 0)
-    *late, table, h0, h1 = lax.optimization_barrier((*late, table, *heats))
-    rest = flux(table, weight, share, *late, scale, 1)
-    ends = own[:, :half] + back[:, :half] + swap(h0, 2) + swap(h1, 3)
-    ends, *rest = lax.optimization_barrier((ends, *rest))
-    side, diagonal = swap(rest[0], 2), swap(rest[1], 3)
+    later, table = lax.optimization_barrier((first, table))
+    third = swap(later, 2)
+    heats = flux(table, weight, share, [first, second], scale)
+    third, table, *tied = lax.optimization_barrier((third, table, heats[0]))
+    (heat,) = flux(table, weight, share, [third], scale)
+    others = swap(tied[0], 1) + swap(heats[1], 2)
+    others, heat, table, rows = lax.optimization_barrier((others, heat, table, rows))
+    last = swap(heat, 3)
+    (total,) = flux(table, weight, share, [rows], scale)
+    total = total + others + last
     pairs = [(i, i ^ 1) for i in range(devices)]
     across = [(i, (i + 1) % devices if i % 2 else (i - 1) % devices) for i in range(devices)]
-    second = lax.ppermute(ends, ("sec", "col"), across)
-    first = lax.ppermute(ends, ("sec", "col"), pairs)
+    second = lax.ppermute(total, ("sec", "col"), across)
+    first = lax.ppermute(total, ("sec", "col"), pairs)
     parity = jnp.bitwise_and(lax.axis_index(("sec", "col")), 1).astype(jnp.int32).reshape(1)
-    return spread(second, first, side, diagonal, own, back, ends, 1 - parity, near, far)
+    return spread(total, second, first, 1 - parity, near, far)
 
 
 def solution(mesh):

time: 37.6 us -> 36.8 us (0.979)
  waiting for transfers between devices: 5.75 us -> 5.31 us
    ppermute x8 -> x6, waiting for transfers between devices: 2.58 us -> 0.13 us  [swap(): return lax.ppermute(x, 'sec', [(i, i ^ m) for i in range(n_sec)])]
    ppermute x2, waiting for transfers between devices: 3.17 us -> 5.18 us  [the longest x1 5.18 us: shards(): second = lax.ppermute(total, ('sec', 'col'), across)]
    ppermute x8 -> x6, starting transfers between devices: 10.2 us -> 10.1 us  [swap(): return lax.ppermute(x, 'sec', [(i, i ^ m) for i in range(n_sec)])]
  transfers between devices with their start and end apart: 10 -> 8, of which waited for: 3 -> 2; matrix products, arithmetic and copies ran while one was open for 0% -> 0% of each run, Pallas kernels for 34% -> 43%
where the time goes in v5:
time: 36.8 us; the launch traced here: 36.6 us
  Pallas kernels  18.7 us (51%)
  starting transfers between devices  11.9 us (32%)
  waiting for transfers between devices  5.31 us (14%)
  between operations  0.72 us (2%)
    pallas_call x3, Pallas kernels, flux(): pl.pallas_call(functools.partial(flux_body, block, scale, count), out_sha...  11.8 us
    ppermute x6, starting transfers between devices, swap(): return lax.ppermute(x, 'sec', [(i, i ^ m) for i in range(n_sec)])  10.1 us
    ppermute x1, waiting for transfers between devices, shards(): second = lax.ppermute(total, ('sec', 'col'), across)  5.18 us
    pallas_call x1, Pallas kernels, prepare(): pl.pallas_call(functools.partial(prepare_body, block), out_shape=(jax.Sha...  4.09 us
    pallas_call x1, Pallas kernels, group(): pl.pallas_call(group_body, out_shape=jax.ShapeDtypeStruct((feat + 8, coar...  1.95 us
    ppermute x1, starting transfers between devices, shards(): second = lax.ppermute(total, ('sec', 'col'), across)  1.81 us
    pallas_call x1, Pallas kernels, spread(): pl.pallas_call(spread_body, out_shape=jax.ShapeDtypeStruct((levels, fine)...  0.91 us
  transfers between devices with their start and end apart: 8, of which 2 were waited for; matrix products, arithmetic and copies ran while one was open for 0% of the time, Pallas kernels for 43%

profile of v5, /device:TPU:0, one launch (start us, length us, event | category | flops | bytes accessed | tf_op | source)
XLA Modules:
  0.0 36.6 jit_solution(4071122872189059043)
XLA Ops:
  0.7 2.0 %group.1.refs_0_ = f32[456,128]{1,0:T(8,128)S(1)} custom-call(f32[448,512]{1,0:T(8,128)} %bitcast.7, f32[1,512]{1,0:T(1,128)} %bitcast.8, s32[1,512]{1,0:T(1,128)} %grouping_in.1, s32[1]{0:T(128)S(6)} %copy.11.sunlit), custom_call_target="tpu_custom_call" | custom-call | flops 234881024 | bytes 917504 | tf_op jit(solution)/shard_map/group/pallas_call | solution.py:72
  2.6 3.0 %collective-permute-start = (f32[456,128]{1,0:T(8,128)S(1)}, f32[456,128]{1,0:T(8,128)S(1)}, u32[]{:S(2)}, u32[]{:S(2)}) collective-permute-start(f32[456,128]{1,0:T(8,128)S(1)} %group.1.refs_0_), channel_id=1, source_target_pairs={{0,8},{8,0},{16,24},{24,16},{1,9},{9,1},{17,25},{25,17},{2,10},{10... | collective-permute-start | bytes 700424 | tf_op jit(solution)/shard_map/ppermute | solution.py:349
  5.6 1.5 %collective-permute-start.2 = (f32[456,128]{1,0:T(8,128)S(1)}, f32[456,128]{1,0:T(8,128)S(1)}, u32[]{:S(2)}, u32[]{:S(2)}) collective-permute-start(f32[456,128]{1,0:T(8,128)S(1)} %group.1.refs_0_), channel_id=1, source_target_pairs={{0,16},{8,24},{16,0},{24,8},{1,17},{9,25},{17,1},{25,9},{2,18},{10... | collective-permute-start | bytes 700424 | tf_op jit(solution)/shard_map/ppermute | solution.py:349
  7.1 4.1 %prepare.1 = (bf16[64,64,1024]{2,1,0:T(8,128)(2,1)S(1)}, f32[64,128]{1,0:T(8,128)S(1)}, f32[64,128]{1,0:T(8,128)S(1)}, bf16[256,512]{1,0:T(8,128)(2,1)S(1)}, bf16[256,512]{1,0:T(8,128)(2,1)S(1)}) custom-call(f32[64,64,448]{2,1,0:T(8,128)} %absorb_in.1, f32[64,64]{1,0:T(8,128)} %bias_in.1, f32[1,64]{1,0:T(1,128)} %bitcast.9, f32[1,64]{1,0:T(1,128)} %bitcast.10, ...), custom_call_target="tpu_custom_call" | custom-call | flops 18350080 | bytes 16777216 | tf_op jit(solution)/shard_map/prepare/pallas_call | solution.py:262
  11.2 0.1 collective-permute-done.refs_0_
  11.3 1.8 %collective-permute-start.1 = (f32[456,128]{1,0:T(8,128)S(1)}, f32[456,128]{1,0:T(8,128)S(1)}, u32[]{:S(2)}, u32[]{:S(2)}) collective-permute-start(f32[456,128]{1,0:T(8,128)S(1)} %collective-permute-done.refs_0_), channel_id=1, source_target_pairs={{0,16},{8,24},{16,0},{24,8},{1,17},{9,25},{17,1},{25,9},{2,18},{10... | collective-permute-start | bytes 700424 | tf_op jit(solution)/shard_map/ppermute | solution.py:349
  13.1 0.0 collective-permute-done.2.refs_1_
  13.1 5.5 %flux.3 = (f32[64,128]{1,0:T(8,128)S(1)}, f32[64,128]{1,0:T(8,128)S(1)}) custom-call(bf16[64,64,1024]{2,1,0:T(8,128)(2,1)S(1)} %get-tuple-element.31.table, f32[64,128]{1,0:T(8,128)S(1)} %get-tuple-element.24.planck, f32[64,128]{1,0:T(8,128)S(1)} %get-tuple-element.25.share, f32[456,128]{1,0:T(8,128)S(1)} %collective-permute-done.refs_0_, ...), custom_call_target="tpu_custom_call" | custom-call | flops 3221225472 | bytes 8388608 | tf_op jit(solution)/shard_map/flux/pallas_call | solution.py:299
  18.6 1.3 %collective-permute-start.4 = (f32[64,128]{1,0:T(8,128)S(1)}, f32[64,128]{1,0:T(8,128)S(1)}, u32[]{:S(2)}, u32[]{:S(2)}) collective-permute-start(f32[64,128]{1,0:T(8,128)S(1)} %get-tuple-element.28), channel_id=1, source_target_pairs={{0,16},{8,24},{16,0},{24,8},{1,17},{9,25},{17,1},{25,9},{2,18},{10... | collective-permute-start | bytes 98312 | tf_op jit(solution)/shard_map/ppermute | solution.py:349
  19.8 0.0 collective-permute-done.1.refs_0_
  19.9 0.8 %collective-permute-start.3 = (f32[64,128]{1,0:T(8,128)S(1)}, f32[64,128]{1,0:T(8,128)S(1)}, u32[]{:S(2)}, u32[]{:S(2)}) collective-permute-start(f32[64,128]{1,0:T(8,128)S(1)} %get-tuple-element.27), channel_id=1, source_target_pairs={{0,8},{8,0},{16,24},{24,16},{1,9},{9,1},{17,25},{25,17},{2,10},{10... | collective-permute-start | bytes 98312 | tf_op jit(solution)/shard_map/ppermute | solution.py:349
  20.6 3.1 %flux.4 = f32[64,128]{1,0:T(8,128)S(1)} custom-call(bf16[64,64,1024]{2,1,0:T(8,128)(2,1)S(1)} %get-tuple-element.31.table, f32[64,128]{1,0:T(8,128)S(1)} %get-tuple-element.24.planck, f32[64,128]{1,0:T(8,128)S(1)} %get-tuple-element.25.share, f32[456,128]{1,0:T(8,128)S(1)} %collective-permute-done.1.refs_0_), custom_call_target="tpu_custom_call" | custom-call | flops 1610612736 | bytes 8388608 | tf_op jit(solution)/shard_map/flux/pallas_call | solution.py:299
  23.8 0.0 collective-permute-done.4
  23.8 0.0 collective-permute-done.3
  23.8 1.7 %collective-permute-start.5 = (f32[64,128]{1,0:T(8,128)S(1)}, f32[64,128]{1,0:T(8,128)S(1)}, u32[]{:S(2)}, u32[]{:S(2)}) collective-permute-start(f32[64,128]{1,0:T(8,128)S(1)} %flux.4), channel_id=1, source_target_pairs={{0,24},{8,16},{16,8},{24,0},{1,25},{9,17},{17,9},{25,1},{2,26},{10... | collective-permute-start | bytes 98312 | tf_op jit(solution)/shard_map/ppermute | solution.py:349
  25.5 3.1 %flux.5 = f32[64,128]{1,0:T(8,128)S(1)} custom-call(bf16[64,64,1024]{2,1,0:T(8,128)(2,1)S(1)} %get-tuple-element.31.table, f32[64,128]{1,0:T(8,128)S(1)} %get-tuple-element.24.planck, f32[64,128]{1,0:T(8,128)S(1)} %get-tuple-element.25.share, f32[456,128]{1,0:T(8,128)S(1)} %group.1.refs_0_), custom_call_target="tpu_custom_call" | custom-call | flops 1610612736 | bytes 8388608 | tf_op jit(solution)/shard_map/flux/pallas_call | solution.py:299
  28.7 0.0 collective-permute-done.5
  28.7 1.8 %collective-permute-start.6 = (f32[64,128]{1,0:T(8,128)S(1)}, f32[64,128]{1,0:T(8,128)S(1)}, u32[]{:S(2)}, u32[]{:S(2)}) collective-permute-start(f32[64,128]{1,0:T(8,128)S(1)} %add_add_fusion.own), channel_id=1, source_target_pairs={{0,31},{1,2},{2,1},{3,4},{4,3},{5,6},{6,5},{7,8},{8,7},{9,10},{10,... | collective-permute-start | bytes 98312 | tf_op jit(solution)/shard_map/ppermute | solution.py:368
  30.5 0.0 collective-permute-start.7
  30.5 5.2 %collective-permute-done.6.first = f32[64,128]{1,0:T(8,128)S(1)} collective-permute-done((f32[64,128]{1,0:T(8,128)S(1)}, f32[64,128]{1,0:T(8,128)S(1)}, u32[]{:S(2)}, u32[]{:S(2)}) %collective-permute-start.6) | collective-permute-done | bytes 32800 | tf_op jit(solution)/shard_map/ppermute | solution.py:368
  35.7 0.0 collective-permute-done.7.second
  35.7 0.9 %spread.1 = f32[64,512]{1,0:T(8,128)} custom-call(f32[64,128]{1,0:T(8,128)S(1)} %add_add_fusion.own, f32[64,128]{1,0:T(8,128)S(1)} %collective-permute-done.6.first, f32[64,128]{1,0:T(8,128)S(1)} %collective-permute-done.7.second, s32[1]{0:T(128)} %bitcast.5.parity, bf16[256,512]{1,0:T(8,128)(2,1)S(1)} %get-tuple-element.35.high, ...), custom_call_target="tpu_custom_call" | custom-call | tf_op jit(solution)/shard_map/spread/pallas_call | solution.py:328
  (2 shorter events, 0.0 us)
Async XLA Ops:
  2.6 8.7 %collective-permute-start = (f32[456,128]{1,0:T(8,128)S(1)}, f32[456,128]{1,0:T(8,128)S(1)}, u32[]{:S(2)}, u32[]{:S(2)}) collective-permute-start(f32[456,128]{1,0:T(8,128)S(1)} %group.1.refs_0_), channel_id=1, source_target_pairs={{0,8},{8,0},{16,24},{24,16},{1,9},{9,1},{17,25},{25,17},{2,10},{10... | collective-permute-start | bytes 700424 | tf_op jit(solution)/shard_map/ppermute | solution.py:349
  5.6 7.5 %collective-permute-start.2 = (f32[456,128]{1,0:T(8,128)S(1)}, f32[456,128]{1,0:T(8,128)S(1)}, u32[]{:S(2)}, u32[]{:S(2)}) collective-permute-start(f32[456,128]{1,0:T(8,128)S(1)} %group.1.refs_0_), channel_id=1, source_target_pairs={{0,16},{8,24},{16,0},{24,8},{1,17},{9,25},{17,1},{25,9},{2,18},{10... | collective-permute-start | bytes 700424 | tf_op jit(solution)/shard_map/ppermute | solution.py:349
  11.3 8.5 %collective-permute-start.1 = (f32[456,128]{1,0:T(8,128)S(1)}, f32[456,128]{1,0:T(8,128)S(1)}, u32[]{:S(2)}, u32[]{:S(2)}) collective-permute-start(f32[456,128]{1,0:T(8,128)S(1)} %collective-permute-done.refs_0_), channel_id=1, source_target_pairs={{0,16},{8,24},{16,0},{24,8},{1,17},{9,25},{17,1},{25,9},{2,18},{10... | collective-permute-start | bytes 700424 | tf_op jit(solution)/shard_map/ppermute | solution.py:349
  18.6 5.2 %collective-permute-start.4 = (f32[64,128]{1,0:T(8,128)S(1)}, f32[64,128]{1,0:T(8,128)S(1)}, u32[]{:S(2)}, u32[]{:S(2)}) collective-permute-start(f32[64,128]{1,0:T(8,128)S(1)} %get-tuple-element.28), channel_id=1, source_target_pairs={{0,16},{8,24},{16,0},{24,8},{1,17},{9,25},{17,1},{25,9},{2,18},{10... | collective-permute-start | bytes 98312 | tf_op jit(solution)/shard_map/ppermute | solution.py:349
  19.9 3.9 %collective-permute-start.3 = (f32[64,128]{1,0:T(8,128)S(1)}, f32[64,128]{1,0:T(8,128)S(1)}, u32[]{:S(2)}, u32[]{:S(2)}) collective-permute-start(f32[64,128]{1,0:T(8,128)S(1)} %get-tuple-element.27), channel_id=1, source_target_pairs={{0,8},{8,0},{16,24},{24,16},{1,9},{9,1},{17,25},{25,17},{2,10},{10... | collective-permute-start | bytes 98312 | tf_op jit(solution)/shard_map/ppermute | solution.py:349
  23.8 4.9 %collective-permute-start.5 = (f32[64,128]{1,0:T(8,128)S(1)}, f32[64,128]{1,0:T(8,128)S(1)}, u32[]{:S(2)}, u32[]{:S(2)}) collective-permute-start(f32[64,128]{1,0:T(8,128)S(1)} %flux.4), channel_id=1, source_target_pairs={{0,24},{8,16},{16,8},{24,0},{1,25},{9,17},{17,9},{25,1},{2,26},{10... | collective-permute-start | bytes 98312 | tf_op jit(solution)/shard_map/ppermute | solution.py:349
  28.7 7.0 %collective-permute-start.6 = (f32[64,128]{1,0:T(8,128)S(1)}, f32[64,128]{1,0:T(8,128)S(1)}, u32[]{:S(2)}, u32[]{:S(2)}) collective-permute-start(f32[64,128]{1,0:T(8,128)S(1)} %add_add_fusion.own), channel_id=1, source_target_pairs={{0,31},{1,2},{2,1},{3,4},{4,3},{5,6},{6,5},{7,8},{8,7},{9,10},{10,... | collective-permute-start | bytes 98312 | tf_op jit(solution)/shard_map/ppermute | solution.py:368
  30.5 5.2 %collective-permute-start.7 = (f32[64,128]{1,0:T(8,128)S(1)}, f32[64,128]{1,0:T(8,128)S(1)}, u32[]{:S(2)}, u32[]{:S(2)}) collective-permute-start(f32[64,128]{1,0:T(8,128)S(1)} %add_add_fusion.own), channel_id=1, source_target_pairs={{0,1},{1,0},{2,3},{3,2},{4,5},{5,4},{6,7},{7,6},{8,9},{9,8},{10,11... | collective-permute-start | bytes 98312 | tf_op jit(solution)/shard_map/ppermute | solution.py:369

commit v6 on v5

--- a/solution.py
+++ b/solution.py
@@ -56,7 +56,7 @@
     copies[1].wait()
     copies[2].wait()
     total = jnp.zeros((feat, coarse), f32)
-    for term in split(state[...], 3)[::-1]:
+    for term in split(state[...], 2)[::-1]:
         total = total + dot(term, weights)
     out[0:feat, :] = total
     light = jnp.zeros((8, coarse), f32)
@@ -93,9 +93,11 @@
     return jnp.exp2(-0.1 * jnp.maximum(low, y))
 
 
-def sweeps(block, scale, table, chunks, planck, share, outs, scratch):
+def sweeps(block, scale, span, table, chunks, planck, share, outs, scratch):
     right, zs, ts, downs, warms = scratch
-    levels, g, double = table.shape
+    levels, _, double = table.shape
+    low, high = span
+    g = high - low
     depth = double // 2
     feat = depth - levels
     half = chunks[0].shape[1]
@@ -118,7 +120,7 @@
         return jnp.sum(x.reshape(g // 8, 8, n), axis=0)
 
     def absorb(b):
-        a = table[b * block : (b + 1) * block].reshape(block * g, double)
+        a = table[b * block : (b + 1) * block, low:high].reshape(block * g, double)
         c = right[0:depth, :]
         z = dot(a[:, 0:depth], c) + dot(a[:, depth:double], c)
         if count == 1:
@@ -127,9 +129,9 @@
             zs[b % 2] = z + dot(a[:, 0:depth], right[depth:double, :])
 
     absorb(0)
-    weight = jnp.concatenate([planck[...]] * count, axis=1)
+    weight = jnp.concatenate([planck[low:high, :]] * count, axis=1)
     lights = jnp.concatenate([rows[feat : feat + 1, :] for rows in chunks], axis=1)
-    d = jnp.concatenate([share[...]] * count, axis=1) * lights - weight * warms[0:1, :]
+    d = jnp.concatenate([share[low:high, :]] * count, axis=1) * lights - weight * warms[0:1, :]
     downs[0] = fold(d)
     for b in range(blocks):
         if b + 1 < blocks:
@@ -287,17 +289,19 @@
     )(*(stay(x) for x in (absorb, bias, planck, share, stencil, weight)))
 
 
-def flux_body(block, scale, count, table, planck, share, *refs):
+def flux_body(block, scale, span, count, table, planck, share, *refs):
     chunks, outs, scratch = refs[:count], refs[count : 2 * count], refs[2 * count :]
-    sweeps(block, scale, table, chunks, planck, share, outs, scratch)
-
-
-def flux(table, planck, share, chunks, scale):
+    sweeps(block, scale, span, table, chunks, planck, share, outs, scratch)
+
+
+def flux(table, planck, share, chunks, scale, span=None):
     levels, g, double = table.shape
+    span = span or (0, g)
+    g = span[1] - span[0]
     count, half = len(chunks), chunks[0].shape[1]
-    block = 4
+    block = 4 if count == 2 or 2 * g > table.shape[1] else 8
     return pl.pallas_call(
-        functools.partial(flux_body, block, scale, count),
+        functools.partial(flux_body, block, scale, span, count),
         out_shape=(jax.ShapeDtypeStruct((levels, half), f32),) * count,
         in_specs=[VMEM] * (3 + count),
         out_specs=(VMEM,) * count,
@@ -319,7 +323,9 @@
     halo = jnp.where(late == parity[0], first[...], second[...])
     wide = jnp.concatenate([own[...], halo], axis=1)
     a, c = split(wide, 2)
-    out[...] = dot(a, high[...]) + (dot(a, low[...]) + dot(c, high[...]))
+    both = dot(jnp.concatenate([a, c], axis=0), high[...])
+    m = a.shape[0]
+    out[...] = both[0:m] + (dot(a, low[...]) + both[m : 2 * m])
 
 
 def spread(own, first, second, parity, high, low):
@@ -356,13 +362,11 @@
     later, table = lax.optimization_barrier((first, table))
     third = swap(later, 2)
     heats = flux(table, weight, share, [first, second], scale)
-    third, table, *tied = lax.optimization_barrier((third, table, heats[0]))
+    third, table, *heats = lax.optimization_barrier((third, table, *heats))
     (heat,) = flux(table, weight, share, [third], scale)
-    others = swap(tied[0], 1) + swap(heats[1], 2)
-    others, heat, table, rows = lax.optimization_barrier((others, heat, table, rows))
-    last = swap(heat, 3)
+    heat, table, rows, *heats = lax.optimization_barrier((heat, table, rows, *heats))
     (total,) = flux(table, weight, share, [rows], scale)
-    total = total + others + last
+    total = swap(heat, 3) + swap(heats[0], 1) + swap(heats[1], 2) + total
     pairs = [(i, i ^ 1) for i in range(devices)]
     across = [(i, (i + 1) % devices if i % 2 else (i - 1) % devices) for i in range(devices)]
     second = lax.ppermute(total, ("sec", "col"), across)

time: 36.8 us -> 36.7 us (level)
  transfers between devices with their start and end apart: 8 -> 8, of which waited for: 2 -> 2; matrix products, arithmetic and copies ran while one was open for 0% -> 0% of each run, Pallas kernels for 43% -> 35%
where the time goes in v6:
time: 36.7 us; the launch traced here: 36.5 us
  Pallas kernels  18.5 us (50%)
  starting transfers between devices  11.8 us (32%)
  waiting for transfers between devices  5.44 us (15%)
  between operations  0.73 us (2%)
    pallas_call x3, Pallas kernels, flux(): pl.pallas_call(functools.partial(flux_body, block, scale, span, count), o...  11.8 us
    ppermute x6, starting transfers between devices, swap(): return lax.ppermute(x, 'sec', [(i, i ^ m) for i in range(n_sec)])  9.84 us
    ppermute x1, waiting for transfers between devices, shards(): second = lax.ppermute(total, ('sec', 'col'), across)  5.34 us
    pallas_call x1, Pallas kernels, prepare(): pl.pallas_call(functools.partial(prepare_body, block), out_shape=(jax.Sha...  4.09 us
    ppermute x1, starting transfers between devices, shards(): second = lax.ppermute(total, ('sec', 'col'), across)  1.98 us
    pallas_call x1, Pallas kernels, group(): pl.pallas_call(group_body, out_shape=jax.ShapeDtypeStruct((feat + 8, coar...  1.8 us
    pallas_call x1, Pallas kernels, spread(): pl.pallas_call(spread_body, out_shape=jax.ShapeDtypeStruct((levels, fine)...  0.87 us
  transfers between devices with their start and end apart: 8, of which 2 were waited for; matrix products, arithmetic and copies ran while one was open for 0% of the time, Pallas kernels for 35%

profile of v6, /device:TPU:0, one launch (start us, length us, event | category | flops | bytes accessed | tf_op | source)
XLA Modules:
  0.0 36.5 jit_solution(6010864040480739529)
XLA Ops:
  0.7 1.8 %group.1.refs_0_ = f32[456,128]{1,0:T(8,128)S(1)} custom-call(f32[448,512]{1,0:T(8,128)} %bitcast.7, f32[1,512]{1,0:T(1,128)} %bitcast.8, s32[1,512]{1,0:T(1,128)} %grouping_in.1, s32[1]{0:T(128)S(6)} %copy.11.sunlit), custom_call_target="tpu_custom_call" | custom-call | flops 234881024 | bytes 917504 | tf_op jit(solution)/shard_map/group/pallas_call | solution.py:72
  2.5 3.0 %collective-permute-start = (f32[456,128]{1,0:T(8,128)S(1)}, f32[456,128]{1,0:T(8,128)S(1)}, u32[]{:S(2)}, u32[]{:S(2)}) collective-permute-start(f32[456,128]{1,0:T(8,128)S(1)} %group.1.refs_0_), channel_id=1, source_target_pairs={{0,8},{8,0},{16,24},{24,16},{1,9},{9,1},{17,25},{25,17},{2,10},{10... | collective-permute-start | bytes 700424 | tf_op jit(solution)/shard_map/ppermute | solution.py:355
  5.5 1.5 %collective-permute-start.2 = (f32[456,128]{1,0:T(8,128)S(1)}, f32[456,128]{1,0:T(8,128)S(1)}, u32[]{:S(2)}, u32[]{:S(2)}) collective-permute-start(f32[456,128]{1,0:T(8,128)S(1)} %group.1.refs_0_), channel_id=1, source_target_pairs={{0,16},{8,24},{16,0},{24,8},{1,17},{9,25},{17,1},{25,9},{2,18},{10... | collective-permute-start | bytes 700424 | tf_op jit(solution)/shard_map/ppermute | solution.py:355
  7.0 4.1 %prepare.1 = (bf16[64,64,1024]{2,1,0:T(8,128)(2,1)S(1)}, f32[64,128]{1,0:T(8,128)S(1)}, f32[64,128]{1,0:T(8,128)S(1)}, bf16[256,512]{1,0:T(8,128)(2,1)S(1)}, bf16[256,512]{1,0:T(8,128)(2,1)S(1)}) custom-call(f32[64,64,448]{2,1,0:T(8,128)} %absorb_in.1, f32[64,64]{1,0:T(8,128)} %bias_in.1, f32[1,64]{1,0:T(1,128)} %bitcast.9, f32[1,64]{1,0:T(1,128)} %bitcast.10, ...), custom_call_target="tpu_custom_call" | custom-call | flops 18350080 | bytes 16777216 | tf_op jit(solution)/shard_map/prepare/pallas_call | solution.py:264
  11.1 0.1 collective-permute-done.refs_0_
  11.2 1.8 %collective-permute-start.1 = (f32[456,128]{1,0:T(8,128)S(1)}, f32[456,128]{1,0:T(8,128)S(1)}, u32[]{:S(2)}, u32[]{:S(2)}) collective-permute-start(f32[456,128]{1,0:T(8,128)S(1)} %collective-permute-done.refs_0_), channel_id=1, source_target_pairs={{0,16},{8,24},{16,0},{24,8},{1,17},{9,25},{17,1},{25,9},{2,18},{10... | collective-permute-start | bytes 700424 | tf_op jit(solution)/shard_map/ppermute | solution.py:355
  12.9 0.0 collective-permute-done.2.refs_1_
  12.9 5.5 %flux.3 = (f32[64,128]{1,0:T(8,128)S(1)}, f32[64,128]{1,0:T(8,128)S(1)}) custom-call(bf16[64,64,1024]{2,1,0:T(8,128)(2,1)S(1)} %get-tuple-element.37.table, f32[64,128]{1,0:T(8,128)S(1)} %get-tuple-element.26.planck, f32[64,128]{1,0:T(8,128)S(1)} %get-tuple-element.27.share, f32[456,128]{1,0:T(8,128)S(1)} %collective-permute-done.refs_0_, ...), custom_call_target="tpu_custom_call" | custom-call | flops 3221225472 | bytes 8388608 | tf_op jit(solution)/shard_map/flux/pallas_call | solution.py:303
  18.4 0.0 collective-permute-done.1.refs_0_
  18.4 3.1 %flux.4 = f32[64,128]{1,0:T(8,128)S(1)} custom-call(bf16[64,64,1024]{2,1,0:T(8,128)(2,1)S(1)} %get-tuple-element.37.table, f32[64,128]{1,0:T(8,128)S(1)} %get-tuple-element.26.planck, f32[64,128]{1,0:T(8,128)S(1)} %get-tuple-element.27.share, f32[456,128]{1,0:T(8,128)S(1)} %collective-permute-done.1.refs_0_), custom_call_target="tpu_custom_call" | custom-call | flops 1610612736 | bytes 8388608 | tf_op jit(solution)/shard_map/flux/pallas_call | solution.py:303
  21.6 2.0 %collective-permute-start.3 = (f32[64,128]{1,0:T(8,128)S(1)}, f32[64,128]{1,0:T(8,128)S(1)}, u32[]{:S(2)}, u32[]{:S(2)}) collective-permute-start(f32[64,128]{1,0:T(8,128)S(1)} %flux.4), channel_id=1, source_target_pairs={{0,24},{8,16},{16,8},{24,0},{1,25},{9,17},{17,9},{25,1},{2,26},{10... | collective-permute-start | bytes 98312 | tf_op jit(solution)/shard_map/ppermute | solution.py:355
  23.6 0.7 %collective-permute-start.4 = (f32[64,128]{1,0:T(8,128)S(1)}, f32[64,128]{1,0:T(8,128)S(1)}, u32[]{:S(2)}, u32[]{:S(2)}) collective-permute-start(f32[64,128]{1,0:T(8,128)S(1)} %get-tuple-element.35), channel_id=1, source_target_pairs={{0,8},{8,0},{16,24},{24,16},{1,9},{9,1},{17,25},{25,17},{2,10},{10... | collective-permute-start | bytes 98312 | tf_op jit(solution)/shard_map/ppermute | solution.py:355
  24.3 0.8 %collective-permute-start.5 = (f32[64,128]{1,0:T(8,128)S(1)}, f32[64,128]{1,0:T(8,128)S(1)}, u32[]{:S(2)}, u32[]{:S(2)}) collective-permute-start(f32[64,128]{1,0:T(8,128)S(1)} %get-tuple-element.36), channel_id=1, source_target_pairs={{0,16},{8,24},{16,0},{24,8},{1,17},{9,25},{17,1},{25,9},{2,18},{10... | collective-permute-start | bytes 98312 | tf_op jit(solution)/shard_map/ppermute | solution.py:355
  25.1 3.1 %flux.5 = f32[64,128]{1,0:T(8,128)S(1)} custom-call(bf16[64,64,1024]{2,1,0:T(8,128)(2,1)S(1)} %get-tuple-element.37.table, f32[64,128]{1,0:T(8,128)S(1)} %get-tuple-element.26.planck, f32[64,128]{1,0:T(8,128)S(1)} %get-tuple-element.27.share, f32[456,128]{1,0:T(8,128)S(1)} %group.1.refs_0_), custom_call_target="tpu_custom_call" | custom-call | flops 1610612736 | bytes 8388608 | tf_op jit(solution)/shard_map/flux/pallas_call | solution.py:303
  28.3 0.0 collective-permute-done.3
  28.3 0.0 collective-permute-done.4
  28.3 0.0 collective-permute-done.5
  28.3 2.0 %collective-permute-start.6 = (f32[64,128]{1,0:T(8,128)S(1)}, f32[64,128]{1,0:T(8,128)S(1)}, u32[]{:S(2)}, u32[]{:S(2)}) collective-permute-start(f32[64,128]{1,0:T(8,128)S(1)} %add_add_fusion.own), channel_id=1, source_target_pairs={{0,31},{1,2},{2,1},{3,4},{4,3},{5,6},{6,5},{7,8},{8,7},{9,10},{10,... | collective-permute-start | bytes 98312 | tf_op jit(solution)/shard_map/ppermute | solution.py:372
  30.3 0.0 collective-permute-start.7
  30.3 5.3 %collective-permute-done.6.first = f32[64,128]{1,0:T(8,128)S(1)} collective-permute-done((f32[64,128]{1,0:T(8,128)S(1)}, f32[64,128]{1,0:T(8,128)S(1)}, u32[]{:S(2)}, u32[]{:S(2)}) %collective-permute-start.6) | collective-permute-done | bytes 32800 | tf_op jit(solution)/shard_map/ppermute | solution.py:372
  35.7 0.0 collective-permute-done.7.second
  35.7 0.9 %spread.1 = f32[64,512]{1,0:T(8,128)} custom-call(f32[64,128]{1,0:T(8,128)S(1)} %add_add_fusion.own, f32[64,128]{1,0:T(8,128)S(1)} %collective-permute-done.6.first, f32[64,128]{1,0:T(8,128)S(1)} %collective-permute-done.7.second, s32[1]{0:T(128)} %bitcast.5.parity, bf16[256,512]{1,0:T(8,128)(2,1)S(1)} %get-tuple-element.39.high, ...), custom_call_target="tpu_custom_call" | custom-call | tf_op jit(solution)/shard_map/spread/pallas_call | solution.py:334
  (1 shorter events, 0.0 us)
Async XLA Ops:
  2.5 8.7 %collective-permute-start = (f32[456,128]{1,0:T(8,128)S(1)}, f32[456,128]{1,0:T(8,128)S(1)}, u32[]{:S(2)}, u32[]{:S(2)}) collective-permute-start(f32[456,128]{1,0:T(8,128)S(1)} %group.1.refs_0_), channel_id=1, source_target_pairs={{0,8},{8,0},{16,24},{24,16},{1,9},{9,1},{17,25},{25,17},{2,10},{10... | collective-permute-start | bytes 700424 | tf_op jit(solution)/shard_map/ppermute | solution.py:355
  5.5 7.5 %collective-permute-start.2 = (f32[456,128]{1,0:T(8,128)S(1)}, f32[456,128]{1,0:T(8,128)S(1)}, u32[]{:S(2)}, u32[]{:S(2)}) collective-permute-start(f32[456,128]{1,0:T(8,128)S(1)} %group.1.refs_0_), channel_id=1, source_target_pairs={{0,16},{8,24},{16,0},{24,8},{1,17},{9,25},{17,1},{25,9},{2,18},{10... | collective-permute-start | bytes 700424 | tf_op jit(solution)/shard_map/ppermute | solution.py:355
  11.2 7.3 %collective-permute-start.1 = (f32[456,128]{1,0:T(8,128)S(1)}, f32[456,128]{1,0:T(8,128)S(1)}, u32[]{:S(2)}, u32[]{:S(2)}) collective-permute-start(f32[456,128]{1,0:T(8,128)S(1)} %collective-permute-done.refs_0_), channel_id=1, source_target_pairs={{0,16},{8,24},{16,0},{24,8},{1,17},{9,25},{17,1},{25,9},{2,18},{10... | collective-permute-start | bytes 700424 | tf_op jit(solution)/shard_map/ppermute | solution.py:355
  21.6 6.7 %collective-permute-start.3 = (f32[64,128]{1,0:T(8,128)S(1)}, f32[64,128]{1,0:T(8,128)S(1)}, u32[]{:S(2)}, u32[]{:S(2)}) collective-permute-start(f32[64,128]{1,0:T(8,128)S(1)} %flux.4), channel_id=1, source_target_pairs={{0,24},{8,16},{16,8},{24,0},{1,25},{9,17},{17,9},{25,1},{2,26},{10... | collective-permute-start | bytes 98312 | tf_op jit(solution)/shard_map/ppermute | solution.py:355
  23.6 4.7 %collective-permute-start.4 = (f32[64,128]{1,0:T(8,128)S(1)}, f32[64,128]{1,0:T(8,128)S(1)}, u32[]{:S(2)}, u32[]{:S(2)}) collective-permute-start(f32[64,128]{1,0:T(8,128)S(1)} %get-tuple-element.35), channel_id=1, source_target_pairs={{0,8},{8,0},{16,24},{24,16},{1,9},{9,1},{17,25},{25,17},{2,10},{10... | collective-permute-start | bytes 98312 | tf_op jit(solution)/shard_map/ppermute | solution.py:355
  24.3 4.0 %collective-permute-start.5 = (f32[64,128]{1,0:T(8,128)S(1)}, f32[64,128]{1,0:T(8,128)S(1)}, u32[]{:S(2)}, u32[]{:S(2)}) collective-permute-start(f32[64,128]{1,0:T(8,128)S(1)} %get-tuple-element.36), channel_id=1, source_target_pairs={{0,16},{8,24},{16,0},{24,8},{1,17},{9,25},{17,1},{25,9},{2,18},{10... | collective-permute-start | bytes 98312 | tf_op jit(solution)/shard_map/ppermute | solution.py:355
  28.3 7.3 %collective-permute-start.6 = (f32[64,128]{1,0:T(8,128)S(1)}, f32[64,128]{1,0:T(8,128)S(1)}, u32[]{:S(2)}, u32[]{:S(2)}) collective-permute-start(f32[64,128]{1,0:T(8,128)S(1)} %add_add_fusion.own), channel_id=1, source_target_pairs={{0,31},{1,2},{2,1},{3,4},{4,3},{5,6},{6,5},{7,8},{8,7},{9,10},{10,... | collective-permute-start | bytes 98312 | tf_op jit(solution)/shard_map/ppermute | solution.py:372
  30.3 5.3 %collective-permute-start.7 = (f32[64,128]{1,0:T(8,128)S(1)}, f32[64,128]{1,0:T(8,128)S(1)}, u32[]{:S(2)}, u32[]{:S(2)}) collective-permute-start(f32[64,128]{1,0:T(8,128)S(1)} %add_add_fusion.own), channel_id=1, source_target_pairs={{0,1},{1,0},{2,3},{3,2},{4,5},{5,4},{6,7},{7,6},{8,9},{9,8},{10,11... | collective-permute-start | bytes 98312 | tf_op jit(solution)/shard_map/ppermute | solution.py:373

commit v7 on v6

--- a/solution.py
+++ b/solution.py
@@ -153,7 +153,7 @@
         downs[l + 1] = (downs[l] - downs[l + 1]) + (below - above)
         return v, above
 
-    lax.fori_loop(0, levels, climb, (v, fold(v)), unroll=8)
+    lax.fori_loop(0, levels, climb, (v, fold(v)), unroll=16)
     heat = downs[1 : levels + 1, 0, :]
     for s in range(1, 8):
         heat = heat + downs[1 : levels + 1, s, :]
@@ -316,29 +316,59 @@
     )(table, planck, share, *chunks)
 
 
-def spread_body(own, first, second, parity, high, low, out):
+def products(x, high, low):
+    a, c = split(x, 2)
+    m = x.shape[0]
+    both = dot(jnp.concatenate([a, c], axis=0), high)
+    return both[0:m] + (dot(a, low) + both[m : 2 * m])
+
+
+def inner_body(own, high, low, out):
     n = own.shape[1]
-    lane = lax.broadcasted_iota(jnp.int32, own.shape, 1)
+    out[...] = products(own[...], high[0:n, :], low[0:n, :])
+
+
+def edge_body(inner, first, second, parity, high, low, out):
+    n = first.shape[1]
+    fine = out.shape[1]
+    lane = lax.broadcasted_iota(jnp.int32, first.shape, 1)
     late = jnp.where(lane >= n // 2, 1, 0)
     halo = jnp.where(late == parity[0], first[...], second[...])
-    wide = jnp.concatenate([own[...], halo], axis=1)
-    a, c = split(wide, 2)
-    both = dot(jnp.concatenate([a, c], axis=0), high[...])
-    m = a.shape[0]
-    out[...] = both[0:m] + (dot(a, low[...]) + both[m : 2 * m])
-
-
-def spread(own, first, second, parity, high, low):
+    parts = [
+        jnp.concatenate([t[n : 2 * n, 0:128], t[n : 2 * n, fine - 128 : fine]], axis=1)
+        for t in (high, low)
+    ]
+    added = products(halo, *parts)
+    out[:, 0:128] = inner[:, 0:128] + added[:, 0:128]
+    out[:, 128 : fine - 128] = inner[:, 128 : fine - 128]
+    out[:, fine - 128 : fine] = inner[:, fine - 128 : fine] + added[:, 128:256]
+
+
+def spread_inner(own, high, low):
     levels = own.shape[0]
     fine = high.shape[1]
     return pl.pallas_call(
-        spread_body,
+        inner_body,
         out_shape=jax.ShapeDtypeStruct((levels, fine), f32),
+        in_specs=[VMEM] * 3,
+        out_specs=VMEM,
+        compiler_params=pltpu.CompilerParams(vmem_limit_bytes=16 * MIB),
+        cost_estimate=pl.CostEstimate(
+            flops=6 * levels * own.shape[1] * fine, bytes_accessed=4 * levels * fine, transcendentals=0
+        ),
+        name="spread_inner",
+    )(own, high, low)
+
+
+def spread(inner, first, second, parity, high, low):
+    return pl.pallas_call(
+        edge_body,
+        out_shape=jax.ShapeDtypeStruct(inner.shape, f32),
         in_specs=[VMEM] * 3 + [pl.BlockSpec(memory_space=pltpu.SMEM)] + [VMEM] * 2,
         out_specs=VMEM,
         compiler_params=pltpu.CompilerParams(vmem_limit_bytes=16 * MIB),
         name="spread",
-    )(own, first, second, parity, high, low)
+    )(inner, first, second, parity, high, low)
 
 
 def shards(
@@ -366,13 +396,13 @@
     (heat,) = flux(table, weight, share, [third], scale)
     heat, table, rows, *heats = lax.optimization_barrier((heat, table, rows, *heats))
     (total,) = flux(table, weight, share, [rows], scale)
-    total = swap(heat, 3) + swap(heats[0], 1) + swap(heats[1], 2) + total
+    total = swap(heats[0], 1) + swap(heat, 3) + swap(heats[1], 2) + total
     pairs = [(i, i ^ 1) for i in range(devices)]
     across = [(i, (i + 1) % devices if i % 2 else (i - 1) % devices) for i in range(devices)]
     second = lax.ppermute(total, ("sec", "col"), across)
     first = lax.ppermute(total, ("sec", "col"), pairs)
     parity = jnp.bitwise_and(lax.axis_index(("sec", "col")), 1).astype(jnp.int32).reshape(1)
-    return spread(total, second, first, 1 - parity, near, far)
+    return spread(spread_inner(total, near, far), second, first, 1 - parity, near, far)
 
 
 def solution(mesh):

time: 36.7 us -> 36.7 us (level)
    pallas_call x1 -> x2, Pallas kernels: 0.87 us -> 1.02 us  [the longest x1 0.83 us: spread(): pl.pallas_call(edge_body, out_shape=jax.ShapeDtypeStruct(inner.shape, f32...]
where the time goes in v7:
time: 36.7 us; the launch traced here: 36.5 us
  Pallas kernels  18.7 us (51%)
  starting transfers between devices  11.8 us (32%)
  waiting for transfers between devices  5.26 us (14%)
  between operations  0.74 us (2%)
    pallas_call x3, Pallas kernels, flux(): pl.pallas_call(functools.partial(flux_body, block, scale, span, count), o...  11.8 us
    ppermute x6, starting transfers between devices, swap(): return lax.ppermute(x, 'sec', [(i, i ^ m) for i in range(n_sec)])  9.84 us
    ppermute x1, waiting for transfers between devices, shards(): second = lax.ppermute(total, ('sec', 'col'), across)  5.17 us
    pallas_call x1, Pallas kernels, prepare(): pl.pallas_call(functools.partial(prepare_body, block), out_shape=(jax.Sha...  4.09 us
    ppermute x1, starting transfers between devices, shards(): second = lax.ppermute(total, ('sec', 'col'), across)  1.98 us
    pallas_call x1, Pallas kernels, group(): pl.pallas_call(group_body, out_shape=jax.ShapeDtypeStruct((feat + 8, coar...  1.8 us
    pallas_call x1, Pallas kernels, spread(): pl.pallas_call(edge_body, out_shape=jax.ShapeDtypeStruct(inner.shape, f32...  0.83 us
  transfers between devices with their start and end apart: 8, of which 2 were waited for; matrix products, arithmetic and copies ran while one was open for 0% of the time, Pallas kernels for 35%

profile of v7, /device:TPU:0, one launch (start us, length us, event | category | flops | bytes accessed | tf_op | source)
XLA Modules:
  0.0 36.5 jit_solution(14824847571687306663)
XLA Ops:
  0.7 1.8 %group.1.refs_0_ = f32[456,128]{1,0:T(8,128)S(1)} custom-call(f32[448,512]{1,0:T(8,128)} %bitcast.7, f32[1,512]{1,0:T(1,128)} %bitcast.8, s32[1,512]{1,0:T(1,128)} %grouping_in.1, s32[1]{0:T(128)S(6)} %copy.11.sunlit), custom_call_target="tpu_custom_call" | custom-call | flops 234881024 | bytes 917504 | tf_op jit(solution)/shard_map/group/pallas_call | solution.py:72
  2.5 3.0 %collective-permute-start = (f32[456,128]{1,0:T(8,128)S(1)}, f32[456,128]{1,0:T(8,128)S(1)}, u32[]{:S(2)}, u32[]{:S(2)}) collective-permute-start(f32[456,128]{1,0:T(8,128)S(1)} %group.1.refs_0_), channel_id=1, source_target_pairs={{0,8},{8,0},{16,24},{24,16},{1,9},{9,1},{17,25},{25,17},{2,10},{10... | collective-permute-start | bytes 700424 | tf_op jit(solution)/shard_map/ppermute | solution.py:385
  5.5 1.5 %collective-permute-start.2 = (f32[456,128]{1,0:T(8,128)S(1)}, f32[456,128]{1,0:T(8,128)S(1)}, u32[]{:S(2)}, u32[]{:S(2)}) collective-permute-start(f32[456,128]{1,0:T(8,128)S(1)} %group.1.refs_0_), channel_id=1, source_target_pairs={{0,16},{8,24},{16,0},{24,8},{1,17},{9,25},{17,1},{25,9},{2,18},{10... | collective-permute-start | bytes 700424 | tf_op jit(solution)/shard_map/ppermute | solution.py:385
  7.0 4.1 %prepare.1 = (bf16[64,64,1024]{2,1,0:T(8,128)(2,1)S(1)}, f32[64,128]{1,0:T(8,128)S(1)}, f32[64,128]{1,0:T(8,128)S(1)}, bf16[256,512]{1,0:T(8,128)(2,1)S(1)}, bf16[256,512]{1,0:T(8,128)(2,1)S(1)}) custom-call(f32[64,64,448]{2,1,0:T(8,128)} %absorb_in.1, f32[64,64]{1,0:T(8,128)} %bias_in.1, f32[1,64]{1,0:T(1,128)} %bitcast.9, f32[1,64]{1,0:T(1,128)} %bitcast.10, ...), custom_call_target="tpu_custom_call" | custom-call | flops 18350080 | bytes 16777216 | tf_op jit(solution)/shard_map/prepare/pallas_call | solution.py:264
  11.1 0.1 collective-permute-done.refs_0_
  11.2 1.8 %collective-permute-start.1 = (f32[456,128]{1,0:T(8,128)S(1)}, f32[456,128]{1,0:T(8,128)S(1)}, u32[]{:S(2)}, u32[]{:S(2)}) collective-permute-start(f32[456,128]{1,0:T(8,128)S(1)} %collective-permute-done.refs_0_), channel_id=1, source_target_pairs={{0,16},{8,24},{16,0},{24,8},{1,17},{9,25},{17,1},{25,9},{2,18},{10... | collective-permute-start | bytes 700424 | tf_op jit(solution)/shard_map/ppermute | solution.py:385
  12.9 0.0 collective-permute-done.2.refs_1_
  12.9 5.5 %flux.3 = (f32[64,128]{1,0:T(8,128)S(1)}, f32[64,128]{1,0:T(8,128)S(1)}) custom-call(bf16[64,64,1024]{2,1,0:T(8,128)(2,1)S(1)} %get-tuple-element.37.table, f32[64,128]{1,0:T(8,128)S(1)} %get-tuple-element.26.planck, f32[64,128]{1,0:T(8,128)S(1)} %get-tuple-element.27.share, f32[456,128]{1,0:T(8,128)S(1)} %collective-permute-done.refs_0_, ...), custom_call_target="tpu_custom_call" | custom-call | flops 3221225472 | bytes 8388608 | tf_op jit(solution)/shard_map/flux/pallas_call | solution.py:303
  18.4 0.0 collective-permute-done.1.refs_0_
  18.4 3.1 %flux.4 = f32[64,128]{1,0:T(8,128)S(1)} custom-call(bf16[64,64,1024]{2,1,0:T(8,128)(2,1)S(1)} %get-tuple-element.37.table, f32[64,128]{1,0:T(8,128)S(1)} %get-tuple-element.26.planck, f32[64,128]{1,0:T(8,128)S(1)} %get-tuple-element.27.share, f32[456,128]{1,0:T(8,128)S(1)} %collective-permute-done.1.refs_0_), custom_call_target="tpu_custom_call" | custom-call | flops 1610612736 | bytes 8388608 | tf_op jit(solution)/shard_map/flux/pallas_call | solution.py:303
  21.6 1.6 %collective-permute-start.3 = (f32[64,128]{1,0:T(8,128)S(1)}, f32[64,128]{1,0:T(8,128)S(1)}, u32[]{:S(2)}, u32[]{:S(2)}) collective-permute-start(f32[64,128]{1,0:T(8,128)S(1)} %get-tuple-element.34), channel_id=1, source_target_pairs={{0,8},{8,0},{16,24},{24,16},{1,9},{9,1},{17,25},{25,17},{2,10},{10... | collective-permute-start | bytes 98312 | tf_op jit(solution)/shard_map/ppermute | solution.py:385
  23.1 1.2 %collective-permute-start.4 = (f32[64,128]{1,0:T(8,128)S(1)}, f32[64,128]{1,0:T(8,128)S(1)}, u32[]{:S(2)}, u32[]{:S(2)}) collective-permute-start(f32[64,128]{1,0:T(8,128)S(1)} %flux.4), channel_id=1, source_target_pairs={{0,24},{8,16},{16,8},{24,0},{1,25},{9,17},{17,9},{25,1},{2,26},{10... | collective-permute-start | bytes 98312 | tf_op jit(solution)/shard_map/ppermute | solution.py:385
  24.3 0.8 %collective-permute-start.5 = (f32[64,128]{1,0:T(8,128)S(1)}, f32[64,128]{1,0:T(8,128)S(1)}, u32[]{:S(2)}, u32[]{:S(2)}) collective-permute-start(f32[64,128]{1,0:T(8,128)S(1)} %get-tuple-element.36), channel_id=1, source_target_pairs={{0,16},{8,24},{16,0},{24,8},{1,17},{9,25},{17,1},{25,9},{2,18},{10... | collective-permute-start | bytes 98312 | tf_op jit(solution)/shard_map/ppermute | solution.py:385
  25.1 3.1 %flux.5 = f32[64,128]{1,0:T(8,128)S(1)} custom-call(bf16[64,64,1024]{2,1,0:T(8,128)(2,1)S(1)} %get-tuple-element.37.table, f32[64,128]{1,0:T(8,128)S(1)} %get-tuple-element.26.planck, f32[64,128]{1,0:T(8,128)S(1)} %get-tuple-element.27.share, f32[456,128]{1,0:T(8,128)S(1)} %group.1.refs_0_), custom_call_target="tpu_custom_call" | custom-call | flops 1610612736 | bytes 8388608 | tf_op jit(solution)/shard_map/flux/pallas_call | solution.py:303
  28.3 0.0 collective-permute-done.3
  28.3 0.0 collective-permute-done.4
  28.3 0.0 collective-permute-done.5
  28.3 2.0 %collective-permute-start.6 = (f32[64,128]{1,0:T(8,128)S(1)}, f32[64,128]{1,0:T(8,128)S(1)}, u32[]{:S(2)}, u32[]{:S(2)}) collective-permute-start(f32[64,128]{1,0:T(8,128)S(1)} %add_add_fusion.own), channel_id=1, source_target_pairs={{0,31},{1,2},{2,1},{3,4},{4,3},{5,6},{6,5},{7,8},{8,7},{9,10},{10,... | collective-permute-start | bytes 98312 | tf_op jit(solution)/shard_map/ppermute | solution.py:402
  30.3 0.0 collective-permute-start.7
  30.3 0.2 spread_inner.1.inner
  30.5 5.2 %collective-permute-done.6.first = f32[64,128]{1,0:T(8,128)S(1)} collective-permute-done((f32[64,128]{1,0:T(8,128)S(1)}, f32[64,128]{1,0:T(8,128)S(1)}, u32[]{:S(2)}, u32[]{:S(2)}) %collective-permute-start.6) | collective-permute-done | bytes 32800 | tf_op jit(solution)/shard_map/ppermute | solution.py:402
  35.7 0.0 collective-permute-done.7.second
  35.7 0.8 %spread.1 = f32[64,512]{1,0:T(8,128)} custom-call(f32[64,512]{1,0:T(8,128)S(1)} %spread_inner.1.inner, f32[64,128]{1,0:T(8,128)S(1)} %collective-permute-done.6.first, f32[64,128]{1,0:T(8,128)S(1)} %collective-permute-done.7.second, s32[1]{0:T(128)} %bitcast.5.parity, bf16[256,512]{1,0:T(8,128)(2,1)S(1)} %get-tuple-element.39.high, ...), custom_call_target="tpu_custom_call" | custom-call | tf_op jit(solution)/shard_map/spread/pallas_call | solution.py:364
  (1 shorter events, 0.0 us)
Async XLA Ops:
  2.5 8.7 %collective-permute-start = (f32[456,128]{1,0:T(8,128)S(1)}, f32[456,128]{1,0:T(8,128)S(1)}, u32[]{:S(2)}, u32[]{:S(2)}) collective-permute-start(f32[456,128]{1,0:T(8,128)S(1)} %group.1.refs_0_), channel_id=1, source_target_pairs={{0,8},{8,0},{16,24},{24,16},{1,9},{9,1},{17,25},{25,17},{2,10},{10... | collective-permute-start | bytes 700424 | tf_op jit(solution)/shard_map/ppermute | solution.py:385
  5.5 7.5 %collective-permute-start.2 = (f32[456,128]{1,0:T(8,128)S(1)}, f32[456,128]{1,0:T(8,128)S(1)}, u32[]{:S(2)}, u32[]{:S(2)}) collective-permute-start(f32[456,128]{1,0:T(8,128)S(1)} %group.1.refs_0_), channel_id=1, source_target_pairs={{0,16},{8,24},{16,0},{24,8},{1,17},{9,25},{17,1},{25,9},{2,18},{10... | collective-permute-start | bytes 700424 | tf_op jit(solution)/shard_map/ppermute | solution.py:385
  11.2 7.2 %collective-permute-start.1 = (f32[456,128]{1,0:T(8,128)S(1)}, f32[456,128]{1,0:T(8,128)S(1)}, u32[]{:S(2)}, u32[]{:S(2)}) collective-permute-start(f32[456,128]{1,0:T(8,128)S(1)} %collective-permute-done.refs_0_), channel_id=1, source_target_pairs={{0,16},{8,24},{16,0},{24,8},{1,17},{9,25},{17,1},{25,9},{2,18},{10... | collective-permute-start | bytes 700424 | tf_op jit(solution)/shard_map/ppermute | solution.py:385
  21.6 6.7 %collective-permute-start.3 = (f32[64,128]{1,0:T(8,128)S(1)}, f32[64,128]{1,0:T(8,128)S(1)}, u32[]{:S(2)}, u32[]{:S(2)}) collective-permute-start(f32[64,128]{1,0:T(8,128)S(1)} %get-tuple-element.34), channel_id=1, source_target_pairs={{0,8},{8,0},{16,24},{24,16},{1,9},{9,1},{17,25},{25,17},{2,10},{10... | collective-permute-start | bytes 98312 | tf_op jit(solution)/shard_map/ppermute | solution.py:385
  23.1 5.2 %collective-permute-start.4 = (f32[64,128]{1,0:T(8,128)S(1)}, f32[64,128]{1,0:T(8,128)S(1)}, u32[]{:S(2)}, u32[]{:S(2)}) collective-permute-start(f32[64,128]{1,0:T(8,128)S(1)} %flux.4), channel_id=1, source_target_pairs={{0,24},{8,16},{16,8},{24,0},{1,25},{9,17},{17,9},{25,1},{2,26},{10... | collective-permute-start | bytes 98312 | tf_op jit(solution)/shard_map/ppermute | solution.py:385
  24.3 4.0 %collective-permute-start.5 = (f32[64,128]{1,0:T(8,128)S(1)}, f32[64,128]{1,0:T(8,128)S(1)}, u32[]{:S(2)}, u32[]{:S(2)}) collective-permute-start(f32[64,128]{1,0:T(8,128)S(1)} %get-tuple-element.36), channel_id=1, source_target_pairs={{0,16},{8,24},{16,0},{24,8},{1,17},{9,25},{17,1},{25,9},{2,18},{10... | collective-permute-start | bytes 98312 | tf_op jit(solution)/shard_map/ppermute | solution.py:385
  28.3 7.3 %collective-permute-start.6 = (f32[64,128]{1,0:T(8,128)S(1)}, f32[64,128]{1,0:T(8,128)S(1)}, u32[]{:S(2)}, u32[]{:S(2)}) collective-permute-start(f32[64,128]{1,0:T(8,128)S(1)} %add_add_fusion.own), channel_id=1, source_target_pairs={{0,31},{1,2},{2,1},{3,4},{4,3},{5,6},{6,5},{7,8},{8,7},{9,10},{10,... | collective-permute-start | bytes 98312 | tf_op jit(solution)/shard_map/ppermute | solution.py:402
  30.3 5.4 %collective-permute-start.7 = (f32[64,128]{1,0:T(8,128)S(1)}, f32[64,128]{1,0:T(8,128)S(1)}, u32[]{:S(2)}, u32[]{:S(2)}) collective-permute-start(f32[64,128]{1,0:T(8,128)S(1)} %add_add_fusion.own), channel_id=1, source_target_pairs={{0,1},{1,0},{2,3},{3,2},{4,5},{5,4},{6,7},{7,6},{8,9},{9,8},{10,11... | collective-permute-start | bytes 98312 | tf_op jit(solution)/shard_map/ppermute | solution.py:403

commit v8 on v6

--- a/solution.py
+++ b/solution.py
@@ -153,7 +153,7 @@
         downs[l + 1] = (downs[l] - downs[l + 1]) + (below - above)
         return v, above
 
-    lax.fori_loop(0, levels, climb, (v, fold(v)), unroll=8)
+    lax.fori_loop(0, levels, climb, (v, fold(v)), unroll=16)
     heat = downs[1 : levels + 1, 0, :]
     for s in range(1, 8):
         heat = heat + downs[1 : levels + 1, s, :]
@@ -366,7 +366,7 @@
     (heat,) = flux(table, weight, share, [third], scale)
     heat, table, rows, *heats = lax.optimization_barrier((heat, table, rows, *heats))
     (total,) = flux(table, weight, share, [rows], scale)
-    total = swap(heat, 3) + swap(heats[0], 1) + swap(heats[1], 2) + total
+    total = swap(heats[0], 1) + swap(heat, 3) + swap(heats[1], 2) + total
     pairs = [(i, i ^ 1) for i in range(devices)]
     across = [(i, (i + 1) % devices if i % 2 else (i - 1) % devices) for i in range(devices)]
     second = lax.ppermute(total, ("sec", "col"), across)

time: 36.7 us -> 36.6 us (level)
  no operation moved by 1% of the time
where the time goes in v8:
time: 36.6 us; the launch traced here: 36.5 us
  Pallas kernels  18.4 us (50%)
  starting transfers between devices  11.8 us (32%)
  waiting for transfers between devices  5.47 us (15%)
  between operations  0.72 us (2%)
    pallas_call x3, Pallas kernels, flux(): pl.pallas_call(functools.partial(flux_body, block, scale, span, count), o...  11.7 us
    ppermute x6, starting transfers between devices, swap(): return lax.ppermute(x, 'sec', [(i, i ^ m) for i in range(n_sec)])  9.84 us
    ppermute x1, waiting for transfers between devices, shards(): second = lax.ppermute(total, ('sec', 'col'), across)  5.35 us
    pallas_call x1, Pallas kernels, prepare(): pl.pallas_call(functools.partial(prepare_body, block), out_shape=(jax.Sha...  4.09 us
    ppermute x1, starting transfers between devices, shards(): second = lax.ppermute(total, ('sec', 'col'), across)  1.97 us
    pallas_call x1, Pallas kernels, group(): pl.pallas_call(group_body, out_shape=jax.ShapeDtypeStruct((feat + 8, coar...  1.8 us
    pallas_call x1, Pallas kernels, spread(): pl.pallas_call(spread_body, out_shape=jax.ShapeDtypeStruct((levels, fine)...  0.87 us
  transfers between devices with their start and end apart: 8, of which 2 were waited for; matrix products, arithmetic and copies ran while one was open for 0% of the time, Pallas kernels for 35%

profile of v8, /device:TPU:0, one launch (start us, length us, event | category | flops | bytes accessed | tf_op | source)
XLA Modules:
  0.0 36.5 jit_solution(11813587100783079243)
XLA Ops:
  0.7 1.8 %group.1.refs_0_ = f32[456,128]{1,0:T(8,128)S(1)} custom-call(f32[448,512]{1,0:T(8,128)} %bitcast.7, f32[1,512]{1,0:T(1,128)} %bitcast.8, s32[1,512]{1,0:T(1,128)} %grouping_in.1, s32[1]{0:T(128)S(6)} %copy.11.sunlit), custom_call_target="tpu_custom_call" | custom-call | flops 234881024 | bytes 917504 | tf_op jit(solution)/shard_map/group/pallas_call | solution.py:72
  2.5 3.0 %collective-permute-start = (f32[456,128]{1,0:T(8,128)S(1)}, f32[456,128]{1,0:T(8,128)S(1)}, u32[]{:S(2)}, u32[]{:S(2)}) collective-permute-start(f32[456,128]{1,0:T(8,128)S(1)} %group.1.refs_0_), channel_id=1, source_target_pairs={{0,8},{8,0},{16,24},{24,16},{1,9},{9,1},{17,25},{25,17},{2,10},{10... | collective-permute-start | bytes 700424 | tf_op jit(solution)/shard_map/ppermute | solution.py:355
  5.5 1.5 %collective-permute-start.2 = (f32[456,128]{1,0:T(8,128)S(1)}, f32[456,128]{1,0:T(8,128)S(1)}, u32[]{:S(2)}, u32[]{:S(2)}) collective-permute-start(f32[456,128]{1,0:T(8,128)S(1)} %group.1.refs_0_), channel_id=1, source_target_pairs={{0,16},{8,24},{16,0},{24,8},{1,17},{9,25},{17,1},{25,9},{2,18},{10... | collective-permute-start | bytes 700424 | tf_op jit(solution)/shard_map/ppermute | solution.py:355
  7.0 4.1 %prepare.1 = (bf16[64,64,1024]{2,1,0:T(8,128)(2,1)S(1)}, f32[64,128]{1,0:T(8,128)S(1)}, f32[64,128]{1,0:T(8,128)S(1)}, bf16[256,512]{1,0:T(8,128)(2,1)S(1)}, bf16[256,512]{1,0:T(8,128)(2,1)S(1)}) custom-call(f32[64,64,448]{2,1,0:T(8,128)} %absorb_in.1, f32[64,64]{1,0:T(8,128)} %bias_in.1, f32[1,64]{1,0:T(1,128)} %bitcast.9, f32[1,64]{1,0:T(1,128)} %bitcast.10, ...), custom_call_target="tpu_custom_call" | custom-call | flops 18350080 | bytes 16777216 | tf_op jit(solution)/shard_map/prepare/pallas_call | solution.py:264
  11.1 0.1 collective-permute-done.refs_0_
  11.2 1.8 %collective-permute-start.1 = (f32[456,128]{1,0:T(8,128)S(1)}, f32[456,128]{1,0:T(8,128)S(1)}, u32[]{:S(2)}, u32[]{:S(2)}) collective-permute-start(f32[456,128]{1,0:T(8,128)S(1)} %collective-permute-done.refs_0_), channel_id=1, source_target_pairs={{0,16},{8,24},{16,0},{24,8},{1,17},{9,25},{17,1},{25,9},{2,18},{10... | collective-permute-start | bytes 700424 | tf_op jit(solution)/shard_map/ppermute | solution.py:355
  12.9 0.0 collective-permute-done.2.refs_1_
  12.9 5.4 %flux.3 = (f32[64,128]{1,0:T(8,128)S(1)}, f32[64,128]{1,0:T(8,128)S(1)}) custom-call(bf16[64,64,1024]{2,1,0:T(8,128)(2,1)S(1)} %get-tuple-element.37.table, f32[64,128]{1,0:T(8,128)S(1)} %get-tuple-element.26.planck, f32[64,128]{1,0:T(8,128)S(1)} %get-tuple-element.27.share, f32[456,128]{1,0:T(8,128)S(1)} %collective-permute-done.refs_0_, ...), custom_call_target="tpu_custom_call" | custom-call | flops 3221225472 | bytes 8388608 | tf_op jit(solution)/shard_map/flux/pallas_call | solution.py:303
  18.4 0.0 collective-permute-done.1.refs_0_
  18.4 3.1 %flux.4 = f32[64,128]{1,0:T(8,128)S(1)} custom-call(bf16[64,64,1024]{2,1,0:T(8,128)(2,1)S(1)} %get-tuple-element.37.table, f32[64,128]{1,0:T(8,128)S(1)} %get-tuple-element.26.planck, f32[64,128]{1,0:T(8,128)S(1)} %get-tuple-element.27.share, f32[456,128]{1,0:T(8,128)S(1)} %collective-permute-done.1.refs_0_), custom_call_target="tpu_custom_call" | custom-call | flops 1610612736 | bytes 8388608 | tf_op jit(solution)/shard_map/flux/pallas_call | solution.py:303
  21.5 1.6 %collective-permute-start.3 = (f32[64,128]{1,0:T(8,128)S(1)}, f32[64,128]{1,0:T(8,128)S(1)}, u32[]{:S(2)}, u32[]{:S(2)}) collective-permute-start(f32[64,128]{1,0:T(8,128)S(1)} %get-tuple-element.34), channel_id=1, source_target_pairs={{0,8},{8,0},{16,24},{24,16},{1,9},{9,1},{17,25},{25,17},{2,10},{10... | collective-permute-start | bytes 98312 | tf_op jit(solution)/shard_map/ppermute | solution.py:355
  23.1 1.2 %collective-permute-start.4 = (f32[64,128]{1,0:T(8,128)S(1)}, f32[64,128]{1,0:T(8,128)S(1)}, u32[]{:S(2)}, u32[]{:S(2)}) collective-permute-start(f32[64,128]{1,0:T(8,128)S(1)} %flux.4), channel_id=1, source_target_pairs={{0,24},{8,16},{16,8},{24,0},{1,25},{9,17},{17,9},{25,1},{2,26},{10... | collective-permute-start | bytes 98312 | tf_op jit(solution)/shard_map/ppermute | solution.py:355
  24.2 0.8 %collective-permute-start.5 = (f32[64,128]{1,0:T(8,128)S(1)}, f32[64,128]{1,0:T(8,128)S(1)}, u32[]{:S(2)}, u32[]{:S(2)}) collective-permute-start(f32[64,128]{1,0:T(8,128)S(1)} %get-tuple-element.36), channel_id=1, source_target_pairs={{0,16},{8,24},{16,0},{24,8},{1,17},{9,25},{17,1},{25,9},{2,18},{10... | collective-permute-start | bytes 98312 | tf_op jit(solution)/shard_map/ppermute | solution.py:355
  25.1 3.1 %flux.5 = f32[64,128]{1,0:T(8,128)S(1)} custom-call(bf16[64,64,1024]{2,1,0:T(8,128)(2,1)S(1)} %get-tuple-element.37.table, f32[64,128]{1,0:T(8,128)S(1)} %get-tuple-element.26.planck, f32[64,128]{1,0:T(8,128)S(1)} %get-tuple-element.27.share, f32[456,128]{1,0:T(8,128)S(1)} %group.1.refs_0_), custom_call_target="tpu_custom_call" | custom-call | flops 1610612736 | bytes 8388608 | tf_op jit(solution)/shard_map/flux/pallas_call | solution.py:303
  28.2 0.0 collective-permute-done.3
  28.2 0.0 collective-permute-done.4
  28.2 0.0 collective-permute-done.5
  28.2 2.0 %collective-permute-start.6 = (f32[64,128]{1,0:T(8,128)S(1)}, f32[64,128]{1,0:T(8,128)S(1)}, u32[]{:S(2)}, u32[]{:S(2)}) collective-permute-start(f32[64,128]{1,0:T(8,128)S(1)} %add_add_fusion.own), channel_id=1, source_target_pairs={{0,31},{1,2},{2,1},{3,4},{4,3},{5,6},{6,5},{7,8},{8,7},{9,10},{10,... | collective-permute-start | bytes 98312 | tf_op jit(solution)/shard_map/ppermute | solution.py:372
  30.2 0.0 collective-permute-start.7
  30.2 5.4 %collective-permute-done.6.first = f32[64,128]{1,0:T(8,128)S(1)} collective-permute-done((f32[64,128]{1,0:T(8,128)S(1)}, f32[64,128]{1,0:T(8,128)S(1)}, u32[]{:S(2)}, u32[]{:S(2)}) %collective-permute-start.6) | collective-permute-done | bytes 32800 | tf_op jit(solution)/shard_map/ppermute | solution.py:372
  35.6 0.0 collective-permute-done.7.second
  35.6 0.9 %spread.1 = f32[64,512]{1,0:T(8,128)} custom-call(f32[64,128]{1,0:T(8,128)S(1)} %add_add_fusion.own, f32[64,128]{1,0:T(8,128)S(1)} %collective-permute-done.6.first, f32[64,128]{1,0:T(8,128)S(1)} %collective-permute-done.7.second, s32[1]{0:T(128)} %bitcast.5.parity, bf16[256,512]{1,0:T(8,128)(2,1)S(1)} %get-tuple-element.39.high, ...), custom_call_target="tpu_custom_call" | custom-call | tf_op jit(solution)/shard_map/spread/pallas_call | solution.py:334
  (1 shorter events, 0.0 us)
Async XLA Ops:
  2.5 8.7 %collective-permute-start = (f32[456,128]{1,0:T(8,128)S(1)}, f32[456,128]{1,0:T(8,128)S(1)}, u32[]{:S(2)}, u32[]{:S(2)}) collective-permute-start(f32[456,128]{1,0:T(8,128)S(1)} %group.1.refs_0_), channel_id=1, source_target_pairs={{0,8},{8,0},{16,24},{24,16},{1,9},{9,1},{17,25},{25,17},{2,10},{10... | collective-permute-start | bytes 700424 | tf_op jit(solution)/shard_map/ppermute | solution.py:355
  5.5 7.5 %collective-permute-start.2 = (f32[456,128]{1,0:T(8,128)S(1)}, f32[456,128]{1,0:T(8,128)S(1)}, u32[]{:S(2)}, u32[]{:S(2)}) collective-permute-start(f32[456,128]{1,0:T(8,128)S(1)} %group.1.refs_0_), channel_id=1, source_target_pairs={{0,16},{8,24},{16,0},{24,8},{1,17},{9,25},{17,1},{25,9},{2,18},{10... | collective-permute-start | bytes 700424 | tf_op jit(solution)/shard_map/ppermute | solution.py:355
  11.2 7.2 %collective-permute-start.1 = (f32[456,128]{1,0:T(8,128)S(1)}, f32[456,128]{1,0:T(8,128)S(1)}, u32[]{:S(2)}, u32[]{:S(2)}) collective-permute-start(f32[456,128]{1,0:T(8,128)S(1)} %collective-permute-done.refs_0_), channel_id=1, source_target_pairs={{0,16},{8,24},{16,0},{24,8},{1,17},{9,25},{17,1},{25,9},{2,18},{10... | collective-permute-start | bytes 700424 | tf_op jit(solution)/shard_map/ppermute | solution.py:355
  21.5 6.7 %collective-permute-start.3 = (f32[64,128]{1,0:T(8,128)S(1)}, f32[64,128]{1,0:T(8,128)S(1)}, u32[]{:S(2)}, u32[]{:S(2)}) collective-permute-start(f32[64,128]{1,0:T(8,128)S(1)} %get-tuple-element.34), channel_id=1, source_target_pairs={{0,8},{8,0},{16,24},{24,16},{1,9},{9,1},{17,25},{25,17},{2,10},{10... | collective-permute-start | bytes 98312 | tf_op jit(solution)/shard_map/ppermute | solution.py:355
  23.1 5.1 %collective-permute-start.4 = (f32[64,128]{1,0:T(8,128)S(1)}, f32[64,128]{1,0:T(8,128)S(1)}, u32[]{:S(2)}, u32[]{:S(2)}) collective-permute-start(f32[64,128]{1,0:T(8,128)S(1)} %flux.4), channel_id=1, source_target_pairs={{0,24},{8,16},{16,8},{24,0},{1,25},{9,17},{17,9},{25,1},{2,26},{10... | collective-permute-start | bytes 98312 | tf_op jit(solution)/shard_map/ppermute | solution.py:355
  24.2 4.0 %collective-permute-start.5 = (f32[64,128]{1,0:T(8,128)S(1)}, f32[64,128]{1,0:T(8,128)S(1)}, u32[]{:S(2)}, u32[]{:S(2)}) collective-permute-start(f32[64,128]{1,0:T(8,128)S(1)} %get-tuple-element.36), channel_id=1, source_target_pairs={{0,16},{8,24},{16,0},{24,8},{1,17},{9,25},{17,1},{25,9},{2,18},{10... | collective-permute-start | bytes 98312 | tf_op jit(solution)/shard_map/ppermute | solution.py:355
  28.2 7.3 %collective-permute-start.6 = (f32[64,128]{1,0:T(8,128)S(1)}, f32[64,128]{1,0:T(8,128)S(1)}, u32[]{:S(2)}, u32[]{:S(2)}) collective-permute-start(f32[64,128]{1,0:T(8,128)S(1)} %add_add_fusion.own), channel_id=1, source_target_pairs={{0,31},{1,2},{2,1},{3,4},{4,3},{5,6},{6,5},{7,8},{8,7},{9,10},{10,... | collective-permute-start | bytes 98312 | tf_op jit(solution)/shard_map/ppermute | solution.py:372
  30.2 5.4 %collective-permute-start.7 = (f32[64,128]{1,0:T(8,128)S(1)}, f32[64,128]{1,0:T(8,128)S(1)}, u32[]{:S(2)}, u32[]{:S(2)}) collective-permute-start(f32[64,128]{1,0:T(8,128)S(1)} %add_add_fusion.own), channel_id=1, source_target_pairs={{0,1},{1,0},{2,3},{3,2},{4,5},{5,4},{6,7},{7,6},{8,9},{9,8},{10,11... | collective-permute-start | bytes 98312 | tf_op jit(solution)/shard_map/ppermute | solution.py:373
